TPU v7x, 512 devices: a whole 4x4x16 slice. The times are simulated.
512 devices in a mesh: seq: 128 (over z, x, core), head: 4 (over y).
Axes of the slice: x: 4, y: 4, z: 16, core: 2. Of those that a mesh axis runs over, the one named last changes fastest.
Arguments:
- out_grad: bfloat16 [16384, 768], P('seq', 'head'), may hold values from -6 to 6
- expert_of: int32 [16384], P('seq'), may hold values from 0 to 127, as said below
- counts: int32 [128, 128], P(None, 'seq'), may hold values from 0 to 2, as said below
- w_up: bfloat16 [128, 768, 3072], P('seq', None, 'head'), may hold values from -0.21875 to 0.21875
- w_down: bfloat16 [128, 3072, 768], P('seq', 'head'), may hold values from -0.109375 to 0.109375
- pre_act: bfloat16 [32768, 3072], P('seq', 'head'), may hold values from -6 to 6
- queries: bfloat16 [16384, 1024], P('seq', 'head'), may hold values from -6 to 6
- keys: bfloat16 [16384, 1024], P('seq', 'head'), may hold values from -6 to 6
- values: bfloat16 [16384, 1024], P('seq', 'head'), may hold values from -6 to 6
- w_out: bfloat16 [1024, 768], P('head'), may hold values from -0.1875 to 0.1875
Outputs:
- grad_hidden: bfloat16 [16384, 768], P('seq')
- grad_queries: bfloat16 [16384, 1024], P('seq', 'head')
- grad_keys: bfloat16 [16384, 1024], P('seq', 'head')
- grad_values: bfloat16 [16384, 1024], P('seq', 'head')
Inputs may be any that keep to these rules, and one draw needn't show every extreme that they name: `expert_of`: in each aligned block of 128 tokens at most 2 tokens name one expert; one expert, the same for every block, is named by exactly 2 tokens of every block, and every other expert by fewer than 2 tokens of a block. counts[s, e] is the number of tokens of block s that name expert e.
All inputs are finite; a program needn't handle non-finite values.
Results may differ from a plain program's by a relative error of at most 0.014.
Values may be sent and summed in bfloat16 or wider, within the bound.
No kernel may reach another device: no remote copies, remote signals or barrier semaphores. Data moves between devices by JAX's collectives and lax.ppermute only.
A program may use at most 64 MiB of HBM per device.

v0:
```python
import math

import jax
import jax.numpy as jnp
from jax import lax
from jax.sharding import Mesh
from jax.sharding import PartitionSpec as P

SEQ = ("seq_0", "seq_1", "seq_2")


def sent_to_all(shard, axis):
    copies = jnp.broadcast_to(shard, (lax.axis_size(axis), *shard.shape))
    return lax.all_to_all(copies, axis, split_axis=0, concat_axis=0, tiled=True)


def joined_along(tiles, dim):
    tiles = jnp.moveaxis(tiles, 0, dim)
    shape = tiles.shape
    return tiles.reshape(*shape[:dim], shape[dim] * shape[dim + 1], *shape[dim + 2 :])


def collect(shard, axis, dim):
    tiles = sent_to_all(shard, axis)
    return joined_along(tiles, dim)


def over_copies(shard, axis):
    everything = sent_to_all(shard, axis)
    return jnp.sum(everything.astype(jnp.float32), axis=0)


def split_up(shard, dim, length):
    before, after = (shard.shape[:dim], shard.shape[dim + 1 :])
    return jnp.moveaxis(shard.reshape(*before, length, -1, *after), dim, 0)


def summed_on_arrival(shard, axis, dim):
    tiles = split_up(shard, dim, lax.axis_size(axis))
    arrived = lax.all_to_all(tiles, axis, split_axis=0, concat_axis=0, tiled=True)
    return arrived.sum(axis=0)


def sum_in_two_steps(shard, axes, dim):
    far, near = axes
    tiles = split_up(shard, dim, lax.axis_size(far))
    nearer = summed_on_arrival(tiles, near, dim + 1)
    arrived = lax.all_to_all(nearer, far, split_axis=0, concat_axis=0, tiled=True)
    return arrived.sum(axis=0)


def padded_to(lines, length):
    spare = -len(lines) % length
    return jnp.pad(lines, [(0, spare)] + [(0, 0)] * (lines.ndim - 1))


def gathered_by_axis(shard, axes, dim):
    far, near = axes
    tiles = sent_to_all(sent_to_all(shard, far), near)
    return joined_along(tiles.swapaxes(0, 1).reshape(-1, *shard.shape), dim)


def total_of(shard, axes):
    own = sum_in_two_steps(
        padded_to(shard, lax.axis_size(axes[0]) * lax.axis_size(axes[1])), axes, 0
    )
    whole = gathered_by_axis(own, axes, 0)
    return whole[: len(shard)].reshape(shard.shape)


def packed_total(arrays, axis):
    flat, at, outs = (jnp.concatenate([a.reshape(-1) for a in arrays]), 0, [])
    so_far = total_of(flat, axis)
    for a in arrays:
        outs.append(so_far[at : at + a.size].reshape(a.shape))
        at += a.size
    return tuple(outs)


def shards(out_grad, expert_of, counts, w_up, w_down, pre_act, queries, keys, values, w_out):
    experts = lax.axis_size(SEQ)
    tok_rows = out_grad.shape[0]
    slot_count = pre_act.shape[0]
    capacity = slot_count // experts
    head_dim = queries.shape[1]
    scaling = 1.0 / math.sqrt(head_dim * tok_rows * experts)
    full_rows = collect(out_grad, "head", 1)
    model_width = full_rows.shape[1]
    expert_ids = jnp.arange(experts, dtype=jnp.int32)
    onehot = (expert_of[:, None] == expert_ids[None, :]).astype(jnp.int32)
    token_rank = jnp.sum((jnp.cumsum(onehot, axis=0) - 1) * onehot, axis=1)
    slot_of = expert_of * capacity + token_rank
    token_of_slot = (
        jnp.full((experts * capacity,), tok_rows, jnp.int32)
        .at[slot_of]
        .set(jnp.arange(tok_rows, dtype=jnp.int32))
    )
    arrived = counts[:, 0]
    offsets = jnp.cumsum(arrived) - arrived
    arrived_total = jnp.sum(arrived)
    packed_ids = jnp.arange(slot_count, dtype=jnp.int32)
    source = jnp.sum((offsets[None, :] <= packed_ids[:, None]).astype(jnp.int32), axis=1) - 1
    within = packed_ids - offsets[source]
    packed_live = packed_ids < arrived_total
    flat_pos = jnp.where(packed_live, source * capacity + within, experts * capacity)
    down_local = w_down[0]
    up_local = w_up[0]
    padded = jnp.concatenate(
        [full_rows, jnp.zeros((1, full_rows.shape[1]), full_rows.dtype)], axis=0
    )
    received = lax.all_to_all(
        padded[token_of_slot].reshape(experts, capacity, full_rows.shape[1]),
        SEQ,
        split_axis=0,
        concat_axis=0,
        tiled=True,
    )
    flat_rows = received.reshape(experts * capacity, received.shape[2])
    padded = jnp.concatenate(
        [flat_rows, jnp.zeros((1, flat_rows.shape[1]), flat_rows.dtype)], axis=0
    )
    middle = jnp.dot(padded[flat_pos], down_local.T, preferred_element_type=jnp.float32)
    mid_grad = jnp.where(pre_act > 0, middle, jnp.zeros_like(middle)).astype(jnp.bfloat16)
    hidden_part = jnp.dot(mid_grad, up_local.T, preferred_element_type=jnp.float32)
    slot_ids = jnp.arange(experts * capacity, dtype=jnp.int32)
    slot_source = slot_ids // capacity
    slot_rank = slot_ids % capacity
    slot_live = slot_rank < arrived[slot_source]
    slot_pos = jnp.where(slot_live, offsets[slot_source] + slot_rank, slot_count)
    expert_packed = (
        over_copies(hidden_part.astype(jnp.bfloat16), "head")
        .astype(jnp.float32)
        .astype(jnp.bfloat16)
    )
    padded_grad = jnp.concatenate(
        [expert_packed, jnp.zeros((1, expert_packed.shape[1]), jnp.bfloat16)], axis=0
    )
    returned = lax.all_to_all(
        padded_grad[slot_pos].reshape(experts, capacity, expert_packed.shape[1]),
        SEQ,
        split_axis=0,
        concat_axis=0,
        tiled=True,
    )
    expert_grad = returned.reshape(experts * capacity, model_width)[slot_of]
    grad_hidden = (full_rows.astype(jnp.float32) + expert_grad.astype(jnp.float32)).astype(
        jnp.bfloat16
    )
    head_grad = jnp.dot(grad_hidden, w_out.T, preferred_element_type=jnp.float32).astype(
        jnp.bfloat16
    )
    query_part = jnp.dot(queries.T, head_grad, preferred_element_type=jnp.float32)
    key_state, query_state = packed_total(
        (jnp.dot(keys.T, values, preferred_element_type=jnp.float32), query_part),
        (("seq_0", "seq_1"), "seq_2"),
    )
    key_round = key_state.astype(jnp.bfloat16)
    query_round = query_state.astype(jnp.bfloat16)
    grad_queries = (
        scaling * jnp.dot(head_grad, key_round.T, preferred_element_type=jnp.float32)
    ).astype(jnp.bfloat16)
    grad_keys = (
        scaling * jnp.dot(values, query_round.T, preferred_element_type=jnp.float32)
    ).astype(jnp.bfloat16)
    grad_values = (scaling * jnp.dot(keys, query_round, preferred_element_type=jnp.float32)).astype(
        jnp.bfloat16
    )
    return (grad_hidden, grad_queries, grad_keys, grad_values)


def solution(mesh):
    finer = Mesh(
        mesh.devices.reshape(16, 4, 2, mesh.shape["head"]), ("seq_0", "seq_1", "seq_2", "head")
    )
    return jax.shard_map(
        shards,
        mesh=finer,
        in_specs=(
            P(SEQ, "head"),
            P(SEQ),
            P(None, SEQ),
            P(SEQ, None, "head"),
            P(SEQ, "head", None),
            P(SEQ, "head"),
            P(SEQ, "head"),
            P(SEQ, "head"),
            P(SEQ, "head"),
            P("head", None),
        ),
        out_specs=(P(SEQ, None), P(SEQ, "head"), P(SEQ, "head"), P(SEQ, "head")),
        check_vma=False,
    )
```

profile of v0, /device:TPU:1, one launch (start us, length us, event | category | flops | bytes accessed | tf_op | source)
XLA Modules:
  0.0 196.2 jit_solution(1646544180343622386)
XLA Ops:
  0.6 1.6 broadcast_in_dim.36
  2.2 5.0 %all-to-all-start = ((bf16[4,128,192]{1,2,0:T(8,128)(2,1)}), bf16[4,128,192]{1,2,0:T(8,128)(2,1)S(1)}, u32[]{:S(2)}, u32[]{:S(2)}) async-start(bf16[4,128,192]{1,2,0:T(8,128)(2,1)} %broadcast_in_dim.36), calls=%async_computation | async-start | bytes 393216 | tf_op jit(solution)/shard_map/all_to_all | solution.py:14
  9.7 1.0 scatter_custom_fusion
  10.7 1.8 all-to-all-done
  12.6 1.2 gather_fusion
  13.8 0.9 reshape.211
  14.7 21.0 %all-to-all-start.1 = ((bf16[128,2,768]{2,1,0:T(2,128)(2,1)}), bf16[128,2,768]{2,1,0:T(2,128)(2,1)S(1)}, u32[]{:S(2)}, u32[]{:S(2)}) async-start(bf16[128,2,768]{2,1,0:T(2,128)(2,1)} %reshape.211), calls=%async_computation.1 | async-start | bytes 786432 | tf_op jit(solution)/shard_map/all_to_all | solution.py:111
  36.9 1.9 gather_fusion.1
  39.4 21.6 %all-to-all-done.1 = bf16[128,2,768]{2,1,0:T(2,128)(2,1)S(1)} async-done(((bf16[128,2,768]{2,1,0:T(2,128)(2,1)}), bf16[128,2,768]{2,1,0:T(2,128)(2,1)S(1)}, u32[]{:S(2)}, u32[]{:S(2)}) %all-to-all-start.1) | async-done | bytes 393248 | tf_op jit(solution)/shard_map/all_to_all | solution.py:111
  61.3 1.2 gather_fusion.2
  62.5 1.9 convolution_convert_fusion
  64.5 1.3 broadcast_in_dim.41
  65.7 3.6 %all-to-all-start.2 = ((bf16[4,256,768]{2,1,0:T(8,128)(2,1)}), bf16[4,256,768]{2,1,0:T(8,128)(2,1)S(1)}, u32[]{:S(2)}, u32[]{:S(2)}) async-start(bf16[4,256,768]{2,1,0:T(8,128)(2,1)} %broadcast_in_dim.41), calls=%async_computation.2 | async-start | bytes 3145728 | tf_op jit(solution)/shard_map/all_to_all | solution.py:14
  69.3 1.9 gather_fusion.4
  71.2 1.9 gather_fusion.3
  73.1 15.9 %all-to-all-done.2 = bf16[4,256,768]{2,1,0:T(8,128)(2,1)S(1)} async-done(((bf16[4,256,768]{2,1,0:T(8,128)(2,1)}), bf16[4,256,768]{2,1,0:T(8,128)(2,1)S(1)}, u32[]{:S(2)}, u32[]{:S(2)}) %all-to-all-start.2) | async-done | bytes 1572896 | tf_op jit(solution)/shard_map/all_to_all | solution.py:14
  89.4 1.2 gather_fusion.5
  91.5 10.1 %all-to-all-start.3 = ((bf16[128,2,768]{2,1,0:T(2,128)(2,1)}), bf16[128,2,768]{2,1,0:T(2,128)(2,1)S(1)}, u32[]{:S(2)}, u32[]{:S(2)}) async-start(bf16[128,2,768]{2,1,0:T(2,128)(2,1)} %reshape.214), calls=%async_computation.3 | async-start | bytes 786432 | tf_op jit(solution)/shard_map/all_to_all | solution.py:138
  102.1 25.0 %all-to-all-done.3 = bf16[128,2,768]{2,1,0:T(2,128)(2,1)S(1)} async-done(((bf16[128,2,768]{2,1,0:T(2,128)(2,1)}), bf16[128,2,768]{2,1,0:T(2,128)(2,1)S(1)}, u32[]{:S(2)}, u32[]{:S(2)}) %all-to-all-start.3) | async-done | bytes 393248 | tf_op jit(solution)/shard_map/all_to_all | solution.py:138
  129.4 5.1 %all_to_all.48 = f32[2,64,1024]{2,1,0:T(8,128)S(1)} all-to-all(f32[2,64,1024]{2,1,0:T(8,128)S(1)} %copy.37), channel_id=1, replica_groups=mesh['seq_0'=16,'seq_1'=4,'seq_2'=2,'head'=4] {'seq_2'}, dimensions={0} | all-to-all | bytes 1048576 | tf_op jit(solution)/shard_map/all_to_all | solution.py:40
  134.7 27.2 %all_to_all.49 = f32[64,1,1024]{2,1,0:T(1,128)S(1)} all-to-all(f32[64,1,1024]{2,1,0:T(1,128)S(1)} %all_to_all.35), channel_id=1, replica_groups=mesh['seq_0'=16,'seq_1'=4,'seq_2'=2,'head'=4] {'seq_0','seq_1'}, dimensions={0} | all-to-all | bytes 524288 | tf_op jit(solution)/shard_map/all_to_all | solution.py:48
  162.8 1.4 reduce.4
  164.3 21.3 %all_to_all.50 = bf16[64,2,512]{2,1,0:T(2,128)(2,1)S(1)} all-to-all(bf16[64,2,512]{2,1,0:T(2,128)(2,1)S(1)} %reshape.286), channel_id=1, replica_groups=mesh['seq_0'=16,'seq_1'=4,'seq_2'=2,'head'=4] {'seq_0','seq_1'}, dimensions={0} | all-to-all | bytes 262144 | tf_op jit(solution)/shard_map/all_to_all | solution.py:14
  185.8 7.2 %all_to_all.51 = bf16[2,64,1024]{2,1,0:T(8,128)(2,1)S(1)} all-to-all(bf16[2,64,1024]{2,1,0:T(8,128)(2,1)S(1)} %broadcast_in_dim.43), channel_id=1, replica_groups=mesh['seq_0'=16,'seq_1'=4,'seq_2'=2,'head'=4] {'seq_2'}, dimensions={0} | all-to-all | bytes 524288 | tf_op jit(solution)/shard_map/all_to_all | solution.py:14
  (76 shorter events, 13.2 us)
Async XLA Ops:
  0.6 61.8 %copy-start = (bf16[1,768,768]{2,1,0:T(8,128)(2,1)S(1)}, bf16[1,768,768]{2,1,0:T(8,128)(2,1)}, u32[]{:S(2)}) copy-start(bf16[1,768,768]{2,1,0:T(8,128)(2,1)} %param.13) | copy-start | bytes 3538948
  2.2 10.2 %all-to-all-start = ((bf16[4,128,192]{1,2,0:T(8,128)(2,1)}), bf16[4,128,192]{1,2,0:T(8,128)(2,1)S(1)}, u32[]{:S(2)}, u32[]{:S(2)}) async-start(bf16[4,128,192]{1,2,0:T(8,128)(2,1)} %broadcast_in_dim.36), calls=%async_computation | async-start | bytes 393216 | tf_op jit(solution)/shard_map/all_to_all | solution.py:14
  13.8 21.9 %copy-start.1 = (s32[128,1]{0,1:T(1,128)S(1)}, s32[128,1]{0,1:T(1,128)}, u32[]{:S(2)}) copy-start(s32[128,1]{0,1:T(1,128)} %param.12) | copy-start | bytes 1540
  14.7 46.4 %all-to-all-start.1 = ((bf16[128,2,768]{2,1,0:T(2,128)(2,1)}), bf16[128,2,768]{2,1,0:T(2,128)(2,1)S(1)}, u32[]{:S(2)}, u32[]{:S(2)}) async-start(bf16[128,2,768]{2,1,0:T(2,128)(2,1)} %reshape.211), calls=%async_computation.1 | async-start | bytes 786432 | tf_op jit(solution)/shard_map/all_to_all | solution.py:111
  61.3 1.3 copy-start.7
  65.7 23.2 %all-to-all-start.2 = ((bf16[4,256,768]{2,1,0:T(8,128)(2,1)}), bf16[4,256,768]{2,1,0:T(8,128)(2,1)S(1)}, u32[]{:S(2)}, u32[]{:S(2)}) async-start(bf16[4,256,768]{2,1,0:T(8,128)(2,1)} %broadcast_in_dim.41), calls=%async_computation.2 | async-start | bytes 3145728 | tf_op jit(solution)/shard_map/all_to_all | solution.py:14
  90.6 11.0 %copy-start.4 = (bf16[128,256]{1,0:T(8,128)(2,1)S(1)}, bf16[128,256]{1,0:T(8,128)(2,1)}, u32[]{:S(2)}) copy-start(bf16[128,256]{1,0:T(8,128)(2,1)} %param.18) | copy-start | bytes 196612
  90.6 11.0 %copy-start.5 = (bf16[128,256]{1,0:T(8,128)(2,1)S(1)}, bf16[128,256]{1,0:T(8,128)(2,1)}, u32[]{:S(2)}) copy-start(bf16[128,256]{1,0:T(8,128)(2,1)} %param.17) | copy-start | bytes 196612
  91.5 35.5 %all-to-all-start.3 = ((bf16[128,2,768]{2,1,0:T(2,128)(2,1)}), bf16[128,2,768]{2,1,0:T(2,128)(2,1)S(1)}, u32[]{:S(2)}, u32[]{:S(2)}) async-start(bf16[128,2,768]{2,1,0:T(2,128)(2,1)} %reshape.214), calls=%async_computation.3 | async-start | bytes 786432 | tf_op jit(solution)/shard_map/all_to_all | solution.py:138
  127.2 1.0 copy-start.3
  127.2 1.3 copy-start.6
  128.2 1.1 copy-start.2
where the time goes:
time: 197 us; the launch traced here: 196 us
  waiting for transfers between devices  64.2 us (33%)
  blocking collectives  60.8 us (31%)
  starting transfers between devices  39.7 us (20%)
  local copies, waits for them, and re-layouts  20 us (10%)
  other arithmetic  6.5 us (3%)
  matrix products  3.86 us (2%)
    all_to_all x2, blocking collectives, sent_to_all(): return lax.all_to_all(copies, axis, split_axis=0, concat_axis=0, tiled=True)  28.5 us
    all_to_all x1, blocking collectives, sum_in_two_steps(): lax.all_to_all(nearer, far, split_axis=0, concat_axis=0, tiled=True)  27.2 us
    all_to_all x1, waiting for transfers between devices, shards(): lax.all_to_all(padded_grad[slot_pos].reshape(experts, capacity, expert_pa...  25 us
    all_to_all x1, waiting for transfers between devices, shards(): lax.all_to_all(padded[token_of_slot].reshape(experts, capacity, full_rows...  21.6 us
    all_to_all x1, starting transfers between devices, shards(): lax.all_to_all(padded[token_of_slot].reshape(experts, capacity, full_rows...  21 us
    all_to_all x2, waiting for transfers between devices, sent_to_all(): return lax.all_to_all(copies, axis, split_axis=0, concat_axis=0, tiled=True)  17.6 us
    all_to_all x1, starting transfers between devices, shards(): lax.all_to_all(padded_grad[slot_pos].reshape(experts, capacity, expert_pa...  10.1 us
    all_to_all x2, starting transfers between devices, sent_to_all(): return lax.all_to_all(copies, axis, split_axis=0, concat_axis=0, tiled=True)  8.56 us
  transfers between devices with their start and end apart: 4, of which 4 were waited for; matrix products, arithmetic and copies ran while one was open for 6% of the time, Pallas kernels for 0%

commit v1 on v0

v1 whole, which is shorter than its diff:
```python
import math

import jax
import jax.numpy as jnp
from jax import lax
from jax.experimental import pallas as pl
from jax.experimental.pallas import tpu as pltpu
from jax.sharding import Mesh
from jax.sharding import PartitionSpec as P

SEQ = ("z", "x", "c")
PLANE = ("x", "c")
BF, F32 = jnp.bfloat16, jnp.float32
NZ, NP, NH = 16, 8, 4
BLOCK = 128
D, HD, DQ = 768, 256, 192
VMEM = pl.BlockSpec(memory_space=pltpu.VMEM)


def nn(a, b):
    return lax.dot_general(a, b, (((1,), (0,)), ((), ())), preferred_element_type=F32)


def nt(a, b):
    return lax.dot_general(a, b, (((1,), (1,)), ((), ())), preferred_element_type=F32)


def tn(a, b):
    return lax.dot_general(a, b, (((0,), (0,)), ((), ())), preferred_element_type=F32)


def hot(cond):
    return jnp.where(cond, 1.0, 0.0).astype(BF)


def iota(shape, dim):
    return lax.broadcasted_iota(jnp.int32, shape, dim)


def halves(state):
    parts = state.reshape(NP, 2, 16, HD)
    return parts[:, 0], parts[:, 1]


def call(kernel, outs, *args, flops=10**8):
    single = not isinstance(outs, (list, tuple))
    shapes = [outs] if single else list(outs)
    nbytes = sum(a.size * a.dtype.itemsize for a in args)
    res = pl.pallas_call(
        kernel,
        out_shape=shapes,
        in_specs=[VMEM] * len(args),
        out_specs=[VMEM] * len(shapes),
        cost_estimate=pl.CostEstimate(flops=flops, bytes_accessed=nbytes, transcendentals=0),
        name=kernel.__name__,
    )(*args)
    return res[0] if single else res


def sds(*shape, dtype=BF):
    return jax.ShapeDtypeStruct(shape, dtype)


def pack(e_ref, og_ref, q_ref, out_ref):
    e = e_ref[...]
    pos = (e & 7) * NZ + (e >> 3)
    match = pos == iota((BLOCK, BLOCK), 0)
    upper = hot(iota((BLOCK, BLOCK), 0) < iota((BLOCK, BLOCK), 1))
    prev = nn(hot(match), upper)
    first = hot(match & (prev < 0.5))
    second = hot(match & (prev >= 0.5))
    og, q = og_ref[...], q_ref[...]
    out_ref[:, 0:384] = jnp.concatenate([nn(first, og), nn(second, og)], axis=1).astype(BF)
    out_ref[:, 384:640] = nn(first, q).astype(BF)
    out_ref[:, 640:896] = nn(second, q).astype(BF)


def prepare(c_ref, pre_ref, k_ref, v_ref, mask_ref, kst_ref):
    c = c_ref[...].astype(F32)
    p = iota((BLOCK, BLOCK), 0)
    s_of_p = (p & (NZ - 1)) * NP + (p >> 4)
    s = iota((BLOCK, BLOCK), 1)
    zero = jnp.zeros((BLOCK, BLOCK), F32)
    offset = jnp.sum(jnp.where(s < s_of_p, c, zero), axis=1, keepdims=True)
    count = jnp.sum(jnp.where(s == s_of_p, c, zero), axis=1, keepdims=True)
    row = iota((BLOCK, 2 * BLOCK), 1).astype(F32)
    live = jnp.where(pre_ref[...].astype(F32) > 0, 1.0, 0.0).astype(BF)
    for r in range(2):
        pick = hot((row == offset + r) & (count > r + 0.5))
        mask_ref[r] = nn(pick, live).astype(BF)
    a, b = halves(tn(k_ref[...], v_ref[...]))
    kst_ref[:, :, 0:HD] = a.astype(BF)
    kst_ref[:, :, HD:] = b.astype(BF)


def experts(rows_ref, mask_ref, wd_ref, wu_ref, full_ref, parts_ref):
    wd, wu = wd_ref[...], wu_ref[...]
    for r in range(2):
        x = jnp.concatenate([rows_ref[h, :, r * DQ : (r + 1) * DQ] for h in range(NH)], axis=1)
        full_ref[r] = x
        mid = jnp.where(mask_ref[r].astype(F32) > 0.5, nt(x, wd), 0.0).astype(BF)
        part = nt(mid, wu).astype(BF)
        for h in range(NH):
            parts_ref[h, r] = part


def combine(parts_ref, full_ref, recv_ref, wo_ref, kst_ref, out_ref):
    wo = wo_ref[...]
    state = jnp.zeros((HD, HD), F32)
    for r in range(2):
        total = parts_ref[0, r].astype(F32)
        for h in range(1, NH):
            total = total + parts_ref[h, r].astype(F32)
        gh = (full_ref[r].astype(F32) + total.astype(BF).astype(F32)).astype(BF)
        hg = nt(gh, wo).astype(BF)
        state = state + tn(recv_ref[:, 384 + r * HD : 384 + (r + 1) * HD], hg)
        out_ref[:, :, r * D : (r + 1) * D] = gh.reshape(NP, 16, D)
    a, b = halves(state)
    out_ref[:, :, 1536:1792] = a.astype(BF)
    out_ref[:, :, 1792:2048] = b.astype(BF)
    out_ref[:, :, 2048:2560] = kst_ref[...]


def regroup(in_ref, out_ref):
    total = in_ref[0, :, 1536:2560].astype(F32)
    for i in range(1, NP):
        total = total + in_ref[i, :, 1536:2560].astype(F32)
    out_ref[:, :, 0:1024] = jnp.broadcast_to(total.astype(BF)[None], (NZ, 16, 1024))
    x0 = in_ref[:, :, 0:D].reshape(BLOCK, D)
    x1 = in_ref[:, :, D : 2 * D].reshape(BLOCK, D)
    o = iota((2 * BLOCK, BLOCK), 0)
    i = iota((2 * BLOCK, BLOCK), 1)
    same = ((o & 7) == (i >> 4)) & ((o >> 4) == (i & 15))
    lower = hot(same & ((o & 8) == 0))
    higher = hot(same & ((o & 8) != 0))
    rows = nn(lower, x0[:, 0:384]) + nn(higher, x0[:, 384:768])
    out_ref[:, :, 1024:1408] = rows.astype(BF).reshape(NZ, 16, 384)
    seconds = jnp.zeros((2 * BLOCK, 128), F32)
    for j in range(6):
        pick = hot(((o & 15) == j) & ((o >> 4) == (i & 15)))
        seconds = seconds + nn(pick, x1[:, j * 128 : (j + 1) * 128])
    out_ref[:, :, 1408:1536] = seconds.astype(BF).reshape(NZ, 16, 128)


def reduce_states(in_ref, out_ref):
    total = in_ref[0, :, 0:1024].astype(F32)
    for i in range(1, NZ):
        total = total + in_ref[i, :, 0:1024].astype(F32)
    out_ref[...] = jnp.broadcast_to(total.astype(BF)[None], (NP, 16, 1024))


def unpack(in_ref, erow_ref, ecol_ref, wo_ref, gh_ref, hg_ref):
    e = ecol_ref[...]
    earlier = iota((BLOCK, BLOCK), 1) < iota((BLOCK, BLOCK), 0)
    twice = jnp.where((e == erow_ref[...]) & earlier, 1.0, 0.0)
    rank = jnp.sum(twice, axis=1, keepdims=True)
    lane = iota((BLOCK, 2 * BLOCK), 1)
    same = (e == (lane >> 4) * NP + (lane & 7)) & (rank < 0.5)
    lower = hot(same & ((lane & 8) == 0))
    higher = hot(same & ((lane & 8) != 0))
    rows = in_ref[:, :, 1024:1408].reshape(2 * BLOCK, 384)
    seconds = in_ref[0, :, 1408:1536].astype(F32)
    for i in range(1, NZ):
        seconds = seconds + in_ref[i, :, 1408:1536].astype(F32)
    second = jnp.concatenate([seconds[j : j + 1] for j in range(6)], axis=1)
    gh = jnp.concatenate([nn(lower, rows), nn(higher, rows)], axis=1)
    gh = (gh + jnp.where(rank > 0.5, second, 0.0)).astype(BF)
    gh_ref[...] = gh
    hg_ref[...] = nt(gh, wo_ref[...]).astype(BF)


def finish(in_ref, hg_ref, k_ref, v_ref, gq_ref, gk_ref, gv_ref):
    scaling = 1.0 / math.sqrt(HD * BLOCK * BLOCK)

    def whole(at):
        a = in_ref[:, :, at : at + HD].reshape(NP, 1, 16, HD)
        b = in_ref[:, :, at + HD : at + 2 * HD].reshape(NP, 1, 16, HD)
        return jnp.concatenate([a, b], axis=1).reshape(HD, HD)

    qr, kr = whole(0), whole(512)
    gq_ref[...] = (scaling * nt(hg_ref[...], kr)).astype(BF)
    gk_ref[...] = (scaling * nt(v_ref[...], qr)).astype(BF)
    gv_ref[...] = (scaling * nn(k_ref[...], qr)).astype(BF)


def swap(tiles, axis):
    return lax.all_to_all(tiles, axis, split_axis=0, concat_axis=0, tiled=True)


def shards(out_grad, expert_of, counts, w_up, w_down, pre_act, queries, keys, values, w_out):
    e_row = expert_of.reshape(1, BLOCK)
    e_col = expert_of.reshape(BLOCK, 1)
    send = call(pack, sds(BLOCK, 896), e_row, out_grad, queries)
    recv = swap(send, ("x", "c", "z"))
    mask, kst = call(
        prepare,
        [sds(2, BLOCK, D), sds(NP, 16, 2 * HD)],
        counts.reshape(1, BLOCK),
        pre_act,
        keys,
        values,
    )
    rows = swap(jnp.broadcast_to(recv[None, :, 0:384], (NH, BLOCK, 384)), "y")
    full, parts = call(
        experts,
        [sds(2, BLOCK, D), sds(NH, 2, BLOCK, D)],
        rows,
        mask,
        w_down[0],
        w_up[0],
    )
    parts = swap(parts.reshape(NH, 2 * BLOCK, D), "y").reshape(NH, 2, BLOCK, D)
    back = call(combine, sds(NP, 16, 2560), parts, full, recv, w_out, kst)
    back = swap(back, PLANE)
    back = call(regroup, sds(NZ, 16, 1536), back)
    back = swap(back, "z")
    states = call(reduce_states, sds(NP, 16, 1024), back)
    states = swap(states, PLANE)
    gh, hg = call(unpack, [sds(BLOCK, D), sds(BLOCK, HD)], back, e_row, e_col, w_out)
    gq, gk, gv = call(finish, [sds(BLOCK, HD)] * 3, states, hg, keys, values)
    return gh, gq, gk, gv


def solution(mesh):
    finer = Mesh(mesh.devices.reshape(16, 4, 2, mesh.shape["head"]), ("z", "x", "c", "y"))
    return jax.shard_map(
        shards,
        mesh=finer,
        in_specs=(
            P(SEQ, "y"),
            P(SEQ),
            P(None, SEQ),
            P(SEQ, None, "y"),
            P(SEQ, "y", None),
            P(SEQ, "y"),
            P(SEQ, "y"),
            P(SEQ, "y"),
            P(SEQ, "y"),
            P("y", None),
        ),
        out_specs=(P(SEQ, None), P(SEQ, "y"), P(SEQ, "y"), P(SEQ, "y")),
        check_vma=False,
    )
```

time: 197 us -> 177 us (0.90)
  blocking collectives: 60.8 us -> 124 us
  waiting for transfers between devices: 64.2 us -> 9.47 us
  starting transfers between devices: 39.7 us -> 14 us
  Pallas kernels: 0 us -> 20.5 us
  local copies, waits for them, and re-layouts: 20 us -> 5.79 us
  other arithmetic: 6.5 us -> 1.66 us
  matrix products: 3.86 us -> 0 us
    all_to_all x4, blocking collectives: 60.8 us -> 124 us  [swap(): return lax.all_to_all(tiles, axis, split_axis=0, concat_axis=0, tiled=True)]
    all_to_all x4 -> x2, waiting for transfers between devices: 64.2 us -> 9.47 us  [swap(): return lax.all_to_all(tiles, axis, split_axis=0, concat_axis=0, tiled=True)]
    all_to_all x4 -> x2, starting transfers between devices: 39.7 us -> 14 us  [swap(): return lax.all_to_all(tiles, axis, split_axis=0, concat_axis=0, tiled=True)]
    pallas_call x0 -> x8, Pallas kernels: none -> 20.5 us  [call(): pl.pallas_call(kernel, out_shape=shapes, in_specs=[VMEM] * len(args), out...]
    gather x7 -> x0, local copies, waits for them, and re-layouts: 10 us -> none  [the longest x1 1.87 us: shards(): slot_live = slot_rank < arrived[slot_source]]
    dot_general x7 -> x0, matrix products: 3.86 us -> none  [the longest x1 1.93 us: shards(): jnp.dot(mid_grad, up_local.T, preferred_element_type=jnp.float32)]
    broadcast_in_dim x5 -> x1, local copies, waits for them, and re-layouts: 3.53 us -> 0.79 us  [shards(): rows = swap(jnp.broadcast_to(recv[None, :, 0:384], (NH, BLOCK, 384)), 'y')]
    reduce_sum x6 -> x0, other arithmetic: 2.23 us -> none  [the longest x1 0.82 us: shards(): token_rank = jnp.sum((jnp.cumsum(onehot, axis=0) - 1) * onehot, axis=1)]
  transfers between devices with their start and end apart: 4 -> 2, of which waited for: 4 -> 2; matrix products, arithmetic and copies ran while one was open for 6% -> 0% of each run, Pallas kernels for 0% -> 3%
where the time goes in v1:
time: 177 us; the launch traced here: 176 us
  blocking collectives  124 us (70%)
  Pallas kernels  20.5 us (12%)
  starting transfers between devices  14 us (8%)
  waiting for transfers between devices  9.47 us (5%)
  local copies, waits for them, and re-layouts  5.79 us (3%)
    all_to_all x4, blocking collectives, swap(): return lax.all_to_all(tiles, axis, split_axis=0, concat_axis=0, tiled=True)  124 us
    pallas_call x8, Pallas kernels, call(): pl.pallas_call(kernel, out_shape=shapes, in_specs=[VMEM] * len(args), out...  20.5 us
    all_to_all x2, starting transfers between devices, swap(): return lax.all_to_all(tiles, axis, split_axis=0, concat_axis=0, tiled=True)  14 us
    all_to_all x2, waiting for transfers between devices, swap(): return lax.all_to_all(tiles, axis, split_axis=0, concat_axis=0, tiled=True)  9.47 us
    unnamed x12, local copies, waits for them, and re-layouts  3.73 us
  transfers between devices with their start and end apart: 2, of which 2 were waited for; matrix products, arithmetic and copies ran while one was open for 0% of the time, Pallas kernels for 3%

profile of v1, /device:TPU:1, one launch (start us, length us, event | category | flops | bytes accessed | tf_op | source)
XLA Modules:
  0.0 176.5 jit_solution(15220724567411927545)
XLA Ops:
  0.6 1.5 copy.19.og_ref
  2.2 1.9 %pack.1 = bf16[128,896]{1,0:T(8,128)(2,1)} custom-call(s32[1,128]{1,0:T(1,128)} %bitcast.18, bf16[128,192]{1,0:T(8,128)(2,1)} %copy.19.og_ref, bf16[128,256]{1,0:T(8,128)(2,1)} %q_ref.1), custom_call_target="tpu_custom_call" | custom-call | flops 100000000 | bytes 115200 | tf_op jit(solution)/shard_map/pack/pallas_call | solution.py:49
  4.1 0.5 broadcast.1
  4.6 1.7 reduce
  6.5 43.3 %all_to_all.36 = bf16[128,2,448]{2,1,0:T(2,128)(2,1)S(1)} all-to-all(bf16[128,2,448]{2,1,0:T(2,128)(2,1)S(1)} %reshape.31), channel_id=1, replica_groups=mesh['z'=16,'x'=4,'c'=2,'y'=4] {'x','c','z'}, dimensions={0} | all-to-all | bytes 458752 | tf_op jit(solution)/shard_map/all_to_all | solution.py:187
  49.8 0.5 reshape.32
  50.4 0.8 broadcast_in_dim.2
  51.2 4.2 %all-to-all-start.1 = ((bf16[4,128,384]{2,1,0:T(8,128)(2,1)}), bf16[4,128,384]{2,1,0:T(8,128)(2,1)S(1)}, u32[]{:S(2)}, u32[]{:S(2)}) async-start(bf16[4,128,384]{2,1,0:T(8,128)(2,1)} %broadcast_in_dim.2), calls=%async_computation.1 | async-start | bytes 786432 | tf_op jit(solution)/shard_map/all_to_all | solution.py:187
  55.4 2.2 %prepare.1 = (bf16[2,128,768]{2,1,0:T(8,128)(2,1)}, bf16[8,16,512]{2,1,0:T(8,128)(2,1)}) custom-call(s32[1,128]{1,0:T(1,128)} %bitcast.21, bf16[256,768]{1,0:T(8,128)(2,1)} %pre_ref.1, bf16[128,256]{1,0:T(8,128)(2,1)} %k_ref.3, bf16[128,256]{1,0:T(8,128)(2,1)} %v_ref.3), custom_call_target="tpu_custom_call" | custom-call | flops 100000000 | bytes 524800 | tf_op jit(solution)/shard_map/prepare/pallas_call | solution.py:49
  57.5 6.2 %all-to-all-done.1.rows_ref = bf16[4,128,384]{2,1,0:T(8,128)(2,1)S(1)} async-done(((bf16[4,128,384]{2,1,0:T(8,128)(2,1)}), bf16[4,128,384]{2,1,0:T(8,128)(2,1)S(1)}, u32[]{:S(2)}, u32[]{:S(2)}) %all-to-all-start.1) | async-done | bytes 393248 | tf_op jit(solution)/shard_map/all_to_all | solution.py:187
  63.7 0.8 copy-done
  64.4 4.6 %experts.1 = (bf16[2,128,768]{2,1,0:T(8,128)(2,1)}, bf16[4,2,128,768]{3,2,1,0:T(8,128)(2,1)}) custom-call(bf16[4,128,384]{2,1,0:T(8,128)(2,1)} %copy-done, bf16[2,128,768]{2,1,0:T(8,128)(2,1)} %get-tuple-element.13.mask_ref, bf16[768,768]{1,0:T(8,128)(2,1)} %bitcast.15, bf16[768,768]{1,0:T(8,128)(2,1)} %bitcast.16), custom_call_target="tpu_custom_call" | custom-call | flops 100000000 | bytes 3145728 | tf_op jit(solution)/shard_map/experts/pallas_call | solution.py:49
  69.0 24.2 %all_to_all.37 = bf16[4,256,768]{2,1,0:T(8,128)(2,1)} all-to-all(bf16[4,256,768]{2,1,0:T(8,128)(2,1)} %bitcast.12), channel_id=1, replica_groups=mesh['z'=16,'x'=4,'c'=2,'y'=4] {'y'}, dimensions={0} | all-to-all | bytes 3145728 | tf_op jit(solution)/shard_map/all_to_all | solution.py:187
  93.2 3.2 %combine.1 = bf16[8,16,2560]{2,1,0:T(8,128)(2,1)} custom-call(bf16[4,2,128,768]{3,2,1,0:T(8,128)(2,1)} %bitcast.11, bf16[2,128,768]{2,1,0:T(8,128)(2,1)} %get-tuple-element.15.full_ref, bf16[128,896]{1,0:T(8,128)(2,1)} %bitcast.14, bf16[256,768]{1,0:T(8,128)(2,1)} %wo_ref.3, bf16[8,16,512]{2,1,0:T(8,128)(2,1)} %get-tuple-element.16.kst_ref), custom_call_target="tpu_custom_call" | custom-call | flops 100000000 | bytes 2719744 | tf_op jit(solution)/shard_map/combine/pallas_call | solution.py:49
  96.5 16.9 %all_to_all.38.in_ref = bf16[8,16,2560]{2,1,0:T(8,128)(2,1)} all-to-all(bf16[8,16,2560]{2,1,0:T(8,128)(2,1)} %combine.1), channel_id=1, replica_groups=mesh['z'=16,'x'=4,'c'=2,'y'=4] {'x','c'}, dimensions={0} | all-to-all | bytes 1310720 | tf_op jit(solution)/shard_map/all_to_all | solution.py:187
  113.4 2.4 %regroup.1 = bf16[16,16,1536]{2,1,0:T(8,128)(2,1)} custom-call(bf16[8,16,2560]{2,1,0:T(8,128)(2,1)} %all_to_all.38.in_ref), custom_call_target="tpu_custom_call" | custom-call | flops 100000000 | bytes 655360 | tf_op jit(solution)/shard_map/regroup/pallas_call | solution.py:49
  115.7 39.9 %all_to_all.39.in_ref = bf16[16,16,1536]{2,1,0:T(8,128)(2,1)} all-to-all(bf16[16,16,1536]{2,1,0:T(8,128)(2,1)} %regroup.1), channel_id=1, replica_groups=mesh['z'=16,'x'=4,'c'=2,'y'=4] {'z'}, dimensions={0} | all-to-all | bytes 1572864 | tf_op jit(solution)/shard_map/all_to_all | solution.py:187
  155.7 1.9 %reduce_states.1 = bf16[8,16,1024]{2,1,0:T(8,128)(2,1)} custom-call(bf16[16,16,1536]{2,1,0:T(8,128)(2,1)} %all_to_all.39.in_ref), custom_call_target="tpu_custom_call" | custom-call | flops 100000000 | bytes 786432 | tf_op jit(solution)/shard_map/reduce_states/pallas_call | solution.py:49
  157.6 9.8 %all-to-all-start.5 = ((bf16[8,16,1024]{2,1,0:T(8,128)(2,1)}), bf16[8,16,1024]{2,1,0:T(8,128)(2,1)S(1)}, u32[]{:S(2)}, u32[]{:S(2)}) async-start(bf16[8,16,1024]{2,1,0:T(8,128)(2,1)} %reduce_states.1), calls=%async_computation.5 | async-start | bytes 524288 | tf_op jit(solution)/shard_map/all_to_all | solution.py:187
  167.4 0.7 copy.21.ecol_ref
  168.1 2.4 %unpack.1 = (bf16[128,768]{1,0:T(8,128)(2,1)}, bf16[128,256]{1,0:T(8,128)(2,1)}) custom-call(bf16[16,16,1536]{2,1,0:T(8,128)(2,1)} %all_to_all.39.in_ref, s32[1,128]{1,0:T(1,128)} %bitcast.19, s32[128,1]{1,0:T(8,128)} %copy.21.ecol_ref, bf16[256,768]{1,0:T(8,128)(2,1)} %wo_ref.3), custom_call_target="tpu_custom_call" | custom-call | flops 100000000 | bytes 1180672 | tf_op jit(solution)/shard_map/unpack/pallas_call | solution.py:49
  170.6 3.3 %all-to-all-done.5.in_ref = bf16[8,16,1024]{2,1,0:T(8,128)(2,1)S(1)} async-done(((bf16[8,16,1024]{2,1,0:T(8,128)(2,1)}), bf16[8,16,1024]{2,1,0:T(8,128)(2,1)S(1)}, u32[]{:S(2)}, u32[]{:S(2)}) %all-to-all-start.5) | async-done | bytes 262176 | tf_op jit(solution)/shard_map/all_to_all | solution.py:187
  173.9 0.7 copy-done.2
  174.6 1.9 %finish.1 = (bf16[128,256]{1,0:T(8,128)(2,1)}, bf16[128,256]{1,0:T(8,128)(2,1)}, bf16[128,256]{1,0:T(8,128)(2,1)}) custom-call(bf16[8,16,1024]{2,1,0:T(8,128)(2,1)} %copy-done.2, bf16[128,256]{1,0:T(8,128)(2,1)} %get-tuple-element.18.hg_ref, bf16[128,256]{1,0:T(8,128)(2,1)} %k_ref.3, bf16[128,256]{1,0:T(8,128)(2,1)} %v_ref.3), custom_call_target="tpu_custom_call" | custom-call | flops 100000000 | bytes 458752 | tf_op jit(solution)/shard_map/finish/pallas_call | solution.py:49
  (9 shorter events, 0.3 us)
Async XLA Ops:
  50.3 18.7 %copy-start.1 = (bf16[128,1,896]{2,0,1:T(8,128)(2,1)}, bf16[128,1,896]{2,0,1:T(8,128)(2,1)S(1)}, u32[]{:S(2)}) copy-start(bf16[128,1,896]{2,0,1:T(8,128)(2,1)S(1)} %copy.24) | copy-start | bytes 688132
  51.2 12.5 %all-to-all-start.1 = ((bf16[4,128,384]{2,1,0:T(8,128)(2,1)}), bf16[4,128,384]{2,1,0:T(8,128)(2,1)S(1)}, u32[]{:S(2)}, u32[]{:S(2)}) async-start(bf16[4,128,384]{2,1,0:T(8,128)(2,1)} %broadcast_in_dim.2), calls=%async_computation.1 | async-start | bytes 786432 | tf_op jit(solution)/shard_map/all_to_all | solution.py:187
  63.7 0.8 copy-start
  115.7 51.6 %copy-start.3 = (s32[128]{0:T(128)S(1)}, s32[128]{0:T(128)}, u32[]{:S(2)}) copy-start(s32[128]{0:T(128)} %param.11) | copy-start | bytes 1540
  157.6 16.3 %all-to-all-start.5 = ((bf16[8,16,1024]{2,1,0:T(8,128)(2,1)}), bf16[8,16,1024]{2,1,0:T(8,128)(2,1)S(1)}, u32[]{:S(2)}, u32[]{:S(2)}) async-start(bf16[8,16,1024]{2,1,0:T(8,128)(2,1)} %reduce_states.1), calls=%async_computation.5 | async-start | bytes 524288 | tf_op jit(solution)/shard_map/all_to_all | solution.py:187
  173.9 0.7 copy-start.2

commit v2 on v1

v2 whole, which is shorter than its diff:
```python
import math

import jax
import jax.numpy as jnp
from jax import lax
from jax.experimental import pallas as pl
from jax.experimental.pallas import tpu as pltpu
from jax.sharding import Mesh
from jax.sharding import PartitionSpec as P

SEQ = ("z", "x", "c")
PLANE = ("x", "c")
BF, F32 = jnp.bfloat16, jnp.float32
NZ, NP, NH = 16, 8, 4
BLOCK = 128
D, HD, DQ = 768, 256, 192
LIMIT = 16 * 2**20
VMEM = pl.BlockSpec(memory_space=pltpu.VMEM)


def nn(a, b):
    return lax.dot_general(a, b, (((1,), (0,)), ((), ())), preferred_element_type=F32)


def nt(a, b):
    return lax.dot_general(a, b, (((1,), (1,)), ((), ())), preferred_element_type=F32)


def tn(a, b):
    return lax.dot_general(a, b, (((0,), (0,)), ((), ())), preferred_element_type=F32)


def hot(cond):
    return jnp.where(cond, 1.0, 0.0).astype(BF)


def iota(shape, dim):
    return lax.broadcasted_iota(jnp.int32, shape, dim)


def halves(state):
    parts = state.reshape(NP, 2, 16, HD)
    return parts[:, 0], parts[:, 1]


def call(kernel, outs, *args, far=(), home=False):
    single = not isinstance(outs, (list, tuple))
    shapes = [outs] if single else list(outs)
    nbytes = sum(a.size * a.dtype.itemsize for a in args)
    near = pltpu.with_memory_space_constraint
    res = pl.pallas_call(
        kernel,
        out_shape=shapes if home else [pltpu.VMEM(s.shape, s.dtype) for s in shapes],
        in_specs=[VMEM] * len(args),
        out_specs=[VMEM] * len(shapes),
        cost_estimate=pl.CostEstimate(flops=10**8, bytes_accessed=nbytes, transcendentals=0),
        compiler_params=pltpu.CompilerParams(vmem_limit_bytes=LIMIT),
        name=kernel.__name__,
    )(*[near(a, pltpu.HBM if n in far else pltpu.VMEM) for n, a in enumerate(args)])
    return res[0] if single else res


def sds(*shape, dtype=BF):
    return jax.ShapeDtypeStruct(shape, dtype)


def eye(n):
    return hot(iota((n, n), 0) == iota((n, n), 1))


def repeats(e):
    match = (e & 7) * NZ + (e >> 3) == iota((BLOCK, BLOCK), 0)
    earlier = hot(iota((BLOCK, BLOCK), 0) < iota((BLOCK, BLOCK), 1))
    return match, jnp.where(match & (nn(hot(match), earlier) > 0.5), 1.0, 0.0)


def pack(e_ref, ogt_ref, q_ref, k_ref, v_ref, out_ref):
    match, again = repeats(e_ref[...])
    first = (jnp.where(match, 1.0, 0.0) - again).astype(BF)
    second = jnp.broadcast_to(jnp.sum(again, axis=0, keepdims=True), (16, BLOCK)).astype(BF)
    ogt, q = ogt_ref[...], q_ref[...]
    token = jnp.concatenate([nt(second, ogt), nn(second, q)], axis=1)
    spare = jnp.concatenate(
        [token[0:1, i * 64 : (i + 1) * 64] for i in range(7)] + [jnp.zeros((9, 64), F32)], axis=0
    )
    spare = jnp.broadcast_to(spare[None], (NP, 16, 64)).reshape(BLOCK, 64)
    rows = jnp.concatenate([nt(first, ogt), nn(first, q), spare], axis=1)
    out_ref[:, :, 0:512] = rows.astype(BF).reshape(NP, 16, 512)
    a, b = halves(tn(k_ref[...], v_ref[...]))
    out_ref[:, :, 512:768] = a.astype(BF)
    out_ref[:, :, 768:1024] = b.astype(BF)


def tile_of(z):
    a, b = z // 4, z % 4
    return (a % 2) * 8, (a // 2) * HD + b * 64


def forward(in_ref, out_ref):
    x = in_ref[:, :, 0:512].reshape(BLOCK, 512)
    o = iota((2 * BLOCK, BLOCK), 0)
    i = iota((2 * BLOCK, BLOCK), 1)
    own = ((o & 7) == (i >> 4)) & ((o & 8) == 0) & ((o >> 4) == (i & 15))
    firsts = nn(hot(own), x[:, 0:448])
    other = ((o & 7) == (i >> 4)) & ((o & 8) != 0)
    spare = x[:, 448:512]
    seconds = jnp.concatenate([nn(hot(other & ((i & 15) == j)), spare) for j in range(7)], axis=1)
    total = in_ref[0, :, 512:1024].astype(F32)
    for p in range(1, NP):
        total = total + in_ref[p, :, 512:1024].astype(F32)
    nothing = jnp.zeros((8, 64), F32)
    pieces = []
    for z in range(NZ):
        row, lane = tile_of(z)
        pieces += [total[row : row + 8, lane : lane + 64], nothing]
    rows = jnp.concatenate([firsts + seconds, jnp.concatenate(pieces, axis=0)], axis=1)
    out_ref[...] = rows.astype(BF).reshape(NZ, 16, 512)


def place(c):
    shape = (2 * BLOCK, BLOCK)
    o, s = iota(shape, 0), iota(shape, 1)
    block = (o >> 4) * NP + (o & 7)
    c = jnp.broadcast_to(c, shape)
    before = jnp.sum(jnp.where(s < block, c, 0.0), axis=1, keepdims=True)
    count = jnp.sum(jnp.where(s == block, c, 0.0), axis=1, keepdims=True)
    r = ((iota((2 * BLOCK, 1), 0) >> 3) & 1).astype(F32)
    return before + r, count > r + 0.5


def masks(c_ref, pre_ref, mask_ref):
    row, live = place(c_ref[...].astype(F32))
    pick = hot((iota((2 * BLOCK, 2 * BLOCK), 1).astype(F32) == row) & live)
    on = jnp.where(pre_ref[...].astype(F32) > 0, 1.0, 0.0).astype(BF)
    mask_ref[...] = jnp.transpose(nn(pick, on)).astype(BF)


def arrive(in_ref, c_ref, out_ref, key_ref):
    _, live = place(c_ref[...].astype(F32))
    x = in_ref[:, :, 0:DQ].reshape(2 * BLOCK, DQ).astype(F32)
    x = jnp.where(live, x, 0.0).astype(BF)
    x = nt(eye(DQ), x).astype(BF)
    out_ref[...] = jnp.broadcast_to(x[None], (NH, DQ, 2 * BLOCK))
    total = in_ref[0, 0:8, 448:512].astype(F32)
    for z in range(1, NZ):
        total = total + in_ref[z, 0:8, 448:512].astype(F32)
    key_ref[...] = total.astype(BF)


def experts(rows_ref, mask_ref, wd_ref, wu_ref, out_ref):
    x = rows_ref[...].reshape(D, 2 * BLOCK)
    mid = jnp.where(mask_ref[...].astype(F32) > 0.5, nn(wd_ref[...], x), 0.0).astype(BF)
    out_ref[...] = nn(wu_ref[...], mid).astype(BF).reshape(NH, DQ, 2 * BLOCK)


def add_up(parts_ref, rows_ref, out_ref):
    total = parts_ref[0].astype(F32)
    for h in range(1, NH):
        total = total + parts_ref[h].astype(F32)
    gh = (rows_ref[0].astype(F32) + total.astype(BF).astype(F32)).astype(BF)
    out_ref[...] = jnp.broadcast_to(gh[None], (NH, DQ, 2 * BLOCK))


def combine(all_ref, own_ref, recv_ref, wo_ref, out_ref):
    gh = all_ref[...].reshape(D, 2 * BLOCK)
    hg = nn(wo_ref[...], gh).astype(BF)
    q = recv_ref[:, :, DQ:448].reshape(2 * BLOCK, HD)
    a, b = halves(nn(hg, q))
    o = iota((BLOCK, 2 * BLOCK), 0)
    i = iota((BLOCK, 2 * BLOCK), 1)
    same = ((o >> 4) == (i & 7)) & ((o & 15) == (i >> 4))
    own = own_ref[0]
    firsts = nt(hot(same & ((i & 8) == 0)), own)
    seconds = nt(hot(same & ((i & 8) != 0)), own)
    rows = jnp.concatenate([firsts, seconds], axis=1)
    out_ref[:, :, 0:384] = rows.astype(BF).reshape(NP, 16, 384)
    out_ref[:, :, 384:640] = a.astype(BF)
    out_ref[:, :, 640:896] = b.astype(BF)


def regroup(in_ref, key_ref, out_ref):
    total = in_ref[0, :, 384:896].astype(F32)
    for p in range(1, NP):
        total = total + in_ref[p, :, 384:896].astype(F32)
    out_ref[:, :, 0:512] = jnp.broadcast_to(total.astype(BF)[None], (NZ, 16, 512))
    o = iota((2 * BLOCK, BLOCK), 0)
    i = iota((2 * BLOCK, BLOCK), 1)
    here = (o >> 4) == (i & 15)
    firsts = nn(hot(here & ((o & 15) == (i >> 4))), in_ref[:, :, 0:DQ].reshape(BLOCK, DQ))
    second = nn(hot(here & ((o & 15) == 8)), in_ref[:, :, DQ : 2 * DQ].reshape(BLOCK, DQ))
    key = jnp.concatenate([key_ref[...].astype(F32), jnp.zeros((8, 64), F32)], axis=0)
    key = jnp.broadcast_to(key[None], (NZ, 16, 64)).reshape(2 * BLOCK, 64)
    rows = jnp.concatenate([firsts + second, key], axis=1)
    out_ref[:, :, 512:768] = rows.astype(BF).reshape(NZ, 16, 256)


def reduce_states(in_ref, out_ref):
    total = in_ref[0, :, 0:512].astype(F32)
    for z in range(1, NZ):
        total = total + in_ref[z, :, 0:512].astype(F32)
    upper = [None] * 8
    lower = [None] * 8
    for z in range(NZ):
        row, lane = tile_of(z)
        (lower if row else upper)[lane // 64] = in_ref[z, 0:8, 704:768].astype(F32)
    key = jnp.concatenate(
        [jnp.concatenate(upper, axis=1), jnp.concatenate(lower, axis=1)], axis=0
    )
    out_ref[:, :, 0:512] = jnp.broadcast_to(total.astype(BF)[None], (NP, 16, 512))
    out_ref[:, :, 512:1024] = jnp.broadcast_to(key.astype(BF)[None], (NP, 16, 512))


def unpack(in_ref, e_ref, out_ref):
    e = e_ref[...]
    match, again = repeats(e)
    rank = jnp.sum(again, axis=0, keepdims=True)
    row = iota((2 * BLOCK, BLOCK), 0)
    slot = row & 15
    first = (slot == (e & 7)) & ((row >> 4) == (e >> 3)) & (rank < 0.5)
    second = (slot == 8) & (rank > 0.5)
    rows = in_ref[:, :, 512 : 512 + DQ].reshape(2 * BLOCK, DQ)
    gh = tn(rows, hot(first | second)).astype(BF)
    out_ref[...] = jnp.broadcast_to(gh[None], (NH, DQ, BLOCK))


def finish(in_ref, all_ref, wo_ref, k_ref, v_ref, gh_ref, gq_ref, gk_ref, gv_ref):
    scaling = 1.0 / math.sqrt(HD * BLOCK * BLOCK)

    def whole(at):
        a = in_ref[:, :, at : at + HD].reshape(NP, 1, 16, HD)
        b = in_ref[:, :, at + HD : at + 2 * HD].reshape(NP, 1, 16, HD)
        return jnp.concatenate([a, b], axis=1).reshape(HD, HD)

    qt, kr = whole(0), whole(512)
    gh = nt(eye(BLOCK), all_ref[...].reshape(D, BLOCK)).astype(BF)
    gh_ref[...] = gh
    hg = nt(gh, wo_ref[...]).astype(BF)
    gq_ref[...] = (scaling * nt(hg, kr)).astype(BF)
    gk_ref[...] = (scaling * nn(v_ref[...], qt)).astype(BF)
    gv_ref[...] = (scaling * nt(k_ref[...], qt)).astype(BF)


def swap(tiles, axis):
    return lax.all_to_all(tiles, axis, split_axis=0, concat_axis=0, tiled=True)


def shards(out_grad, expert_of, counts, w_up, w_down, pre_act, queries, keys, values, w_out):
    e = expert_of.reshape(1, BLOCK)
    c = counts.reshape(1, BLOCK)
    rows_t = sds(NH, DQ, 2 * BLOCK)
    sent = call(pack, sds(NP, 16, 1024), e, out_grad.T, queries, keys, values, far=range(5))
    sent = call(forward, sds(NZ, 16, 512), swap(sent, PLANE))
    recv = swap(sent, "z")
    mask = call(masks, sds(D, 2 * BLOCK), c, pre_act, far=(0, 1))
    own, key = call(arrive, [rows_t, sds(8, 64)], recv, c, far=(1,))
    parts = call(experts, rows_t, swap(own, "y"), mask, w_down[0], w_up[0])
    own = call(add_up, rows_t, swap(parts, "y"), own)
    back = call(combine, sds(NP, 16, 896), swap(own, "y"), own, recv, w_out)
    back = call(regroup, sds(NZ, 16, 768), swap(back, PLANE), key)
    back = swap(back, "z")
    states = call(reduce_states, sds(NP, 16, 1024), back)
    own = call(unpack, sds(NH, DQ, BLOCK), back, e, far=(1,))
    states, rows = swap(states, PLANE), swap(own, "y")
    outs = [sds(BLOCK, D)] + [sds(BLOCK, HD)] * 3
    return tuple(call(finish, outs, states, rows, w_out, keys, values, home=True))


def solution(mesh):
    finer = Mesh(mesh.devices.reshape(16, 4, 2, mesh.shape["head"]), ("z", "x", "c", "y"))
    return jax.shard_map(
        shards,
        mesh=finer,
        in_specs=(
            P(SEQ, "y"),
            P(SEQ),
            P(None, SEQ),
            P(SEQ, None, "y"),
            P(SEQ, "y", None),
            P(SEQ, "y"),
            P(SEQ, "y"),
            P(SEQ, "y"),
            P(SEQ, "y"),
            P("y", None),
        ),
        out_specs=(P(SEQ, None), P(SEQ, "y"), P(SEQ, "y"), P(SEQ, "y")),
        check_vma=False,
    )
```

time: 177 us -> 146 us (0.82)
  Pallas kernels: 20.5 us -> 11.5 us
  blocking collectives: 124 us -> 116 us
  starting transfers between devices: 14 us -> 7.55 us
  local copies, waits for them, and re-layouts: 5.79 us -> 0.02 us
    pallas_call x8 -> x11, Pallas kernels: 20.5 us -> 11.5 us  [call(): pl.pallas_call(kernel, out_shape=shapes if home else [pltpu.VMEM(s.shape,...]
    all_to_all x4 -> x7, blocking collectives: 124 us -> 116 us  [swap(): return lax.all_to_all(tiles, axis, split_axis=0, concat_axis=0, tiled=True)]
    all_to_all x2, starting transfers between devices: 14 us -> 7.55 us  [swap(): return lax.all_to_all(tiles, axis, split_axis=0, concat_axis=0, tiled=True)]
    unnamed x12 -> x10, local copies, waits for them, and re-layouts: 3.73 us -> 0.02 us
  transfers between devices with their start and end apart: 2 -> 2, of which waited for: 2 -> 2; matrix products, arithmetic and copies ran while one was open for 0% -> 0% of each run, Pallas kernels for 3% -> 1%
where the time goes in v2:
time: 146 us
  blocking collectives  116 us (79%)
  Pallas kernels  11.5 us (8%)
  waiting for transfers between devices  9.8 us (7%)
  starting transfers between devices  7.55 us (5%)
    all_to_all x7, blocking collectives, swap(): return lax.all_to_all(tiles, axis, split_axis=0, concat_axis=0, tiled=True)  116 us
    pallas_call x11, Pallas kernels, call(): pl.pallas_call(kernel, out_shape=shapes if home else [pltpu.VMEM(s.shape,...  11.5 us
    all_to_all x2, waiting for transfers between devices, swap(): return lax.all_to_all(tiles, axis, split_axis=0, concat_axis=0, tiled=True)  9.8 us
    all_to_all x2, starting transfers between devices, swap(): return lax.all_to_all(tiles, axis, split_axis=0, concat_axis=0, tiled=True)  7.55 us
  transfers between devices with their start and end apart: 2, of which 2 were waited for; matrix products, arithmetic and copies ran while one was open for 0% of the time, Pallas kernels for 1%

profile of v2, /device:TPU:1, one launch (start us, length us, event | category | flops | bytes accessed | tf_op | source)
XLA Modules:
  0.0 145.6 jit_solution(10851885328270984693)
XLA Ops:
  0.6 1.4 pack.1
  2.1 15.7 %all_to_all.45.in_ref = bf16[8,16,1024]{2,1,0:T(8,128)(2,1)S(1)} all-to-all(bf16[8,16,1024]{2,1,0:T(8,128)(2,1)S(1)} %pack.1), channel_id=1, replica_groups=mesh['z'=16,'x'=4,'c'=2,'y'=4] {'x','c'}, dimensions={0} | all-to-all | bytes 524288 | tf_op jit(solution)/shard_map/all_to_all | solution.py:244
  17.8 0.4 forward.1
  18.2 0.0 copy-start.1
  18.2 0.0 copy-start.2
  18.2 24.1 %all_to_all.46.in_ref.recv_ref = bf16[16,16,512]{2,1,0:T(8,128)(2,1)S(1)} all-to-all(bf16[16,16,512]{2,1,0:T(8,128)(2,1)S(1)} %forward.1), channel_id=1, replica_groups=mesh['z'=16,'x'=4,'c'=2,'y'=4] {'z'}, dimensions={0} | all-to-all | bytes 524288 | tf_op jit(solution)/shard_map/all_to_all | solution.py:244
  42.3 1.7 %arrive.1 = (bf16[4,192,256]{2,1,0:T(8,128)(2,1)}, bf16[8,64]{1,0:T(8,128)(2,1)S(1)}) custom-call(bf16[16,16,512]{2,1,0:T(8,128)(2,1)S(1)} %all_to_all.46.in_ref.recv_ref, s32[1,128]{1,0:T(1,128)} %bitcast.10), custom_call_target="tpu_custom_call" | custom-call | flops 100000000 | bytes 262656 | tf_op jit(solution)/shard_map/arrive/pallas_call | solution.py:51
  44.0 4.2 %all-to-all-start.2 = ((bf16[4,192,256]{2,1,0:T(8,128)(2,1)}), bf16[4,192,256]{2,1,0:T(8,128)(2,1)S(1)}, u32[]{:S(2)}, u32[]{:S(2)}) async-start(bf16[4,192,256]{2,1,0:T(8,128)(2,1)} %get-tuple-element.6.rows_ref), calls=%async_computation.2 | async-start | bytes 786432 | tf_op jit(solution)/shard_map/all_to_all | solution.py:244
  48.2 1.5 masks.1.mask_ref
  49.7 4.8 %all-to-all-done.2.rows_ref = bf16[4,192,256]{2,1,0:T(8,128)(2,1)S(1)} async-done(((bf16[4,192,256]{2,1,0:T(8,128)(2,1)}), bf16[4,192,256]{2,1,0:T(8,128)(2,1)S(1)}, u32[]{:S(2)}, u32[]{:S(2)}) %all-to-all-start.2) | async-done | bytes 393248 | tf_op jit(solution)/shard_map/all_to_all | solution.py:244
  54.4 1.3 experts.1
  55.8 8.6 %all_to_all.47.parts_ref = bf16[4,192,256]{2,1,0:T(8,128)(2,1)S(1)} all-to-all(bf16[4,192,256]{2,1,0:T(8,128)(2,1)S(1)} %experts.1), channel_id=1, replica_groups=mesh['z'=16,'x'=4,'c'=2,'y'=4] {'y'}, dimensions={0} | all-to-all | bytes 786432 | tf_op jit(solution)/shard_map/all_to_all | solution.py:244
  64.4 1.1 add_up.1.own_ref
  65.5 9.5 %all_to_all.48.all_ref = bf16[4,192,256]{2,1,0:T(8,128)(2,1)S(1)} all-to-all(bf16[4,192,256]{2,1,0:T(8,128)(2,1)S(1)} %add_up.1.own_ref), channel_id=1, replica_groups=mesh['z'=16,'x'=4,'c'=2,'y'=4] {'y'}, dimensions={0} | all-to-all | bytes 786432 | tf_op jit(solution)/shard_map/all_to_all | solution.py:244
  75.0 0.6 combine.1
  75.6 18.9 %all_to_all.49.in_ref = bf16[8,16,896]{2,1,0:T(8,128)(2,1)S(1)} all-to-all(bf16[8,16,896]{2,1,0:T(8,128)(2,1)S(1)} %combine.1), channel_id=1, replica_groups=mesh['z'=16,'x'=4,'c'=2,'y'=4] {'x','c'}, dimensions={0} | all-to-all | bytes 458752 | tf_op jit(solution)/shard_map/all_to_all | solution.py:244
  94.5 0.3 regroup.1
  94.8 23.0 %all_to_all.50.in_ref = bf16[16,16,768]{2,1,0:T(8,128)(2,1)S(1)} all-to-all(bf16[16,16,768]{2,1,0:T(8,128)(2,1)S(1)} %regroup.1), channel_id=1, replica_groups=mesh['z'=16,'x'=4,'c'=2,'y'=4] {'z'}, dimensions={0} | all-to-all | bytes 786432 | tf_op jit(solution)/shard_map/all_to_all | solution.py:244
  117.8 1.7 %unpack.1 = bf16[4,192,128]{2,1,0:T(8,128)(2,1)} custom-call(bf16[16,16,768]{2,1,0:T(8,128)(2,1)S(1)} %all_to_all.50.in_ref, s32[1,128]{1,0:T(1,128)} %bitcast.9), custom_call_target="tpu_custom_call" | custom-call | flops 100000000 | bytes 393728 | tf_op jit(solution)/shard_map/unpack/pallas_call | solution.py:51
  119.5 3.4 %all-to-all-start.8 = ((bf16[4,192,128]{2,1,0:T(8,128)(2,1)}), bf16[4,192,128]{2,1,0:T(8,128)(2,1)S(1)}, u32[]{:S(2)}, u32[]{:S(2)}) async-start(bf16[4,192,128]{2,1,0:T(8,128)(2,1)} %unpack.1), calls=%async_computation.8 | async-start | bytes 393216 | tf_op jit(solution)/shard_map/all_to_all | solution.py:244
  122.9 0.1 reduce_states.1
  123.0 5.0 %all-to-all-done.8.all_ref = bf16[4,192,128]{2,1,0:T(8,128)(2,1)S(1)} async-done(((bf16[4,192,128]{2,1,0:T(8,128)(2,1)}), bf16[4,192,128]{2,1,0:T(8,128)(2,1)S(1)}, u32[]{:S(2)}, u32[]{:S(2)}) %all-to-all-start.8) | async-done | bytes 196640 | tf_op jit(solution)/shard_map/all_to_all | solution.py:244
  128.0 16.3 %all_to_all.51.in_ref = bf16[8,16,1024]{2,1,0:T(8,128)(2,1)S(1)} all-to-all(bf16[8,16,1024]{2,1,0:T(8,128)(2,1)S(1)} %reduce_states.1), channel_id=1, replica_groups=mesh['z'=16,'x'=4,'c'=2,'y'=4] {'x','c'}, dimensions={0} | all-to-all | bytes 524288 | tf_op jit(solution)/shard_map/all_to_all | solution.py:244
  144.3 1.3 finish.1
  (8 shorter events, 0.0 us)
Async XLA Ops:
  18.2 36.2 %copy-start.1 = (bf16[1,768,768]{2,1,0:T(8,128)(2,1)S(1)}, bf16[1,768,768]{2,1,0:T(8,128)(2,1)}, u32[]{:S(2)}) copy-start(bf16[1,768,768]{2,1,0:T(8,128)(2,1)} %param.14) | copy-start | bytes 3538948
  18.2 36.2 %copy-start.2 = (bf16[1,768,768]{2,1,0:T(8,128)(2,1)S(1)}, bf16[1,768,768]{2,1,0:T(8,128)(2,1)}, u32[]{:S(2)}) copy-start(bf16[1,768,768]{2,1,0:T(8,128)(2,1)} %param.13) | copy-start | bytes 3538948
  44.0 10.4 %all-to-all-start.2 = ((bf16[4,192,256]{2,1,0:T(8,128)(2,1)}), bf16[4,192,256]{2,1,0:T(8,128)(2,1)S(1)}, u32[]{:S(2)}, u32[]{:S(2)}) async-start(bf16[4,192,256]{2,1,0:T(8,128)(2,1)} %get-tuple-element.6.rows_ref), calls=%async_computation.2 | async-start | bytes 786432 | tf_op jit(solution)/shard_map/all_to_all | solution.py:244
  64.4 10.6 %copy-start = (bf16[256,768]{1,0:T(8,128)(2,1)S(1)}, bf16[256,768]{1,0:T(8,128)(2,1)}, u32[]{:S(2)}) copy-start(bf16[256,768]{1,0:T(8,128)(2,1)} %wo_ref.3) | copy-start | bytes 1179652
  117.8 26.5 %copy-start.3 = (bf16[128,256]{1,0:T(8,128)(2,1)S(1)}, bf16[128,256]{1,0:T(8,128)(2,1)}, u32[]{:S(2)}) copy-start(bf16[128,256]{1,0:T(8,128)(2,1)} %k_ref.3) | copy-start | bytes 196612
  117.8 26.5 %copy-start.4 = (bf16[128,256]{1,0:T(8,128)(2,1)S(1)}, bf16[128,256]{1,0:T(8,128)(2,1)}, u32[]{:S(2)}) copy-start(bf16[128,256]{1,0:T(8,128)(2,1)} %v_ref.3) | copy-start | bytes 196612
  119.5 8.5 %all-to-all-start.8 = ((bf16[4,192,128]{2,1,0:T(8,128)(2,1)}), bf16[4,192,128]{2,1,0:T(8,128)(2,1)S(1)}, u32[]{:S(2)}, u32[]{:S(2)}) async-start(bf16[4,192,128]{2,1,0:T(8,128)(2,1)} %unpack.1), calls=%async_computation.8 | async-start | bytes 393216 | tf_op jit(solution)/shard_map/all_to_all | solution.py:244

commit v3 on v2

--- a/solution.py
+++ b/solution.py
@@ -43,14 +43,14 @@
     return parts[:, 0], parts[:, 1]
 
 
-def call(kernel, outs, *args, far=(), home=False):
+def call(kernel, outs, *args, far=(), home=0):
     single = not isinstance(outs, (list, tuple))
     shapes = [outs] if single else list(outs)
     nbytes = sum(a.size * a.dtype.itemsize for a in args)
     near = pltpu.with_memory_space_constraint
     res = pl.pallas_call(
         kernel,
-        out_shape=shapes if home else [pltpu.VMEM(s.shape, s.dtype) for s in shapes],
+        out_shape=[s if n < home else pltpu.VMEM(s.shape, s.dtype) for n, s in enumerate(shapes)],
         in_specs=[VMEM] * len(args),
         out_specs=[VMEM] * len(shapes),
         cost_estimate=pl.CostEstimate(flops=10**8, bytes_accessed=nbytes, transcendentals=0),
@@ -135,16 +135,17 @@
     mask_ref[...] = jnp.transpose(nn(pick, on)).astype(BF)
 
 
-def arrive(in_ref, c_ref, out_ref, key_ref):
+def arrive(in_ref, c_ref, own_ref, out_ref, key_ref):
     _, live = place(c_ref[...].astype(F32))
     x = in_ref[:, :, 0:DQ].reshape(2 * BLOCK, DQ).astype(F32)
     x = jnp.where(live, x, 0.0).astype(BF)
     x = nt(eye(DQ), x).astype(BF)
+    own_ref[...] = x
     out_ref[...] = jnp.broadcast_to(x[None], (NH, DQ, 2 * BLOCK))
     total = in_ref[0, 0:8, 448:512].astype(F32)
     for z in range(1, NZ):
         total = total + in_ref[z, 0:8, 448:512].astype(F32)
-    key_ref[...] = total.astype(BF)
+    key_ref[...] = jnp.concatenate([total[0:4], total[4:8]], axis=1)
 
 
 def experts(rows_ref, mask_ref, wd_ref, wu_ref, out_ref):
@@ -157,11 +158,11 @@
     total = parts_ref[0].astype(F32)
     for h in range(1, NH):
         total = total + parts_ref[h].astype(F32)
-    gh = (rows_ref[0].astype(F32) + total.astype(BF).astype(F32)).astype(BF)
+    gh = (rows_ref[...].astype(F32) + total.astype(BF).astype(F32)).astype(BF)
     out_ref[...] = jnp.broadcast_to(gh[None], (NH, DQ, 2 * BLOCK))
 
 
-def combine(all_ref, own_ref, recv_ref, wo_ref, out_ref):
+def combine(all_ref, recv_ref, wo_ref, out_ref):
     gh = all_ref[...].reshape(D, 2 * BLOCK)
     hg = nn(wo_ref[...], gh).astype(BF)
     q = recv_ref[:, :, DQ:448].reshape(2 * BLOCK, HD)
@@ -169,29 +170,38 @@
     o = iota((BLOCK, 2 * BLOCK), 0)
     i = iota((BLOCK, 2 * BLOCK), 1)
     same = ((o >> 4) == (i & 7)) & ((o & 15) == (i >> 4))
-    own = own_ref[0]
-    firsts = nt(hot(same & ((i & 8) == 0)), own)
-    seconds = nt(hot(same & ((i & 8) != 0)), own)
-    rows = jnp.concatenate([firsts, seconds], axis=1)
-    out_ref[:, :, 0:384] = rows.astype(BF).reshape(NP, 16, 384)
-    out_ref[:, :, 384:640] = a.astype(BF)
-    out_ref[:, :, 640:896] = b.astype(BF)
+    out_ref[:, :, 0:D] = nt(hot(same & ((i & 8) == 0)), gh).astype(BF).reshape(NP, 16, D)
+    out_ref[:, :, D : 2 * D] = nt(hot(same & ((i & 8) != 0)), gh).astype(BF).reshape(NP, 16, D)
+    out_ref[:, :, 1536:1792] = a.astype(BF)
+    out_ref[:, :, 1792:2048] = b.astype(BF)
 
 
 def regroup(in_ref, key_ref, out_ref):
-    total = in_ref[0, :, 384:896].astype(F32)
+    total = in_ref[0, :, 1536:2048].astype(F32)
     for p in range(1, NP):
-        total = total + in_ref[p, :, 384:896].astype(F32)
+        total = total + in_ref[p, :, 1536:2048].astype(F32)
     out_ref[:, :, 0:512] = jnp.broadcast_to(total.astype(BF)[None], (NZ, 16, 512))
+    x = in_ref[:, :, 0:D].reshape(BLOCK, D)
     o = iota((2 * BLOCK, BLOCK), 0)
     i = iota((2 * BLOCK, BLOCK), 1)
-    here = (o >> 4) == (i & 15)
-    firsts = nn(hot(here & ((o & 15) == (i >> 4))), in_ref[:, :, 0:DQ].reshape(BLOCK, DQ))
-    second = nn(hot(here & ((o & 15) == 8)), in_ref[:, :, DQ : 2 * DQ].reshape(BLOCK, DQ))
-    key = jnp.concatenate([key_ref[...].astype(F32), jnp.zeros((8, 64), F32)], axis=0)
-    key = jnp.broadcast_to(key[None], (NZ, 16, 64)).reshape(2 * BLOCK, 64)
-    rows = jnp.concatenate([firsts + second, key], axis=1)
-    out_ref[:, :, 512:768] = rows.astype(BF).reshape(NZ, 16, 256)
+    here = ((o & 7) == (i >> 4)) & ((o >> 4) == (i & 15))
+    lower, higher = hot(here & ((o & 8) == 0)), hot(here & ((o & 8) != 0))
+    rows = nn(lower, x[:, 0:384]) + nn(higher, x[:, 384:768])
+    out_ref[:, :, 512:896] = rows.astype(BF).reshape(NZ, 16, 384)
+    second = in_ref[0, :, D : 2 * D].astype(F32)
+    for p in range(1, NP):
+        second = second + in_ref[p, :, D : 2 * D].astype(F32)
+    second = second.astype(BF)
+    o = iota((2 * BLOCK, NZ), 0)
+    i = iota((2 * BLOCK, NZ), 1)
+    rows = jnp.zeros((2 * BLOCK, BLOCK), F32)
+    for n in range(6):
+        pick = hot(((o >> 4) == i) & ((o & 15) == n))
+        rows = rows + nn(pick, second[:, n * BLOCK : (n + 1) * BLOCK])
+    nothing = jnp.zeros((8, BLOCK), F32)
+    key = jnp.concatenate([nothing, key_ref[...], nothing[0:4]], axis=0)
+    rows = rows.reshape(NZ, 16, BLOCK) + key[None]
+    out_ref[:, :, 896:1024] = rows.astype(BF)
 
 
 def reduce_states(in_ref, out_ref):
@@ -202,7 +212,9 @@
     lower = [None] * 8
     for z in range(NZ):
         row, lane = tile_of(z)
-        (lower if row else upper)[lane // 64] = in_ref[z, 0:8, 704:768].astype(F32)
+        piece = in_ref[z, 8:16, 896:1024].astype(F32)
+        piece = jnp.concatenate([piece[0:4, 0:64], piece[0:4, 64:128]], axis=0)
+        (lower if row else upper)[lane // 64] = piece
     key = jnp.concatenate(
         [jnp.concatenate(upper, axis=1), jnp.concatenate(lower, axis=1)], axis=0
     )
@@ -210,20 +222,32 @@
     out_ref[:, :, 512:1024] = jnp.broadcast_to(key.astype(BF)[None], (NP, 16, 512))
 
 
-def unpack(in_ref, e_ref, out_ref):
+def unpack(in_ref, e_ref, wo_ref, gh_ref, hg_ref):
     e = e_ref[...]
     match, again = repeats(e)
     rank = jnp.sum(again, axis=0, keepdims=True)
     row = iota((2 * BLOCK, BLOCK), 0)
-    slot = row & 15
-    first = (slot == (e & 7)) & ((row >> 4) == (e >> 3)) & (rank < 0.5)
-    second = (slot == 8) & (rank > 0.5)
-    rows = in_ref[:, :, 512 : 512 + DQ].reshape(2 * BLOCK, DQ)
-    gh = tn(rows, hot(first | second)).astype(BF)
-    out_ref[...] = jnp.broadcast_to(gh[None], (NH, DQ, BLOCK))
-
-
-def finish(in_ref, all_ref, wo_ref, k_ref, v_ref, gh_ref, gq_ref, gk_ref, gv_ref):
+    first = ((row & 7) == (e & 7)) & ((row >> 4) == (e >> 3)) & (rank < 0.5)
+    rows = in_ref[:, :, 512:896].reshape(2 * BLOCK, 384)
+    second = in_ref[0, 0:8, 896:1024].astype(F32)
+    for z in range(1, NZ):
+        second = second + in_ref[z, 0:8, 896:1024].astype(F32)
+    second = jnp.concatenate([second[n : n + 1] for n in range(6)], axis=1)
+    second = jnp.broadcast_to(second, (16, D)).astype(BF)
+    one = iota((16, BLOCK), 0) == 0
+    gh = jnp.concatenate(
+        [
+            tn(hot(first & ((row & 8) == 0)), rows),
+            tn(hot(first & ((row & 8) != 0)), rows),
+        ],
+        axis=1,
+    )
+    gh = (gh + tn(hot(one & (rank > 0.5)), second)).astype(BF)
+    gh_ref[...] = gh
+    hg_ref[...] = nt(gh, wo_ref[...]).astype(BF)
+
+
+def finish(in_ref, hg_ref, k_ref, v_ref, gq_ref, gk_ref, gv_ref):
     scaling = 1.0 / math.sqrt(HD * BLOCK * BLOCK)
 
     def whole(at):
@@ -232,10 +256,7 @@
         return jnp.concatenate([a, b], axis=1).reshape(HD, HD)
 
     qt, kr = whole(0), whole(512)
-    gh = nt(eye(BLOCK), all_ref[...].reshape(D, BLOCK)).astype(BF)
-    gh_ref[...] = gh
-    hg = nt(gh, wo_ref[...]).astype(BF)
-    gq_ref[...] = (scaling * nt(hg, kr)).astype(BF)
+    gq_ref[...] = (scaling * nt(hg_ref[...], kr)).astype(BF)
     gk_ref[...] = (scaling * nn(v_ref[...], qt)).astype(BF)
     gv_ref[...] = (scaling * nt(k_ref[...], qt)).astype(BF)
 
@@ -252,17 +273,18 @@
     sent = call(forward, sds(NZ, 16, 512), swap(sent, PLANE))
     recv = swap(sent, "z")
     mask = call(masks, sds(D, 2 * BLOCK), c, pre_act, far=(0, 1))
-    own, key = call(arrive, [rows_t, sds(8, 64)], recv, c, far=(1,))
-    parts = call(experts, rows_t, swap(own, "y"), mask, w_down[0], w_up[0])
-    own = call(add_up, rows_t, swap(parts, "y"), own)
-    back = call(combine, sds(NP, 16, 896), swap(own, "y"), own, recv, w_out)
-    back = call(regroup, sds(NZ, 16, 768), swap(back, PLANE), key)
+    own, rows, key = call(
+        arrive, [sds(DQ, 2 * BLOCK), rows_t, sds(4, BLOCK, dtype=F32)], recv, c
+    )
+    parts = call(experts, rows_t, swap(rows, "y"), mask, w_down[0], w_up[0])
+    rows = call(add_up, rows_t, swap(parts, "y"), own)
+    back = call(combine, sds(NP, 16, 2048), swap(rows, "y"), recv, w_out)
+    back = call(regroup, sds(NZ, 16, 1024), swap(back, PLANE), key)
     back = swap(back, "z")
-    states = call(reduce_states, sds(NP, 16, 1024), back)
-    own = call(unpack, sds(NH, DQ, BLOCK), back, e, far=(1,))
-    states, rows = swap(states, PLANE), swap(own, "y")
-    outs = [sds(BLOCK, D)] + [sds(BLOCK, HD)] * 3
-    return tuple(call(finish, outs, states, rows, w_out, keys, values, home=True))
+    states = swap(call(reduce_states, sds(NP, 16, 1024), back), PLANE)
+    gh, hg = call(unpack, [sds(BLOCK, D), sds(BLOCK, HD)], back, e, w_out, home=1)
+    outs = [sds(BLOCK, HD)] * 3
+    return (gh, *call(finish, outs, states, hg, keys, values, home=3))
 
 
 def solution(mesh):

time: 146 us -> 144 us (0.986)
  blocking collectives: 116 us -> 108 us
  starting transfers between devices: 7.55 us -> 14.4 us
  Pallas kernels: 11.5 us -> 9.81 us
    all_to_all x7 -> x6, blocking collectives: 116 us -> 108 us  [swap(): return lax.all_to_all(tiles, axis, split_axis=0, concat_axis=0, tiled=True)]
    all_to_all x2, starting transfers between devices: 7.55 us -> 14.4 us  [swap(): return lax.all_to_all(tiles, axis, split_axis=0, concat_axis=0, tiled=True)]
    pallas_call x11, Pallas kernels: 11.5 us -> 9.81 us  [call(): pl.pallas_call(kernel, out_shape=[s if n < home else pltpu.VMEM(s.shape,...]
  transfers between devices with their start and end apart: 2 -> 2, of which waited for: 2 -> 2; matrix products, arithmetic and copies ran while one was open for 0% -> 0% of each run, Pallas kernels for 1% -> 2%
where the time goes in v3:
time: 144 us; the launch traced here: 143 us
  blocking collectives  108 us (75%)
  starting transfers between devices  14.4 us (10%)
  waiting for transfers between devices  10.1 us (7%)
  Pallas kernels  9.81 us (7%)
    all_to_all x6, blocking collectives, swap(): return lax.all_to_all(tiles, axis, split_axis=0, concat_axis=0, tiled=True)  108 us
    all_to_all x2, starting transfers between devices, swap(): return lax.all_to_all(tiles, axis, split_axis=0, concat_axis=0, tiled=True)  14.4 us
    all_to_all x2, waiting for transfers between devices, swap(): return lax.all_to_all(tiles, axis, split_axis=0, concat_axis=0, tiled=True)  10.1 us
    pallas_call x11, Pallas kernels, call(): pl.pallas_call(kernel, out_shape=[s if n < home else pltpu.VMEM(s.shape,...  9.81 us
  transfers between devices with their start and end apart: 2, of which 2 were waited for; matrix products, arithmetic and copies ran while one was open for 0% of the time, Pallas kernels for 2%

profile of v3, /device:TPU:1, one launch (start us, length us, event | category | flops | bytes accessed | tf_op | source)
XLA Modules:
  0.0 143.0 jit_solution(13668394549070449724)
XLA Ops:
  0.6 1.4 %pack.1 = bf16[8,16,1024]{2,1,0:T(8,128)(2,1)S(1)} custom-call(s32[1,128]{1,0:T(1,128)} %bitcast.7, bf16[192,128]{1,0:T(8,128)(2,1)} %bitcast.11, bf16[128,256]{1,0:T(8,128)(2,1)} %q_ref.1, bf16[128,256]{1,0:T(8,128)(2,1)} %k_ref.3, bf16[128,256]{1,0:T(8,128)(2,1)} %v_ref.3), custom_call_target="tpu_custom_call" | custom-call | flops 100000000 | bytes 246272 | tf_op jit(solution)/shard_map/pack/pallas_call | solution.py:51
  2.1 15.7 %all_to_all.40.in_ref = bf16[8,16,1024]{2,1,0:T(8,128)(2,1)S(1)} all-to-all(bf16[8,16,1024]{2,1,0:T(8,128)(2,1)S(1)} %pack.1), channel_id=1, replica_groups=mesh['z'=16,'x'=4,'c'=2,'y'=4] {'x','c'}, dimensions={0} | all-to-all | bytes 524288 | tf_op jit(solution)/shard_map/all_to_all | solution.py:265
  17.8 0.4 forward.1
  18.2 0.0 copy-start.1
  18.2 0.0 copy-start.2
  18.2 24.1 %all_to_all.41.in_ref.recv_ref = bf16[16,16,512]{2,1,0:T(8,128)(2,1)S(1)} all-to-all(bf16[16,16,512]{2,1,0:T(8,128)(2,1)S(1)} %forward.1), channel_id=1, replica_groups=mesh['z'=16,'x'=4,'c'=2,'y'=4] {'z'}, dimensions={0} | all-to-all | bytes 524288 | tf_op jit(solution)/shard_map/all_to_all | solution.py:265
  42.3 1.1 arrive.1
  43.4 4.2 %all-to-all-start.2 = ((bf16[4,192,256]{2,1,0:T(8,128)(2,1)}), bf16[4,192,256]{2,1,0:T(8,128)(2,1)S(1)}, u32[]{:S(2)}, u32[]{:S(2)}) async-start(bf16[4,192,256]{2,1,0:T(8,128)(2,1)} %get-tuple-element.12), calls=%async_computation.2 | async-start | bytes 786432 | tf_op jit(solution)/shard_map/all_to_all | solution.py:265
  47.6 1.5 %masks.1.mask_ref = bf16[768,256]{1,0:T(8,128)(2,1)S(1)} custom-call(s32[1,128]{1,0:T(1,128)} %bitcast.9, bf16[256,768]{1,0:T(8,128)(2,1)} %pre_ref.1), custom_call_target="tpu_custom_call" | custom-call | flops 100000000 | bytes 393728 | tf_op jit(solution)/shard_map/masks/pallas_call | solution.py:51
  49.0 4.8 %all-to-all-done.2.rows_ref = bf16[4,192,256]{2,1,0:T(8,128)(2,1)S(1)} async-done(((bf16[4,192,256]{2,1,0:T(8,128)(2,1)}), bf16[4,192,256]{2,1,0:T(8,128)(2,1)S(1)}, u32[]{:S(2)}, u32[]{:S(2)}) %all-to-all-start.2) | async-done | bytes 393248 | tf_op jit(solution)/shard_map/all_to_all | solution.py:265
  53.8 1.3 experts.1
  55.2 0.0 copy-start
  55.2 8.8 %all_to_all.42.parts_ref = bf16[4,192,256]{2,1,0:T(8,128)(2,1)S(1)} all-to-all(bf16[4,192,256]{2,1,0:T(8,128)(2,1)S(1)} %experts.1), channel_id=1, replica_groups=mesh['z'=16,'x'=4,'c'=2,'y'=4] {'y'}, dimensions={0} | all-to-all | bytes 786432 | tf_op jit(solution)/shard_map/all_to_all | solution.py:265
  63.9 0.1 add_up.1
  64.0 10.6 %all_to_all.43.all_ref = bf16[4,192,256]{2,1,0:T(8,128)(2,1)S(1)} all-to-all(bf16[4,192,256]{2,1,0:T(8,128)(2,1)S(1)} %add_up.1), channel_id=1, replica_groups=mesh['z'=16,'x'=4,'c'=2,'y'=4] {'y'}, dimensions={0} | all-to-all | bytes 786432 | tf_op jit(solution)/shard_map/all_to_all | solution.py:265
  74.6 0.7 combine.1
  75.4 22.0 %all_to_all.44.in_ref = bf16[8,16,2048]{2,1,0:T(8,128)(2,1)S(1)} all-to-all(bf16[8,16,2048]{2,1,0:T(8,128)(2,1)S(1)} %combine.1), channel_id=1, replica_groups=mesh['z'=16,'x'=4,'c'=2,'y'=4] {'x','c'}, dimensions={0} | all-to-all | bytes 1048576 | tf_op jit(solution)/shard_map/all_to_all | solution.py:265
  97.3 0.4 regroup.1
  97.8 26.8 %all_to_all.45.in_ref = bf16[16,16,1024]{2,1,0:T(8,128)(2,1)S(1)} all-to-all(bf16[16,16,1024]{2,1,0:T(8,128)(2,1)S(1)} %regroup.1), channel_id=1, replica_groups=mesh['z'=16,'x'=4,'c'=2,'y'=4] {'z'}, dimensions={0} | all-to-all | bytes 1048576 | tf_op jit(solution)/shard_map/all_to_all | solution.py:265
  124.6 0.9 reduce_states.1
  125.5 10.2 %all-to-all-start.7 = ((bf16[8,16,1024]{2,1,0:T(8,128)(2,1)}), bf16[8,16,1024]{2,1,0:T(8,128)(2,1)S(1)}, u32[]{:S(2)}, u32[]{:S(2)}) async-start(bf16[8,16,1024]{2,1,0:T(8,128)(2,1)} %reduce_states.1), calls=%async_computation.7 | async-start | bytes 524288 | tf_op jit(solution)/shard_map/all_to_all | solution.py:265
  135.6 1.2 unpack.1
  136.8 5.3 %all-to-all-done.7.in_ref = bf16[8,16,1024]{2,1,0:T(8,128)(2,1)S(1)} async-done(((bf16[8,16,1024]{2,1,0:T(8,128)(2,1)}), bf16[8,16,1024]{2,1,0:T(8,128)(2,1)S(1)}, u32[]{:S(2)}, u32[]{:S(2)}) %all-to-all-start.7) | async-done | bytes 262176 | tf_op jit(solution)/shard_map/all_to_all | solution.py:265
  142.1 0.9 finish.1
  (11 shorter events, 0.0 us)
Async XLA Ops:
  0.6 41.7 %copy-start.6 = (s32[128,1]{0,1:T(1,128)S(1)}, s32[128,1]{0,1:T(1,128)}, u32[]{:S(2)}) copy-start(s32[128,1]{0,1:T(1,128)} %param.12) | copy-start | bytes 1540
  18.2 35.6 %copy-start.1 = (bf16[1,768,768]{2,1,0:T(8,128)(2,1)S(1)}, bf16[1,768,768]{2,1,0:T(8,128)(2,1)}, u32[]{:S(2)}) copy-start(bf16[1,768,768]{2,1,0:T(8,128)(2,1)} %param.14) | copy-start | bytes 3538948
  18.2 35.6 %copy-start.2 = (bf16[1,768,768]{2,1,0:T(8,128)(2,1)S(1)}, bf16[1,768,768]{2,1,0:T(8,128)(2,1)}, u32[]{:S(2)}) copy-start(bf16[1,768,768]{2,1,0:T(8,128)(2,1)} %param.13) | copy-start | bytes 3538948
  43.4 10.4 %all-to-all-start.2 = ((bf16[4,192,256]{2,1,0:T(8,128)(2,1)}), bf16[4,192,256]{2,1,0:T(8,128)(2,1)S(1)}, u32[]{:S(2)}, u32[]{:S(2)}) async-start(bf16[4,192,256]{2,1,0:T(8,128)(2,1)} %get-tuple-element.12), calls=%async_computation.2 | async-start | bytes 786432 | tf_op jit(solution)/shard_map/all_to_all | solution.py:265
  55.2 19.5 %copy-start = (bf16[256,768]{1,0:T(8,128)(2,1)S(1)}, bf16[256,768]{1,0:T(8,128)(2,1)}, u32[]{:S(2)}) copy-start(bf16[256,768]{1,0:T(8,128)(2,1)} %wo_ref.3) | copy-start | bytes 1179652
  97.7 37.9 %copy-start.5 = (s32[128]{0:T(128)S(1)}, s32[128]{0:T(128)}, u32[]{:S(2)}) copy-start(s32[128]{0:T(128)} %param.11) | copy-start | bytes 1540
  124.6 17.5 %copy-start.3 = (bf16[128,256]{1,0:T(8,128)(2,1)S(1)}, bf16[128,256]{1,0:T(8,128)(2,1)}, u32[]{:S(2)}) copy-start(bf16[128,256]{1,0:T(8,128)(2,1)} %k_ref.3) | copy-start | bytes 196612
  124.6 17.5 %copy-start.4 = (bf16[128,256]{1,0:T(8,128)(2,1)S(1)}, bf16[128,256]{1,0:T(8,128)(2,1)}, u32[]{:S(2)}) copy-start(bf16[128,256]{1,0:T(8,128)(2,1)} %v_ref.3) | copy-start | bytes 196612
  125.5 16.7 %all-to-all-start.7 = ((bf16[8,16,1024]{2,1,0:T(8,128)(2,1)}), bf16[8,16,1024]{2,1,0:T(8,128)(2,1)S(1)}, u32[]{:S(2)}, u32[]{:S(2)}) async-start(bf16[8,16,1024]{2,1,0:T(8,128)(2,1)} %reduce_states.1), calls=%async_computation.7 | async-start | bytes 524288 | tf_op jit(solution)/shard_map/all_to_all | solution.py:265

commit v4 on v3

v4 whole, which is shorter than its diff:
```python
import math

import jax
import jax.numpy as jnp
from jax import lax
from jax.experimental import pallas as pl
from jax.experimental.pallas import tpu as pltpu
from jax.sharding import Mesh
from jax.sharding import PartitionSpec as P

SEQ = ("z", "x", "c")
PLANE = ("x", "c")
BF, F32 = jnp.bfloat16, jnp.float32
NZ, NP, NH = 16, 8, 4
BLOCK = 128
D, HD, DQ = 768, 256, 192
LIMIT = 16 * 2**20
VMEM = pl.BlockSpec(memory_space=pltpu.VMEM)
SMEM = pl.BlockSpec(memory_space=pltpu.SMEM)


def nn(a, b):
    return lax.dot_general(a, b, (((1,), (0,)), ((), ())), preferred_element_type=F32)


def nt(a, b):
    return lax.dot_general(a, b, (((1,), (1,)), ((), ())), preferred_element_type=F32)


def tn(a, b):
    return lax.dot_general(a, b, (((0,), (0,)), ((), ())), preferred_element_type=F32)


def hot(cond):
    return jnp.where(cond, 1.0, 0.0).astype(BF)


def iota(shape, dim):
    return lax.broadcasted_iota(jnp.int32, shape, dim)


def halves(state):
    parts = state.reshape(NP, 2, 16, HD)
    return parts[:, 0], parts[:, 1]


def call(kernel, outs, *args, far=(), home=0, scalars=0):
    single = not isinstance(outs, (list, tuple))
    shapes = [outs] if single else list(outs)
    nbytes = sum(a.size * a.dtype.itemsize for a in args)

    def near(n, a):
        space = pltpu.HBM if n in far else pltpu.VMEM
        return a if n < scalars else pltpu.with_memory_space_constraint(a, space)

    res = pl.pallas_call(
        kernel,
        out_shape=[s if n < home else pltpu.VMEM(s.shape, s.dtype) for n, s in enumerate(shapes)],
        in_specs=[SMEM] * scalars + [VMEM] * (len(args) - scalars),
        out_specs=[VMEM] * len(shapes),
        cost_estimate=pl.CostEstimate(flops=10**8, bytes_accessed=nbytes, transcendentals=0),
        compiler_params=pltpu.CompilerParams(vmem_limit_bytes=LIMIT),
        name=kernel.__name__,
    )(*[near(n, a) for n, a in enumerate(args)])
    return res[0] if single else res


def sds(*shape, dtype=BF):
    return jax.ShapeDtypeStruct(shape, dtype)


def eye(n):
    return hot(iota((n, n), 0) == iota((n, n), 1))


def repeats(e):
    match = e == iota((BLOCK, BLOCK), 0)
    earlier = hot(iota((BLOCK, BLOCK), 0) < iota((BLOCK, BLOCK), 1))
    return match, jnp.where(match & (nn(hot(match), earlier) > 0.5), 1.0, 0.0)


def pack(e_ref, ogt_ref, q_ref, k_ref, v_ref, out_ref):
    match, again = repeats(e_ref[...])
    first = (jnp.where(match, 1.0, 0.0) - again).astype(BF)
    second = jnp.broadcast_to(jnp.sum(again, axis=0, keepdims=True), (16, BLOCK)).astype(BF)
    ogt, q = ogt_ref[...], q_ref[...]
    token = jnp.concatenate([nt(second, ogt), nn(second, q)], axis=1)
    spare = jnp.concatenate(
        [token[0:1, i * 64 : (i + 1) * 64] for i in range(7)] + [jnp.zeros((1, 64), F32)], axis=0
    )
    spare = jnp.broadcast_to(spare[None], (NZ, 8, 64)).reshape(BLOCK, 64)
    rows = jnp.concatenate([nt(first, ogt), nn(first, q), spare], axis=1)
    state = tn(k_ref[...], v_ref[...]).reshape(NZ, 2, 8, HD)
    state = jnp.concatenate([state[:, 0], state[:, 1]], axis=2)
    out = jnp.concatenate([rows.reshape(NZ, 8, 512), state], axis=1)
    out_ref[...] = out.astype(BF)


def forward(in_ref, out_ref, q_ref, sq_ref):
    x = in_ref[...].reshape(2 * BLOCK, 512)
    o = iota((BLOCK, 2 * BLOCK), 0)
    i = iota((BLOCK, 2 * BLOCK), 1)
    own = ((i >> 4) == (o & 15)) & ((i & 15) == (o >> 4))
    firsts = nn(hot(own), x[:, 0:448])
    q_ref[...] = firsts[:, DQ:448].astype(BF)
    spare = x[:, 448:512]
    o = iota((NZ, 2 * BLOCK), 0)
    i = iota((NZ, 2 * BLOCK), 1)
    seconds = jnp.concatenate(
        [nn(hot(((i >> 4) == o) & ((i & 15) == n)), spare) for n in range(7)], axis=1
    )
    sq_ref[...] = seconds[:, DQ:448].astype(BF)
    seconds = jnp.broadcast_to(seconds[None, :, 0:DQ], (NP, NZ, DQ)).reshape(BLOCK, DQ)
    total = in_ref[0, 8:16, :].astype(F32)
    for z in range(1, NZ):
        total = total + in_ref[z, 8:16, :].astype(F32)
    total = jnp.concatenate([total, jnp.zeros((8, 512), F32)], axis=0).astype(BF)
    o = iota((BLOCK, 16), 0)
    i = iota((BLOCK, 16), 1)
    key = jnp.zeros((BLOCK, BLOCK), F32)
    for n in range(4):
        pick = hot(((o >> 4) == i) & ((o & 15) == n))
        key = key + nn(pick, total[:, n * BLOCK : (n + 1) * BLOCK])
    rows = jnp.concatenate([firsts[:, 0:DQ], seconds, key], axis=1).astype(BF)
    rows = jnp.broadcast_to(rows.reshape(NP, 1, 16, 512), (NP, NH, 16, 512))
    out_ref[...] = rows.reshape(NP * NH, 16, 512)


def place(c):
    shape = (2 * BLOCK, BLOCK)
    o, s = iota(shape, 0), iota(shape, 1)
    block = (o & 15) * NP + ((o >> 4) & 7)
    c = jnp.broadcast_to(c, shape)
    before = jnp.sum(jnp.where(s < block, c, 0.0), axis=1, keepdims=True)
    count = jnp.sum(jnp.where(s == block, c, 0.0), axis=1, keepdims=True)
    r = (iota((2 * BLOCK, 1), 0) >> 7).astype(F32)
    return before + r, count > r + 0.5


def masks(c_ref, pre_ref, mask_ref):
    row, live = place(c_ref[...].astype(F32))
    pick = hot((iota((2 * BLOCK, 2 * BLOCK), 1).astype(F32) == row) & live)
    on = jnp.where(pre_ref[...].astype(F32) > 0, 1.0, 0.0).astype(BF)
    mask_ref[...] = jnp.transpose(nn(pick, on)).astype(BF)


def experts(h_ref, in_ref, c_ref, mask_ref, wd_ref, wu_ref, out_ref, own_ref, key_ref):
    _, live = place(c_ref[...].astype(F32))
    live = hot(live)

    def columns(h):
        x = [in_ref[p * NH + h] for p in range(NP)]
        x = jnp.concatenate(x, axis=0)
        return jnp.concatenate([x[:, 0:DQ], x[:, DQ : 2 * DQ]], axis=0) * live

    x = jnp.concatenate([columns(h) for h in range(NH)], axis=1)
    mid = jnp.where(mask_ref[...].astype(F32) > 0.5, nt(wd_ref[...], x), 0.0).astype(BF)
    out_ref[...] = nn(wu_ref[...], mid).astype(BF).reshape(NH, DQ, 2 * BLOCK)
    h = h_ref[0]
    own_ref[...] = nt(eye(DQ), columns(h)).astype(BF)
    total = in_ref[h, 0:8, 384:512].astype(F32)
    for p in range(1, NP):
        total = total + in_ref[p * NH + h, 0:8, 384:512].astype(F32)
    key_ref[...] = total[0:4]


def add_up(parts_ref, own_ref, out_ref):
    total = parts_ref[0].astype(F32)
    for h in range(1, NH):
        total = total + parts_ref[h].astype(F32)
    gh = (own_ref[...].astype(F32) + total.astype(BF).astype(F32)).astype(BF)
    rows = nt(eye(2 * BLOCK), gh)
    rows = jnp.concatenate([rows[0:BLOCK], rows[BLOCK:]], axis=1).astype(BF)
    rows = jnp.broadcast_to(rows.reshape(NP, 1, 16, 384), (NP, NH, 16, 384))
    out_ref[...] = rows.reshape(NP * NH, 16, 384)


def query_part(in_ref, q_ref, sq_ref, wo_ref, out_ref, first_ref, second_ref):
    def columns(h):
        return jnp.concatenate([in_ref[p * NH + h, :, 0:DQ] for p in range(NP)], axis=0)

    def seconds(h):
        total = in_ref[h, :, DQ : 2 * DQ].astype(F32)
        for p in range(1, NP):
            total = total + in_ref[p * NH + h, :, DQ : 2 * DQ].astype(F32)
        return total

    first = jnp.concatenate([columns(h) for h in range(NH)], axis=1)
    second = jnp.concatenate([seconds(h) for h in range(NH)], axis=1).astype(BF)
    first_ref[...] = first
    second_ref[...] = second
    wo = wo_ref[...]
    state = tn(nt(first, wo).astype(BF), q_ref[...]) + tn(nt(second, wo).astype(BF), sq_ref[...])
    a, b = halves(state)
    out_ref[:, :, 0:HD] = a.astype(BF)
    out_ref[:, :, HD:] = b.astype(BF)


def regroup(in_ref, first_ref, second_ref, key_ref, out_ref):
    total = in_ref[0].astype(F32)
    for p in range(1, NP):
        total = total + in_ref[p].astype(F32)
    out_ref[:, :, 0:512] = jnp.broadcast_to(total.astype(BF)[None], (NZ, 16, 512))
    x = first_ref[...]
    o = iota((2 * BLOCK, BLOCK), 0)
    i = iota((2 * BLOCK, BLOCK), 1)
    here = ((o & 7) == (i >> 4)) & ((o >> 4) == (i & 15))
    lower, higher = hot(here & ((o & 8) == 0)), hot(here & ((o & 8) != 0))
    rows = nn(lower, x[:, 0:384]) + nn(higher, x[:, 384:768])
    out_ref[:, :, 512:896] = rows.astype(BF).reshape(NZ, 16, 384)
    second = second_ref[...]
    o = iota((2 * BLOCK, NZ), 0)
    i = iota((2 * BLOCK, NZ), 1)
    rows = jnp.zeros((2 * BLOCK, BLOCK), F32)
    for n in range(6):
        pick = hot(((o >> 4) == i) & ((o & 15) == n))
        rows = rows + nn(pick, second[:, n * BLOCK : (n + 1) * BLOCK])
    nothing = jnp.zeros((8, BLOCK), F32)
    key = jnp.concatenate([nothing, key_ref[...], nothing[0:4]], axis=0)
    rows = rows.reshape(NZ, 16, BLOCK) + key[None]
    out_ref[:, :, 896:1024] = rows.astype(BF)


def reduce_states(in_ref, out_ref):
    total = in_ref[0, :, 0:512].astype(F32)
    for z in range(1, NZ):
        total = total + in_ref[z, :, 0:512].astype(F32)
    key = []
    for z in range(NZ):
        piece = in_ref[z, 8:16, 896:1024].astype(F32)
        key.append(jnp.concatenate([piece[n : n + 1] for n in range(4)], axis=1))
    key = jnp.concatenate(key, axis=0)
    out_ref[:, :, 0:512] = jnp.broadcast_to(total.astype(BF)[None], (NP, 16, 512))
    out_ref[:, :, 512:1024] = jnp.broadcast_to(key.astype(BF)[None], (NP, 16, 512))


def unpack(in_ref, e_ref, wo_ref, gh_ref, hg_ref):
    e = e_ref[...]
    match, again = repeats(e)
    rank = jnp.sum(again, axis=0, keepdims=True)
    row = iota((2 * BLOCK, BLOCK), 0)
    first = ((row & 7) == (e & 7)) & ((row >> 4) == (e >> 3)) & (rank < 0.5)
    rows = in_ref[:, :, 512:896].reshape(2 * BLOCK, 384)
    second = in_ref[0, 0:8, 896:1024].astype(F32)
    for z in range(1, NZ):
        second = second + in_ref[z, 0:8, 896:1024].astype(F32)
    second = jnp.concatenate([second[n : n + 1] for n in range(6)], axis=1)
    second = jnp.broadcast_to(second, (16, D)).astype(BF)
    one = iota((16, BLOCK), 0) == 0
    gh = jnp.concatenate(
        [
            tn(hot(first & ((row & 8) == 0)), rows),
            tn(hot(first & ((row & 8) != 0)), rows),
        ],
        axis=1,
    )
    gh = (gh + tn(hot(one & (rank > 0.5)), second)).astype(BF)
    gh_ref[...] = gh
    hg_ref[...] = nt(gh, wo_ref[...]).astype(BF)


def finish(in_ref, hg_ref, k_ref, v_ref, gq_ref, gk_ref, gv_ref):
    scaling = 1.0 / math.sqrt(HD * BLOCK * BLOCK)

    a = in_ref[:, :, 0:HD].reshape(NP, 1, 16, HD)
    b = in_ref[:, :, HD : 2 * HD].reshape(NP, 1, 16, HD)
    qt = jnp.concatenate([a, b], axis=1).reshape(HD, HD)
    x = in_ref[:, :, 512:1024].reshape(BLOCK, 512)
    o = iota((HD, BLOCK), 0)
    i = iota((HD, BLOCK), 1)
    same = ((i >> 4) == (o & 7)) & ((i & 15) == (o >> 4))
    kr = nn(hot(same & ((o & 8) == 0)), x[:, 0:HD]) + nn(hot(same & ((o & 8) != 0)), x[:, HD:])
    kr = kr.astype(BF)
    gq_ref[...] = (scaling * nt(hg_ref[...], kr)).astype(BF)
    gk_ref[...] = (scaling * nn(v_ref[...], qt)).astype(BF)
    gv_ref[...] = (scaling * nt(k_ref[...], qt)).astype(BF)


def swap(tiles, axis):
    return lax.all_to_all(tiles, axis, split_axis=0, concat_axis=0, tiled=True)


def shards(out_grad, expert_of, counts, w_up, w_down, pre_act, queries, keys, values, w_out):
    e = expert_of.reshape(1, BLOCK)
    c = counts.reshape(1, BLOCK)
    h = lax.axis_index("y").reshape(1)
    sent = call(pack, sds(NZ, 16, 512), e, out_grad.T, queries, keys, values, far=range(5))
    msgs, q, sq = call(
        forward, [sds(32, 16, 512), sds(BLOCK, HD), sds(NZ, HD)], swap(sent, "z")
    )
    mask = call(masks, sds(D, 2 * BLOCK), c, pre_act, far=(0, 1))
    parts, own, key = call(
        experts,
        [sds(NH, DQ, 2 * BLOCK), sds(DQ, 2 * BLOCK), sds(4, BLOCK, dtype=F32)],
        h,
        swap(msgs, PLANE + ("y",)),
        c,
        mask,
        w_down[0],
        w_up[0],
        scalars=1,
    )
    msgs = call(add_up, sds(32, 16, 384), swap(parts, "y"), own)
    msgs, first, second = call(
        query_part,
        [sds(NP, 16, 512), sds(BLOCK, D), sds(NZ, D)],
        swap(msgs, PLANE + ("y",)),
        q,
        sq,
        w_out,
    )
    back = call(regroup, sds(NZ, 16, 1024), swap(msgs, PLANE), first, second, key)
    back = swap(back, "z")
    states = swap(call(reduce_states, sds(NP, 16, 1024), back), PLANE)
    gh, hg = call(unpack, [sds(BLOCK, D), sds(BLOCK, HD)], back, e, w_out, home=1)
    outs = [sds(BLOCK, HD)] * 3
    return (gh, *call(finish, outs, states, hg, keys, values, home=3))


def solution(mesh):
    finer = Mesh(mesh.devices.reshape(16, 4, 2, mesh.shape["head"]), ("z", "x", "c", "y"))
    return jax.shard_map(
        shards,
        mesh=finer,
        in_specs=(
            P(SEQ, "y"),
            P(SEQ),
            P(None, SEQ),
            P(SEQ, None, "y"),
            P(SEQ, "y", None),
            P(SEQ, "y"),
            P(SEQ, "y"),
            P(SEQ, "y"),
            P(SEQ, "y"),
            P("y", None),
        ),
        out_specs=(P(SEQ, None), P(SEQ, "y"), P(SEQ, "y"), P(SEQ, "y")),
        check_vma=False,
    )
```

time: 144 us -> 141 us (0.979)
  blocking collectives: 108 us -> 91.4 us
  starting transfers between devices: 14.4 us -> 22.9 us
  waiting for transfers between devices: 10.1 us -> 14.9 us
    all_to_all x6 -> x5, blocking collectives: 108 us -> 91.4 us  [swap(): return lax.all_to_all(tiles, axis, split_axis=0, concat_axis=0, tiled=True)]
    all_to_all x2, starting transfers between devices: 14.4 us -> 22.9 us  [swap(): return lax.all_to_all(tiles, axis, split_axis=0, concat_axis=0, tiled=True)]
    all_to_all x2, waiting for transfers between devices: 10.1 us -> 14.9 us  [swap(): return lax.all_to_all(tiles, axis, split_axis=0, concat_axis=0, tiled=True)]
    pallas_call x11 -> x10, Pallas kernels: 9.81 us -> 10.2 us  [call(): pl.pallas_call(kernel, out_shape=[s if n < home else pltpu.VMEM(s.shape,...]
where the time goes in v4:
time: 141 us; the launch traced here: 140 us
  blocking collectives  91.4 us (65%)
  starting transfers between devices  22.9 us (16%)
  waiting for transfers between devices  14.9 us (11%)
  Pallas kernels  10.2 us (7%)
    all_to_all x5, blocking collectives, swap(): return lax.all_to_all(tiles, axis, split_axis=0, concat_axis=0, tiled=True)  91.4 us
    all_to_all x2, starting transfers between devices, swap(): return lax.all_to_all(tiles, axis, split_axis=0, concat_axis=0, tiled=True)  22.9 us
    all_to_all x2, waiting for transfers between devices, swap(): return lax.all_to_all(tiles, axis, split_axis=0, concat_axis=0, tiled=True)  14.9 us
    pallas_call x10, Pallas kernels, call(): pl.pallas_call(kernel, out_shape=[s if n < home else pltpu.VMEM(s.shape,...  10.2 us
  transfers between devices with their start and end apart: 2, of which 2 were waited for; matrix products, arithmetic and copies ran while one was open for 0% of the time, Pallas kernels for 2%

profile of v4, /device:TPU:1, one launch (start us, length us, event | category | flops | bytes accessed | tf_op | source)
XLA Modules:
  0.0 140.2 jit_solution(18141675917974231379)
XLA Ops:
  0.6 1.4 %pack.1 = bf16[16,16,512]{2,1,0:T(8,128)(2,1)S(1)} custom-call(s32[1,128]{1,0:T(1,128)} %bitcast.8, bf16[192,128]{1,0:T(8,128)(2,1)} %bitcast.12, bf16[128,256]{1,0:T(8,128)(2,1)} %q_ref.1, bf16[128,256]{1,0:T(8,128)(2,1)} %k_ref.3, bf16[128,256]{1,0:T(8,128)(2,1)} %v_ref.3), custom_call_target="tpu_custom_call" | custom-call | flops 100000000 | bytes 246272 | tf_op jit(solution)/shard_map/pack/pallas_call | solution.py:56
  2.1 0.0 copy-start.2
  2.1 29.4 %all_to_all.35.in_ref = bf16[16,16,512]{2,1,0:T(8,128)(2,1)S(1)} all-to-all(bf16[16,16,512]{2,1,0:T(8,128)(2,1)S(1)} %pack.1), channel_id=1, replica_groups=mesh['z'=16,'x'=4,'c'=2,'y'=4] {'z'}, dimensions={0} | all-to-all | bytes 524288 | tf_op jit(solution)/shard_map/all_to_all | solution.py:280
  31.5 1.2 forward.1
  32.7 12.7 %all-to-all-start.1 = ((bf16[32,16,512]{2,1,0:T(8,128)(2,1)}), bf16[32,16,512]{2,1,0:T(8,128)(2,1)S(1)}, u32[]{:S(2)}, u32[]{:S(2)}) async-start(bf16[32,16,512]{2,1,0:T(8,128)(2,1)} %get-tuple-element.18), calls=%async_computation.1 | async-start | bytes 1048576 | tf_op jit(solution)/shard_map/all_to_all | solution.py:280
  45.4 1.5 %masks.1.mask_ref = bf16[768,256]{1,0:T(8,128)(2,1)S(1)} custom-call(s32[1,128]{1,0:T(1,128)} %bitcast.10, bf16[256,768]{1,0:T(8,128)(2,1)} %pre_ref.1), custom_call_target="tpu_custom_call" | custom-call | flops 100000000 | bytes 393728 | tf_op jit(solution)/shard_map/masks/pallas_call | solution.py:56
  46.9 9.6 %all-to-all-done.1.in_ref = bf16[32,16,512]{2,1,0:T(8,128)(2,1)S(1)} async-done(((bf16[32,16,512]{2,1,0:T(8,128)(2,1)}), bf16[32,16,512]{2,1,0:T(8,128)(2,1)S(1)}, u32[]{:S(2)}, u32[]{:S(2)}) %all-to-all-start.1) | async-done | bytes 524320 | tf_op jit(solution)/shard_map/all_to_all | solution.py:280
  56.5 0.0 copy-done.1
  56.5 1.7 %experts.1 = (bf16[4,192,256]{2,1,0:T(8,128)(2,1)S(1)}, bf16[192,256]{1,0:T(8,128)(2,1)S(1)}, f32[4,128]{1,0:T(4,128)S(1)}) custom-call(s32[1]{0:T(128)} %bitcast.h_ref, bf16[32,16,512]{2,1,0:T(8,128)(2,1)S(1)} %all-to-all-done.1.in_ref, s32[1,128]{1,0:T(1,128)S(1)} %bitcast.11, bf16[768,256]{1,0:T(8,128)(2,1)S(1)} %masks.1.mask_ref, ...), custom_call_target="tpu_custom_call" | custom-call | flops 100000000 | bytes 3277316 | tf_op jit(solution)/shard_map/experts/pallas_call | solution.py:56
  58.2 0.0 copy-start
  58.2 9.7 %all_to_all.36.parts_ref = bf16[4,192,256]{2,1,0:T(8,128)(2,1)S(1)} all-to-all(bf16[4,192,256]{2,1,0:T(8,128)(2,1)S(1)} %get-tuple-element.19), channel_id=1, replica_groups=mesh['z'=16,'x'=4,'c'=2,'y'=4] {'y'}, dimensions={0} | all-to-all | bytes 786432 | tf_op jit(solution)/shard_map/all_to_all | solution.py:280
  68.0 0.3 add_up.1
  68.3 15.6 %all_to_all.37.in_ref = bf16[32,16,384]{2,1,0:T(8,128)(2,1)S(1)} all-to-all(bf16[32,16,384]{2,1,0:T(8,128)(2,1)S(1)} %add_up.1), channel_id=1, replica_groups=mesh['z'=16,'x'=4,'c'=2,'y'=4] {'x','c','y'}, dimensions={0} | all-to-all | bytes 786432 | tf_op jit(solution)/shard_map/all_to_all | solution.py:280
  83.8 0.7 query_part.1
  84.5 8.3 %all_to_all.38.in_ref = bf16[8,16,512]{2,1,0:T(8,128)(2,1)S(1)} all-to-all(bf16[8,16,512]{2,1,0:T(8,128)(2,1)S(1)} %get-tuple-element.23), channel_id=1, replica_groups=mesh['z'=16,'x'=4,'c'=2,'y'=4] {'x','c'}, dimensions={0} | all-to-all | bytes 262144 | tf_op jit(solution)/shard_map/all_to_all | solution.py:280
  92.8 0.4 regroup.1
  93.2 0.0 copy-start.5
  93.2 28.4 %all_to_all.39.in_ref = bf16[16,16,1024]{2,1,0:T(8,128)(2,1)S(1)} all-to-all(bf16[16,16,1024]{2,1,0:T(8,128)(2,1)S(1)} %regroup.1), channel_id=1, replica_groups=mesh['z'=16,'x'=4,'c'=2,'y'=4] {'z'}, dimensions={0} | all-to-all | bytes 1048576 | tf_op jit(solution)/shard_map/all_to_all | solution.py:280
  121.6 0.8 reduce_states.1
  122.4 10.3 %all-to-all-start.6 = ((bf16[8,16,1024]{2,1,0:T(8,128)(2,1)}), bf16[8,16,1024]{2,1,0:T(8,128)(2,1)S(1)}, u32[]{:S(2)}, u32[]{:S(2)}) async-start(bf16[8,16,1024]{2,1,0:T(8,128)(2,1)} %reduce_states.1), calls=%async_computation.6 | async-start | bytes 524288 | tf_op jit(solution)/shard_map/all_to_all | solution.py:280
  132.6 1.2 unpack.1
  133.8 5.3 %all-to-all-done.6.in_ref = bf16[8,16,1024]{2,1,0:T(8,128)(2,1)S(1)} async-done(((bf16[8,16,1024]{2,1,0:T(8,128)(2,1)}), bf16[8,16,1024]{2,1,0:T(8,128)(2,1)S(1)}, u32[]{:S(2)}, u32[]{:S(2)}) %all-to-all-start.6) | async-done | bytes 262176 | tf_op jit(solution)/shard_map/all_to_all | solution.py:280
  139.1 0.0 copy-done.3
  139.1 1.1 finish.1
  (9 shorter events, 0.0 us)
Async XLA Ops:
  2.1 54.4 %copy-start.2 = (bf16[1,768,768]{2,1,0:T(8,128)(2,1)S(1)}, bf16[1,768,768]{2,1,0:T(8,128)(2,1)}, u32[]{:S(2)}) copy-start(bf16[1,768,768]{2,1,0:T(8,128)(2,1)} %param.13) | copy-start | bytes 3538948
  31.5 25.0 %copy-start.1 = (bf16[1,768,768]{2,1,0:T(8,128)(2,1)S(1)}, bf16[1,768,768]{2,1,0:T(8,128)(2,1)}, u32[]{:S(2)}) copy-start(bf16[1,768,768]{2,1,0:T(8,128)(2,1)} %param.14) | copy-start | bytes 3538948
  31.5 25.0 %copy-start.6 = (s32[128,1]{0,1:T(1,128)S(1)}, s32[128,1]{0,1:T(1,128)}, u32[]{:S(2)}) copy-start(s32[128,1]{0,1:T(1,128)} %param.12) | copy-start | bytes 1540
  32.7 23.8 %all-to-all-start.1 = ((bf16[32,16,512]{2,1,0:T(8,128)(2,1)}), bf16[32,16,512]{2,1,0:T(8,128)(2,1)S(1)}, u32[]{:S(2)}, u32[]{:S(2)}) async-start(bf16[32,16,512]{2,1,0:T(8,128)(2,1)} %get-tuple-element.18), calls=%async_computation.1 | async-start | bytes 1048576 | tf_op jit(solution)/shard_map/all_to_all | solution.py:280
  58.2 25.6 %copy-start = (bf16[256,768]{1,0:T(8,128)(2,1)S(1)}, bf16[256,768]{1,0:T(8,128)(2,1)}, u32[]{:S(2)}) copy-start(bf16[256,768]{1,0:T(8,128)(2,1)} %wo_ref.3) | copy-start | bytes 1179652
  93.2 39.4 %copy-start.5 = (s32[128]{0:T(128)S(1)}, s32[128]{0:T(128)}, u32[]{:S(2)}) copy-start(s32[128]{0:T(128)} %param.11) | copy-start | bytes 1540
  121.6 17.5 %copy-start.3 = (bf16[128,256]{1,0:T(8,128)(2,1)S(1)}, bf16[128,256]{1,0:T(8,128)(2,1)}, u32[]{:S(2)}) copy-start(bf16[128,256]{1,0:T(8,128)(2,1)} %k_ref.3) | copy-start | bytes 196612
  121.6 17.5 %copy-start.4 = (bf16[128,256]{1,0:T(8,128)(2,1)S(1)}, bf16[128,256]{1,0:T(8,128)(2,1)}, u32[]{:S(2)}) copy-start(bf16[128,256]{1,0:T(8,128)(2,1)} %v_ref.3) | copy-start | bytes 196612
  122.4 16.8 %all-to-all-start.6 = ((bf16[8,16,1024]{2,1,0:T(8,128)(2,1)}), bf16[8,16,1024]{2,1,0:T(8,128)(2,1)S(1)}, u32[]{:S(2)}, u32[]{:S(2)}) async-start(bf16[8,16,1024]{2,1,0:T(8,128)(2,1)} %reduce_states.1), calls=%async_computation.6 | async-start | bytes 524288 | tf_op jit(solution)/shard_map/all_to_all | solution.py:280

commit v5 on v4

v5 whole, which is shorter than its diff:
```python
import math

import jax
import jax.numpy as jnp
from jax import lax
from jax.experimental import pallas as pl
from jax.experimental.pallas import tpu as pltpu
from jax.sharding import Mesh
from jax.sharding import PartitionSpec as P

Z = ("zh", "zl")
PLANE = ("x", "c")
SEQ = Z + PLANE
BF, F32 = jnp.bfloat16, jnp.float32
NZ, NP, NH = 16, 8, 4
BLOCK = 128
D, HD, DQ = 768, 256, 192
LIMIT = 16 * 2**20
FLOPS = 10**10
VMEM = pl.BlockSpec(memory_space=pltpu.VMEM)
SMEM = pl.BlockSpec(memory_space=pltpu.SMEM)


def nn(a, b):
    return lax.dot_general(a, b, (((1,), (0,)), ((), ())), preferred_element_type=F32)


def nt(a, b):
    return lax.dot_general(a, b, (((1,), (1,)), ((), ())), preferred_element_type=F32)


def tn(a, b):
    return lax.dot_general(a, b, (((0,), (0,)), ((), ())), preferred_element_type=F32)


def hot(cond):
    return jnp.where(cond, 1.0, 0.0).astype(BF)


def iota(shape, dim):
    return lax.broadcasted_iota(jnp.int32, shape, dim)


def call(kernel, outs, *args, far=(), home=0, scalars=0):
    single = not isinstance(outs, (list, tuple))
    shapes = [outs] if single else list(outs)
    nbytes = sum(a.size * a.dtype.itemsize for a in args)

    def near(n, a):
        space = pltpu.HBM if n in far else pltpu.VMEM
        return a if n < scalars else pltpu.with_memory_space_constraint(a, space)

    res = pl.pallas_call(
        kernel,
        out_shape=[s if n < home else pltpu.VMEM(s.shape, s.dtype) for n, s in enumerate(shapes)],
        in_specs=[SMEM] * scalars + [VMEM] * (len(args) - scalars),
        out_specs=[VMEM] * len(shapes),
        cost_estimate=pl.CostEstimate(flops=FLOPS, bytes_accessed=nbytes, transcendentals=0),
        compiler_params=pltpu.CompilerParams(vmem_limit_bytes=LIMIT),
        name=kernel.__name__,
    )(*[near(n, a) for n, a in enumerate(args)])
    return res[0] if single else res


def sds(*shape, dtype=BF):
    return jax.ShapeDtypeStruct(shape, dtype)


def eye(n):
    return hot(iota((n, n), 0) == iota((n, n), 1))


def repeats(e):
    match = e == iota((BLOCK, BLOCK), 0)
    earlier = hot(iota((BLOCK, BLOCK), 0) < iota((BLOCK, BLOCK), 1))
    return match, jnp.where(match & (nn(hot(match), earlier) > 0.5), 1.0, 0.0)


def pack(_, e_ref, ogt_ref, q_ref, out_ref):
    match, again = repeats(e_ref[...])
    first = (jnp.where(match, 1.0, 0.0) - again).astype(BF)
    second = jnp.broadcast_to(jnp.sum(again, axis=0, keepdims=True), (16, BLOCK)).astype(BF)
    ogt, q = ogt_ref[...], q_ref[...]
    token = jnp.concatenate([nt(second, ogt), nn(second, q)], axis=1)
    spare = jnp.concatenate(
        [token[0:1, i * 64 : (i + 1) * 64] for i in range(7)] + [jnp.zeros((1, 64), F32)], axis=0
    )
    spare = jnp.broadcast_to(spare[None], (NZ, 8, 64)).reshape(BLOCK, 64)
    rows = jnp.concatenate([nt(first, ogt), spare], axis=1)
    out = [rows.reshape(NZ, 8, HD), nn(first, q).reshape(NZ, 8, HD)]
    out_ref[...] = jnp.concatenate(out, axis=1).astype(BF)


def forward(in_ref, out_ref, q_ref, sq_ref):
    x = in_ref[...].reshape(2 * BLOCK, HD)
    o = iota((BLOCK, 2 * BLOCK), 0)
    i = iota((BLOCK, 2 * BLOCK), 1)
    here = (i >> 4) == (o & 15)
    firsts = nn(hot(here & ((i & 15) == (o >> 4))), x[:, 0:DQ])
    q_ref[...] = nn(hot(here & ((i & 15) == (o >> 4) + 8)), x).astype(BF)
    o = iota((NZ, 2 * BLOCK), 0)
    i = iota((NZ, 2 * BLOCK), 1)
    here = (i >> 4) == o
    spare = x[:, DQ:HD]
    seconds = jnp.concatenate([nn(hot(here & ((i & 15) == n)), spare) for n in range(7)], axis=1)
    sq_ref[...] = seconds[:, DQ:448].astype(BF)
    seconds = jnp.broadcast_to(seconds[None, :, 0:DQ], (NP, NZ, DQ)).reshape(BLOCK, DQ)
    rows = jnp.concatenate([firsts, seconds], axis=1).astype(BF)
    rows = jnp.broadcast_to(rows.reshape(NP, 1, 16, 384), (NP, NH, 16, 384))
    out_ref[...] = rows.reshape(NP * NH, 16, 384)


def place(c):
    shape = (BLOCK, 2 * BLOCK)
    s, o = iota(shape, 0), iota(shape, 1)
    block = (o & 15) * NP + ((o >> 4) & 7)
    c = jnp.broadcast_to(c, (16, BLOCK)).astype(BF)
    before, count = nn(c, hot(s < block))[0:1], nn(c, hot(s == block))[0:1]
    r = (iota((1, 2 * BLOCK), 1) >> 7).astype(F32)
    return before + r, count > r + 0.5


def experts(h_ref, in_ref, c_ref, pre_ref, wd_ref, wu_ref, out_ref, own_ref):
    def columns(h):
        x = jnp.concatenate([in_ref[p * NH + h] for p in range(NP)], axis=0)
        return jnp.concatenate([x[:, 0:DQ], x[:, DQ : 2 * DQ]], axis=0)

    row, live = place(c_ref[...].astype(F32))
    pick = hot((iota((2 * BLOCK, 2 * BLOCK), 0).astype(F32) == row) & live)
    on = hot(pre_ref[...].astype(F32) > 0)
    mask = tn(on, pick)
    x = jnp.concatenate([columns(h) for h in range(NH)], axis=1)
    mid = jnp.where(mask > 0.5, nt(wd_ref[...], x), 0.0).astype(BF)
    out_ref[...] = nn(wu_ref[...], mid).astype(BF).reshape(NH, DQ, 2 * BLOCK)
    own = nt(eye(DQ), columns(h_ref[0]))
    own_ref[...] = jnp.where(live, own, 0.0).astype(BF)


def add_up(parts_ref, own_ref, out_ref):
    total = parts_ref[0].astype(F32)
    for h in range(1, NH):
        total = total + parts_ref[h].astype(F32)
    gh = (own_ref[...].astype(F32) + total.astype(BF).astype(F32)).astype(BF)
    rows = nt(eye(2 * BLOCK), gh)
    rows = jnp.concatenate([rows[0:BLOCK], rows[BLOCK:]], axis=1).astype(BF)
    rows = jnp.broadcast_to(rows.reshape(NP, 1, 16, 384), (NP, NH, 16, 384))
    out_ref[...] = rows.reshape(NP * NH, 16, 384)


def state_parts(in_ref, q_ref, sq_ref, wo_ref, k_ref, v_ref, out_ref, first_ref, second_ref):
    def columns(h):
        return jnp.concatenate([in_ref[p * NH + h, :, 0:DQ] for p in range(NP)], axis=0)

    def seconds(h):
        total = in_ref[h, :, DQ : 2 * DQ].astype(F32)
        for p in range(1, NP):
            total = total + in_ref[p * NH + h, :, DQ : 2 * DQ].astype(F32)
        return total

    first = jnp.concatenate([columns(h) for h in range(NH)], axis=1)
    second = jnp.concatenate([seconds(h) for h in range(NH)], axis=1).astype(BF)
    first_ref[...] = first
    second_ref[...] = second
    wo = wo_ref[...]
    query = tn(nt(first, wo).astype(BF), q_ref[...]) + tn(nt(second, wo).astype(BF), sq_ref[...])
    out_ref[:, :, 0:HD] = query.astype(BF).reshape(16, 16, HD)
    out_ref[:, :, HD:] = tn(k_ref[...], v_ref[...]).astype(BF).reshape(16, 16, HD)


def regroup(in_ref, first_ref, second_ref, out_ref):
    total = in_ref[0].astype(F32)
    for p in range(1, 2 * NP):
        total = total + in_ref[p].astype(F32)
    out_ref[:, :, 0:512] = jnp.broadcast_to(total.astype(BF)[None], (NZ, 16, 512))
    x = first_ref[...]
    o = iota((2 * BLOCK, BLOCK), 0)
    i = iota((2 * BLOCK, BLOCK), 1)
    here = ((o & 7) == (i >> 4)) & ((o >> 4) == (i & 15))
    lower, higher = hot(here & ((o & 8) == 0)), hot(here & ((o & 8) != 0))
    rows = nn(lower, x[:, 0:384]) + nn(higher, x[:, 384:768])
    out_ref[:, :, 512:896] = rows.astype(BF).reshape(NZ, 16, 384)
    second = second_ref[...]
    o = iota((2 * BLOCK, NZ), 0)
    i = iota((2 * BLOCK, NZ), 1)
    rows = jnp.zeros((2 * BLOCK, BLOCK), F32)
    for n in range(6):
        pick = hot(((o >> 4) == i) & ((o & 15) == n))
        rows = rows + nn(pick, second[:, n * BLOCK : (n + 1) * BLOCK])
    out_ref[:, :, 896:1024] = rows.astype(BF).reshape(NZ, 16, BLOCK)


def reduce_states(in_ref, out_ref):
    for zl in range(2):
        total = in_ref[zl, :, 0:512].astype(F32)
        for z in range(2 + zl, NZ, 2):
            total = total + in_ref[z, :, 0:512].astype(F32)
        total = jnp.broadcast_to(total.astype(BF)[None], (NP, 16, 512))
        out_ref[:, :, zl * HD : (zl + 1) * HD] = total[:, :, 0:HD]
        out_ref[:, :, 512 + zl * HD : 512 + (zl + 1) * HD] = total[:, :, HD:]


def finish(in_ref, back_ref, e_ref, wo_ref, k_ref, v_ref, gh_ref, gq_ref, gk_ref, gv_ref):
    scaling = 1.0 / math.sqrt(HD * BLOCK * BLOCK)

    def whole(at):
        a = in_ref[:, :, at : at + HD].reshape(NP, 1, 16, HD)
        b = in_ref[:, :, at + HD : at + 2 * HD].reshape(NP, 1, 16, HD)
        return jnp.concatenate([a, b], axis=1).reshape(HD, HD)

    qt, kr = whole(0), whole(512)
    e = e_ref[...]
    match, again = repeats(e)
    rank = jnp.sum(again, axis=0, keepdims=True)
    row = iota((2 * BLOCK, BLOCK), 0)
    first = ((row & 7) == (e & 7)) & ((row >> 4) == (e >> 3)) & (rank < 0.5)
    lower, higher = hot(first & ((row & 8) == 0)), hot(first & ((row & 8) != 0))
    rows = back_ref[:, :, 512:896].reshape(2 * BLOCK, 384)
    second = back_ref[0, 0:8, 896:1024].astype(F32)
    for z in range(1, NZ):
        second = second + back_ref[z, 0:8, 896:1024].astype(F32)
    second = jnp.concatenate([second[n : n + 1] for n in range(6)], axis=1)
    second = jnp.broadcast_to(second, (16, D)).astype(BF)
    one = iota((16, BLOCK), 0) == 0
    gh = jnp.concatenate([tn(lower, rows), tn(higher, rows)], axis=1)
    gh = (gh + tn(hot(one & (rank > 0.5)), second)).astype(BF)
    gh_ref[...] = gh
    hg = nt(gh, wo_ref[...]).astype(BF)
    gq_ref[...] = (scaling * nt(hg, kr)).astype(BF)
    gk_ref[...] = (scaling * nn(v_ref[...], qt)).astype(BF)
    gv_ref[...] = (scaling * nt(k_ref[...], qt)).astype(BF)


def swap(tiles, axis):
    return lax.all_to_all(tiles, axis, split_axis=0, concat_axis=0, tiled=True)


def shards(out_grad, expert_of, counts, w_up, w_down, pre_act, queries, keys, values, w_out):
    e = expert_of.reshape(1, BLOCK)
    c = counts.reshape(1, BLOCK)
    h = lax.axis_index("y").reshape(1)
    sent = call(pack, sds(NZ, 16, HD), h, e, out_grad.T, queries, far=range(1, 4), scalars=1)
    outs = [sds(32, 16, 384), sds(BLOCK, HD), sds(NZ, HD)]
    msgs, q, sq = call(forward, outs, swap(sent, Z))
    msgs = swap(msgs, PLANE + ("y",))
    outs = [sds(NH, DQ, 2 * BLOCK), sds(DQ, 2 * BLOCK)]
    parts, own = call(experts, outs, h, msgs, c, pre_act, w_down[0], w_up[0], scalars=1)
    msgs = swap(call(add_up, sds(32, 16, 384), swap(parts, "y"), own), PLANE + ("y",))
    outs = [sds(16, 16, 512), sds(BLOCK, D), sds(NZ, D)]
    msgs, first, second = call(state_parts, outs, msgs, q, sq, w_out, keys, values)
    msgs = swap(msgs, PLANE + ("zl",))
    back = swap(call(regroup, sds(NZ, 16, 1024), msgs, first, second), Z)
    states = swap(call(reduce_states, sds(NP, 16, 1024), back), PLANE)
    outs = [sds(BLOCK, D)] + [sds(BLOCK, HD)] * 3
    return tuple(call(finish, outs, states, back, e, w_out, keys, values, home=4))


def solution(mesh):
    finer = Mesh(mesh.devices.reshape(8, 2, 4, 2, mesh.shape["head"]), ("zh", "zl", "x", "c", "y"))
    return jax.shard_map(
        shards,
        mesh=finer,
        in_specs=(
            P(SEQ, "y"),
            P(SEQ),
            P(None, SEQ),
            P(SEQ, None, "y"),
            P(SEQ, "y", None),
            P(SEQ, "y"),
            P(SEQ, "y"),
            P(SEQ, "y"),
            P(SEQ, "y"),
            P("y", None),
        ),
        out_specs=(P(SEQ, None), P(SEQ, "y"), P(SEQ, "y"), P(SEQ, "y")),
        check_vma=False,
    )
```

time: 141 us -> 134 us (0.950)
  blocking collectives: 91.4 us -> 126 us
  starting transfers between devices: 22.9 us -> 0 us
  waiting for transfers between devices: 14.9 us -> 0 us
  Pallas kernels: 10.2 us -> 6.33 us
    all_to_all x5 -> x7, blocking collectives: 91.4 us -> 126 us  [swap(): return lax.all_to_all(tiles, axis, split_axis=0, concat_axis=0, tiled=True)]
    all_to_all x2 -> x0, starting transfers between devices: 22.9 us -> none  [swap(): return lax.all_to_all(tiles, axis, split_axis=0, concat_axis=0, tiled=True)]
    all_to_all x2 -> x0, waiting for transfers between devices: 14.9 us -> none  [swap(): return lax.all_to_all(tiles, axis, split_axis=0, concat_axis=0, tiled=True)]
    pallas_call x10 -> x8, Pallas kernels: 10.2 us -> 6.33 us  [call(): pl.pallas_call(kernel, out_shape=[s if n < home else pltpu.VMEM(s.shape,...]
  transfers between devices with their start and end apart: 2 -> 0, of which waited for: 2 -> 0; matrix products, arithmetic and copies ran while one was open for 0% -> 0% of each run, Pallas kernels for 2% -> 0%
where the time goes in v5:
time: 134 us
  blocking collectives  126 us (94%)
  Pallas kernels  6.33 us (5%)
    all_to_all x7, blocking collectives, swap(): return lax.all_to_all(tiles, axis, split_axis=0, concat_axis=0, tiled=True)  126 us
    pallas_call x8, Pallas kernels, call(): pl.pallas_call(kernel, out_shape=[s if n < home else pltpu.VMEM(s.shape,...  6.33 us

profile of v5, /device:TPU:1, one launch (start us, length us, event | category | flops | bytes accessed | tf_op | source)
XLA Modules:
  0.0 133.6 jit_solution(16527583937477384726)
XLA Ops:
  0.6 1.4 %pack.1 = bf16[16,16,256]{2,1,0:T(8,128)(2,1)S(1)} custom-call(s32[1]{0:T(128)} %bitcast._.h_ref, s32[1,128]{1,0:T(1,128)} %bitcast.9, bf16[192,128]{1,0:T(8,128)(2,1)} %bitcast.11, bf16[128,256]{1,0:T(8,128)(2,1)} %q_ref.1), custom_call_target="tpu_custom_call" | custom-call | flops 10000000000 | bytes 115204 | tf_op jit(solution)/shard_map/pack/pallas_call | solution.py:53
  2.0 27.5 %all_to_all.35.in_ref = bf16[16,16,256]{2,1,0:T(8,128)(2,1)S(1)} all-to-all(bf16[16,16,256]{2,1,0:T(8,128)(2,1)S(1)} %pack.1), channel_id=1, replica_groups=mesh['zh'=8,'zl'=2,'x'=4,'c'=2,'y'=4] {'zh','zl'}, dimensions={0} | all-to-all | bytes 262144 | tf_op jit(solution)/shard_map/all_to_all | solution.py:234
  29.5 0.0 copy-start
  29.5 0.0 copy-start.1
  29.5 0.4 forward.1
  29.9 20.9 %all_to_all.36.in_ref = bf16[32,16,384]{2,1,0:T(8,128)(2,1)S(1)} all-to-all(bf16[32,16,384]{2,1,0:T(8,128)(2,1)S(1)} %get-tuple-element.12), channel_id=1, replica_groups=mesh['zh'=8,'zl'=2,'x'=4,'c'=2,'y'=4] {'x','c','y'}, dimensions={0} | all-to-all | bytes 786432 | tf_op jit(solution)/shard_map/all_to_all | solution.py:234
  50.8 0.0 copy-done
  50.8 0.0 copy-done.1
  50.8 0.0 copy-done.2
  50.8 0.0 copy-done.6
  50.8 1.6 %experts.1 = (bf16[4,192,256]{2,1,0:T(8,128)(2,1)S(1)}, bf16[192,256]{1,0:T(8,128)(2,1)S(1)}) custom-call(s32[1]{0:T(128)} %bitcast._.h_ref, bf16[32,16,384]{2,1,0:T(8,128)(2,1)S(1)} %all_to_all.36.in_ref, s32[1,128]{1,0:T(1,128)S(1)} %bitcast.8, bf16[256,768]{1,0:T(8,128)(2,1)S(1)} %copy-done.2, bf16[768,768]{1,0:T(8,128)(2,1)S(1)} %bitcast.6, ...), custom_call_target="tpu_custom_call" | custom-call | flops 10000000000 | bytes 3146244 | tf_op jit(solution)/shard_map/experts/pallas_call | solution.py:53
  52.4 9.6 %all_to_all.37.parts_ref = bf16[4,192,256]{2,1,0:T(8,128)(2,1)S(1)} all-to-all(bf16[4,192,256]{2,1,0:T(8,128)(2,1)S(1)} %get-tuple-element.13), channel_id=1, replica_groups=mesh['zh'=8,'zl'=2,'x'=4,'c'=2,'y'=4] {'y'}, dimensions={0} | all-to-all | bytes 786432 | tf_op jit(solution)/shard_map/all_to_all | solution.py:234
  62.1 0.3 add_up.1
  62.4 15.1 %all_to_all.38.in_ref = bf16[32,16,384]{2,1,0:T(8,128)(2,1)S(1)} all-to-all(bf16[32,16,384]{2,1,0:T(8,128)(2,1)S(1)} %add_up.1), channel_id=1, replica_groups=mesh['zh'=8,'zl'=2,'x'=4,'c'=2,'y'=4] {'x','c','y'}, dimensions={0} | all-to-all | bytes 786432 | tf_op jit(solution)/shard_map/all_to_all | solution.py:234
  77.5 0.0 copy-done.3
  77.5 0.0 copy-done.4
  77.5 0.0 copy-done.5
  77.5 0.7 state_parts.1
  78.2 11.0 %all_to_all.39.in_ref = bf16[16,16,512]{2,1,0:T(8,128)(2,1)S(1)} all-to-all(bf16[16,16,512]{2,1,0:T(8,128)(2,1)S(1)} %get-tuple-element.17), channel_id=1, replica_groups=mesh['zh'=8,'zl'=2,'x'=4,'c'=2,'y'=4] {'x','c','zl'}, dimensions={0} | all-to-all | bytes 524288 | tf_op jit(solution)/shard_map/all_to_all | solution.py:234
  89.2 0.4 regroup.1
  89.6 26.0 %all_to_all.40.in_ref.back_ref = bf16[16,16,1024]{2,1,0:T(8,128)(2,1)S(1)} all-to-all(bf16[16,16,1024]{2,1,0:T(8,128)(2,1)S(1)} %regroup.1), channel_id=1, replica_groups=mesh['zh'=8,'zl'=2,'x'=4,'c'=2,'y'=4] {'zh','zl'}, dimensions={0} | all-to-all | bytes 1048576 | tf_op jit(solution)/shard_map/all_to_all | solution.py:234
  115.7 16.3 %all_to_all.41.in_ref = bf16[8,16,1024]{2,1,0:T(8,128)(2,1)S(1)} all-to-all(bf16[8,16,1024]{2,1,0:T(8,128)(2,1)S(1)} %reduce_states.1), channel_id=1, replica_groups=mesh['zh'=8,'zl'=2,'x'=4,'c'=2,'y'=4] {'x','c'}, dimensions={0} | all-to-all | bytes 524288 | tf_op jit(solution)/shard_map/all_to_all | solution.py:234
  132.0 0.0 copy-done.7
  132.0 1.6 %finish.1 = (bf16[128,768]{1,0:T(8,128)(2,1)}, bf16[128,256]{1,0:T(8,128)(2,1)}, bf16[128,256]{1,0:T(8,128)(2,1)}, bf16[128,256]{1,0:T(8,128)(2,1)}) custom-call(bf16[8,16,1024]{2,1,0:T(8,128)(2,1)S(1)} %all_to_all.41.in_ref, bf16[16,16,1024]{2,1,0:T(8,128)(2,1)S(1)} %all_to_all.40.in_ref.back_ref, s32[1,128]{1,0:T(1,128)S(1)} %bitcast.10, ...), custom_call_target="tpu_custom_call" | custom-call | flops 10000000000 | bytes 1311232 | tf_op jit(solution)/shard_map/finish/pallas_call | solution.py:53
  (7 shorter events, 0.1 us)
Async XLA Ops:
  29.5 21.3 %copy-start = (bf16[1,768,768]{2,1,0:T(8,128)(2,1)S(1)}, bf16[1,768,768]{2,1,0:T(8,128)(2,1)}, u32[]{:S(2)}) copy-start(bf16[1,768,768]{2,1,0:T(8,128)(2,1)} %param.14) | copy-start | bytes 3538948
  29.5 21.3 %copy-start.1 = (bf16[1,768,768]{2,1,0:T(8,128)(2,1)S(1)}, bf16[1,768,768]{2,1,0:T(8,128)(2,1)}, u32[]{:S(2)}) copy-start(bf16[1,768,768]{2,1,0:T(8,128)(2,1)} %param.13) | copy-start | bytes 3538948
  29.5 21.3 %copy-start.2 = (bf16[256,768]{1,0:T(8,128)(2,1)S(1)}, bf16[256,768]{1,0:T(8,128)(2,1)}, u32[]{:S(2)}) copy-start(bf16[256,768]{1,0:T(8,128)(2,1)} %pre_ref.1) | copy-start | bytes 1179652
  29.5 21.3 %copy-start.6 = (s32[128,1]{0,1:T(1,128)S(1)}, s32[128,1]{0,1:T(1,128)}, u32[]{:S(2)}) copy-start(s32[128,1]{0,1:T(1,128)} %param.12) | copy-start | bytes 1540
  62.1 15.5 %copy-start.3 = (bf16[256,768]{1,0:T(8,128)(2,1)S(1)}, bf16[256,768]{1,0:T(8,128)(2,1)}, u32[]{:S(2)}) copy-start(bf16[256,768]{1,0:T(8,128)(2,1)} %wo_ref.3) | copy-start | bytes 1179652
  62.1 15.5 %copy-start.4 = (bf16[128,256]{1,0:T(8,128)(2,1)S(1)}, bf16[128,256]{1,0:T(8,128)(2,1)}, u32[]{:S(2)}) copy-start(bf16[128,256]{1,0:T(8,128)(2,1)} %k_ref.3) | copy-start | bytes 196612
  62.1 15.5 %copy-start.5 = (bf16[128,256]{1,0:T(8,128)(2,1)S(1)}, bf16[128,256]{1,0:T(8,128)(2,1)}, u32[]{:S(2)}) copy-start(bf16[128,256]{1,0:T(8,128)(2,1)} %v_ref.3) | copy-start | bytes 196612
  115.7 16.3 %copy-start.7 = (s32[128]{0:T(128)S(1)}, s32[128]{0:T(128)}, u32[]{:S(2)}) copy-start(s32[128]{0:T(128)} %param.11) | copy-start | bytes 1540

commit v6 on v5

--- a/solution.py
+++ b/solution.py
@@ -18,7 +18,6 @@
 LIMIT = 16 * 2**20
 FLOPS = 10**10
 VMEM = pl.BlockSpec(memory_space=pltpu.VMEM)
-SMEM = pl.BlockSpec(memory_space=pltpu.SMEM)
 
 
 def nn(a, b):
@@ -41,19 +40,19 @@
     return lax.broadcasted_iota(jnp.int32, shape, dim)
 
 
-def call(kernel, outs, *args, far=(), home=0, scalars=0):
+def call(kernel, outs, *args, far=(), home=0):
     single = not isinstance(outs, (list, tuple))
     shapes = [outs] if single else list(outs)
     nbytes = sum(a.size * a.dtype.itemsize for a in args)
 
     def near(n, a):
         space = pltpu.HBM if n in far else pltpu.VMEM
-        return a if n < scalars else pltpu.with_memory_space_constraint(a, space)
+        return pltpu.with_memory_space_constraint(a, space)
 
     res = pl.pallas_call(
         kernel,
         out_shape=[s if n < home else pltpu.VMEM(s.shape, s.dtype) for n, s in enumerate(shapes)],
-        in_specs=[SMEM] * scalars + [VMEM] * (len(args) - scalars),
+        in_specs=[VMEM] * len(args),
         out_specs=[VMEM] * len(shapes),
         cost_estimate=pl.CostEstimate(flops=FLOPS, bytes_accessed=nbytes, transcendentals=0),
         compiler_params=pltpu.CompilerParams(vmem_limit_bytes=LIMIT),
@@ -76,7 +75,7 @@
     return match, jnp.where(match & (nn(hot(match), earlier) > 0.5), 1.0, 0.0)
 
 
-def pack(_, e_ref, ogt_ref, q_ref, out_ref):
+def pack(e_ref, ogt_ref, q_ref, out_ref):
     match, again = repeats(e_ref[...])
     first = (jnp.where(match, 1.0, 0.0) - again).astype(BF)
     second = jnp.broadcast_to(jnp.sum(again, axis=0, keepdims=True), (16, BLOCK)).astype(BF)
@@ -86,23 +85,28 @@
         [token[0:1, i * 64 : (i + 1) * 64] for i in range(7)] + [jnp.zeros((1, 64), F32)], axis=0
     )
     spare = jnp.broadcast_to(spare[None], (NZ, 8, 64)).reshape(BLOCK, 64)
+    same = hot((iota((BLOCK, BLOCK), 0) >> 3) == (iota((BLOCK, BLOCK), 1) >> 3))
+    goes = jnp.broadcast_to(jnp.sum(again, axis=1, keepdims=True), (BLOCK, BLOCK)).astype(BF)
+    spare = jnp.where(nn(same, goes)[:, 0:64] > 0.5, spare, 0.0)
     rows = jnp.concatenate([nt(first, ogt), spare], axis=1)
     out = [rows.reshape(NZ, 8, HD), nn(first, q).reshape(NZ, 8, HD)]
     out_ref[...] = jnp.concatenate(out, axis=1).astype(BF)
 
 
-def forward(in_ref, out_ref, q_ref, sq_ref):
+def forward(in_ref, out_ref, first_ref, second_ref, q_ref, sq_ref):
     x = in_ref[...].reshape(2 * BLOCK, HD)
     o = iota((BLOCK, 2 * BLOCK), 0)
     i = iota((BLOCK, 2 * BLOCK), 1)
     here = (i >> 4) == (o & 15)
     firsts = nn(hot(here & ((i & 15) == (o >> 4))), x[:, 0:DQ])
+    first_ref[...] = firsts.astype(BF)
     q_ref[...] = nn(hot(here & ((i & 15) == (o >> 4) + 8)), x).astype(BF)
     o = iota((NZ, 2 * BLOCK), 0)
     i = iota((NZ, 2 * BLOCK), 1)
     here = (i >> 4) == o
     spare = x[:, DQ:HD]
     seconds = jnp.concatenate([nn(hot(here & ((i & 15) == n)), spare) for n in range(7)], axis=1)
+    second_ref[...] = seconds[:, 0:DQ].astype(BF)
     sq_ref[...] = seconds[:, DQ:448].astype(BF)
     seconds = jnp.broadcast_to(seconds[None, :, 0:DQ], (NP, NZ, DQ)).reshape(BLOCK, DQ)
     rows = jnp.concatenate([firsts, seconds], axis=1).astype(BF)
@@ -120,45 +124,59 @@
     return before + r, count > r + 0.5
 
 
-def experts(h_ref, in_ref, c_ref, pre_ref, wd_ref, wu_ref, out_ref, own_ref):
+def experts(in_ref, c_ref, pre_ref, wd_ref, wu_ref, out_ref):
     def columns(h):
         x = jnp.concatenate([in_ref[p * NH + h] for p in range(NP)], axis=0)
         return jnp.concatenate([x[:, 0:DQ], x[:, DQ : 2 * DQ]], axis=0)
 
     row, live = place(c_ref[...].astype(F32))
     pick = hot((iota((2 * BLOCK, 2 * BLOCK), 0).astype(F32) == row) & live)
-    on = hot(pre_ref[...].astype(F32) > 0)
-    mask = tn(on, pick)
+    mask = tn(pick, hot(pre_ref[...].astype(F32) > 0))
     x = jnp.concatenate([columns(h) for h in range(NH)], axis=1)
-    mid = jnp.where(mask > 0.5, nt(wd_ref[...], x), 0.0).astype(BF)
-    out_ref[...] = nn(wu_ref[...], mid).astype(BF).reshape(NH, DQ, 2 * BLOCK)
-    own = nt(eye(DQ), columns(h_ref[0]))
-    own_ref[...] = jnp.where(live, own, 0.0).astype(BF)
-
-
-def add_up(parts_ref, own_ref, out_ref):
-    total = parts_ref[0].astype(F32)
-    for h in range(1, NH):
-        total = total + parts_ref[h].astype(F32)
-    gh = (own_ref[...].astype(F32) + total.astype(BF).astype(F32)).astype(BF)
-    rows = nt(eye(2 * BLOCK), gh)
-    rows = jnp.concatenate([rows[0:BLOCK], rows[BLOCK:]], axis=1).astype(BF)
-    rows = jnp.broadcast_to(rows.reshape(NP, 1, 16, 384), (NP, NH, 16, 384))
-    out_ref[...] = rows.reshape(NP * NH, 16, 384)
+    mid = jnp.where(mask > 0.5, nt(x, wd_ref[...]), 0.0).astype(BF)
+    part = nt(mid, wu_ref[...])
+    for h in range(NH):
+        own = part[:, h * DQ : (h + 1) * DQ]
+        own = jnp.concatenate([own[0:BLOCK], own[BLOCK:]], axis=1).astype(BF)
+        for p in range(NP):
+            out_ref[p * NH + h] = own[p * 16 : (p + 1) * 16]
+
+
+def add_up(in_ref, first_ref, second_ref, out_ref):
+    firsts, seconds = [], jnp.zeros((16, DQ), F32)
+    for p in range(NP):
+        total = in_ref[p * NH].astype(F32)
+        for h in range(1, NH):
+            total = total + in_ref[p * NH + h].astype(F32)
+        firsts.append(total[:, 0:DQ])
+        seconds = seconds + total[:, DQ : 2 * DQ]
+
+    def grad(own, added):
+        return own.astype(F32) + added.astype(BF).astype(F32)
+
+    first = grad(first_ref[...], jnp.concatenate(firsts, axis=0))
+    second = grad(second_ref[...], seconds)
+    rows = [
+        first[:, 0:128],
+        jnp.concatenate([first[0:64, 128:DQ], first[64:128, 128:DQ]], axis=1),
+        second[:, 0:128],
+        jnp.concatenate([second[0:8, 128:DQ], second[8:16, 128:DQ]], axis=1),
+    ]
+    rows = jnp.concatenate(rows, axis=0).astype(BF)
+    out_ref[...] = jnp.broadcast_to(rows[None], (NH, 216, BLOCK))
 
 
 def state_parts(in_ref, q_ref, sq_ref, wo_ref, k_ref, v_ref, out_ref, first_ref, second_ref):
     def columns(h):
-        return jnp.concatenate([in_ref[p * NH + h, :, 0:DQ] for p in range(NP)], axis=0)
-
-    def seconds(h):
-        total = in_ref[h, :, DQ : 2 * DQ].astype(F32)
-        for p in range(1, NP):
-            total = total + in_ref[p * NH + h, :, DQ : 2 * DQ].astype(F32)
-        return total
-
-    first = jnp.concatenate([columns(h) for h in range(NH)], axis=1)
-    second = jnp.concatenate([seconds(h) for h in range(NH)], axis=1).astype(BF)
+        x = in_ref[h].astype(F32)
+        last = jnp.concatenate([x[128:192, 0:64], x[128:192, 64:128]], axis=0)
+        first = jnp.concatenate([x[0:128], last], axis=1)
+        last = jnp.concatenate([x[208:216, 0:64], x[208:216, 64:128]], axis=0)
+        return first, jnp.concatenate([x[192:208], last], axis=1)
+
+    parts = [columns(h) for h in range(NH)]
+    first = jnp.concatenate([a for a, _ in parts], axis=1).astype(BF)
+    second = jnp.concatenate([b for _, b in parts], axis=1).astype(BF)
     first_ref[...] = first
     second_ref[...] = second
     wo = wo_ref[...]
@@ -237,14 +255,13 @@
 def shards(out_grad, expert_of, counts, w_up, w_down, pre_act, queries, keys, values, w_out):
     e = expert_of.reshape(1, BLOCK)
     c = counts.reshape(1, BLOCK)
-    h = lax.axis_index("y").reshape(1)
-    sent = call(pack, sds(NZ, 16, HD), h, e, out_grad.T, queries, far=range(1, 4), scalars=1)
-    outs = [sds(32, 16, 384), sds(BLOCK, HD), sds(NZ, HD)]
-    msgs, q, sq = call(forward, outs, swap(sent, Z))
+    sent = call(pack, sds(NZ, 16, HD), e, out_grad.T, queries, far=range(3))
+    outs = [sds(32, 16, 384), sds(BLOCK, DQ), sds(NZ, DQ), sds(BLOCK, HD), sds(NZ, HD)]
+    msgs, first, second, q, sq = call(forward, outs, swap(sent, Z))
     msgs = swap(msgs, PLANE + ("y",))
-    outs = [sds(NH, DQ, 2 * BLOCK), sds(DQ, 2 * BLOCK)]
-    parts, own = call(experts, outs, h, msgs, c, pre_act, w_down[0], w_up[0], scalars=1)
-    msgs = swap(call(add_up, sds(32, 16, 384), swap(parts, "y"), own), PLANE + ("y",))
+    msgs = call(experts, sds(32, 16, 384), msgs, c, pre_act, w_down[0], w_up[0])
+    msgs = swap(msgs, PLANE + ("y",))
+    msgs = swap(call(add_up, sds(NH, 216, BLOCK), msgs, first, second), "y")
     outs = [sds(16, 16, 512), sds(BLOCK, D), sds(NZ, D)]
     msgs, first, second = call(state_parts, outs, msgs, q, sq, w_out, keys, values)
     msgs = swap(msgs, PLANE + ("zl",))

time: 134 us -> 132 us (0.985)
    all_to_all x7, blocking collectives: 126 us -> 125 us  [swap(): return lax.all_to_all(tiles, axis, split_axis=0, concat_axis=0, tiled=True)]
where the time goes in v6:
time: 132 us; the launch traced here: 131 us
  blocking collectives  125 us (95%)
  Pallas kernels  5.87 us (4%)
    all_to_all x7, blocking collectives, swap(): return lax.all_to_all(tiles, axis, split_axis=0, concat_axis=0, tiled=True)  125 us
    pallas_call x8, Pallas kernels, call(): pl.pallas_call(kernel, out_shape=[s if n < home else pltpu.VMEM(s.shape,...  5.87 us

profile of v6, /device:TPU:1, one launch (start us, length us, event | category | flops | bytes accessed | tf_op | source)
XLA Modules:
  0.0 131.4 jit_solution(11812598880331673548)
XLA Ops:
  0.6 1.4 %pack.1 = bf16[16,16,256]{2,1,0:T(8,128)(2,1)S(1)} custom-call(s32[1,128]{1,0:T(1,128)} %bitcast.8, bf16[192,128]{1,0:T(8,128)(2,1)} %bitcast.10, bf16[128,256]{1,0:T(8,128)(2,1)} %q_ref.1), custom_call_target="tpu_custom_call" | custom-call | flops 10000000000 | bytes 115200 | tf_op jit(solution)/shard_map/pack/pallas_call | solution.py:52
  2.0 27.5 %all_to_all.35.in_ref = bf16[16,16,256]{2,1,0:T(8,128)(2,1)S(1)} all-to-all(bf16[16,16,256]{2,1,0:T(8,128)(2,1)S(1)} %pack.1), channel_id=1, replica_groups=mesh['zh'=8,'zl'=2,'x'=4,'c'=2,'y'=4] {'zh','zl'}, dimensions={0} | all-to-all | bytes 262144 | tf_op jit(solution)/shard_map/all_to_all | solution.py:252
  29.5 0.0 copy-start
  29.5 0.0 copy-start.1
  29.5 0.4 forward.1
  30.0 20.9 %all_to_all.36.in_ref = bf16[32,16,384]{2,1,0:T(8,128)(2,1)S(1)} all-to-all(bf16[32,16,384]{2,1,0:T(8,128)(2,1)S(1)} %get-tuple-element.12), channel_id=1, replica_groups=mesh['zh'=8,'zl'=2,'x'=4,'c'=2,'y'=4] {'x','c','y'}, dimensions={0} | all-to-all | bytes 786432 | tf_op jit(solution)/shard_map/all_to_all | solution.py:252
  50.8 0.0 copy-done
  50.8 0.0 copy-done.1
  50.8 0.0 copy-done.2
  50.8 0.0 copy-done.6
  50.8 1.3 experts.1
  52.1 14.0 %all_to_all.37.in_ref = bf16[32,16,384]{2,1,0:T(8,128)(2,1)S(1)} all-to-all(bf16[32,16,384]{2,1,0:T(8,128)(2,1)S(1)} %experts.1), channel_id=1, replica_groups=mesh['zh'=8,'zl'=2,'x'=4,'c'=2,'y'=4] {'x','c','y'}, dimensions={0} | all-to-all | bytes 786432 | tf_op jit(solution)/shard_map/all_to_all | solution.py:252
  66.1 0.2 add_up.1
  66.3 7.8 %all_to_all.38.in_ref = bf16[4,216,128]{2,1,0:T(8,128)(2,1)S(1)} all-to-all(bf16[4,216,128]{2,1,0:T(8,128)(2,1)S(1)} %add_up.1), channel_id=1, replica_groups=mesh['zh'=8,'zl'=2,'x'=4,'c'=2,'y'=4] {'y'}, dimensions={0} | all-to-all | bytes 442368 | tf_op jit(solution)/shard_map/all_to_all | solution.py:252
  74.1 0.0 copy-done.3
  74.1 0.0 copy-done.4
  74.1 0.0 copy-done.5
  74.1 0.7 state_parts.1
  74.8 12.3 %all_to_all.39.in_ref = bf16[16,16,512]{2,1,0:T(8,128)(2,1)S(1)} all-to-all(bf16[16,16,512]{2,1,0:T(8,128)(2,1)S(1)} %get-tuple-element.17), channel_id=1, replica_groups=mesh['zh'=8,'zl'=2,'x'=4,'c'=2,'y'=4] {'x','c','zl'}, dimensions={0} | all-to-all | bytes 524288 | tf_op jit(solution)/shard_map/all_to_all | solution.py:252
  87.0 0.4 regroup.1
  87.4 26.0 %all_to_all.40.in_ref.back_ref = bf16[16,16,1024]{2,1,0:T(8,128)(2,1)S(1)} all-to-all(bf16[16,16,1024]{2,1,0:T(8,128)(2,1)S(1)} %regroup.1), channel_id=1, replica_groups=mesh['zh'=8,'zl'=2,'x'=4,'c'=2,'y'=4] {'zh','zl'}, dimensions={0} | all-to-all | bytes 1048576 | tf_op jit(solution)/shard_map/all_to_all | solution.py:252
  113.5 16.3 %all_to_all.41.in_ref = bf16[8,16,1024]{2,1,0:T(8,128)(2,1)S(1)} all-to-all(bf16[8,16,1024]{2,1,0:T(8,128)(2,1)S(1)} %reduce_states.1), channel_id=1, replica_groups=mesh['zh'=8,'zl'=2,'x'=4,'c'=2,'y'=4] {'x','c'}, dimensions={0} | all-to-all | bytes 524288 | tf_op jit(solution)/shard_map/all_to_all | solution.py:252
  129.8 0.0 copy-done.7
  129.8 1.6 %finish.1 = (bf16[128,768]{1,0:T(8,128)(2,1)}, bf16[128,256]{1,0:T(8,128)(2,1)}, bf16[128,256]{1,0:T(8,128)(2,1)}, bf16[128,256]{1,0:T(8,128)(2,1)}) custom-call(bf16[8,16,1024]{2,1,0:T(8,128)(2,1)S(1)} %all_to_all.41.in_ref, bf16[16,16,1024]{2,1,0:T(8,128)(2,1)S(1)} %all_to_all.40.in_ref.back_ref, s32[1,128]{1,0:T(1,128)S(1)} %bitcast.9, ...), custom_call_target="tpu_custom_call" | custom-call | flops 10000000000 | bytes 1311232 | tf_op jit(solution)/shard_map/finish/pallas_call | solution.py:52
  (7 shorter events, 0.1 us)
Async XLA Ops:
  29.5 21.3 %copy-start = (bf16[1,768,768]{2,1,0:T(8,128)(2,1)S(1)}, bf16[1,768,768]{2,1,0:T(8,128)(2,1)}, u32[]{:S(2)}) copy-start(bf16[1,768,768]{2,1,0:T(8,128)(2,1)} %param.14) | copy-start | bytes 3538948
  29.5 21.3 %copy-start.1 = (bf16[1,768,768]{2,1,0:T(8,128)(2,1)S(1)}, bf16[1,768,768]{2,1,0:T(8,128)(2,1)}, u32[]{:S(2)}) copy-start(bf16[1,768,768]{2,1,0:T(8,128)(2,1)} %param.13) | copy-start | bytes 3538948
  29.5 21.3 %copy-start.2 = (bf16[256,768]{1,0:T(8,128)(2,1)S(1)}, bf16[256,768]{1,0:T(8,128)(2,1)}, u32[]{:S(2)}) copy-start(bf16[256,768]{1,0:T(8,128)(2,1)} %pre_ref.1) | copy-start | bytes 1179652
  29.5 21.3 %copy-start.6 = (s32[128,1]{0,1:T(1,128)S(1)}, s32[128,1]{0,1:T(1,128)}, u32[]{:S(2)}) copy-start(s32[128,1]{0,1:T(1,128)} %param.12) | copy-start | bytes 1540
  66.1 8.0 %copy-start.3 = (bf16[256,768]{1,0:T(8,128)(2,1)S(1)}, bf16[256,768]{1,0:T(8,128)(2,1)}, u32[]{:S(2)}) copy-start(bf16[256,768]{1,0:T(8,128)(2,1)} %wo_ref.3) | copy-start | bytes 1179652
  66.1 8.0 %copy-start.4 = (bf16[128,256]{1,0:T(8,128)(2,1)S(1)}, bf16[128,256]{1,0:T(8,128)(2,1)}, u32[]{:S(2)}) copy-start(bf16[128,256]{1,0:T(8,128)(2,1)} %k_ref.3) | copy-start | bytes 196612
  66.1 8.0 %copy-start.5 = (bf16[128,256]{1,0:T(8,128)(2,1)S(1)}, bf16[128,256]{1,0:T(8,128)(2,1)}, u32[]{:S(2)}) copy-start(bf16[128,256]{1,0:T(8,128)(2,1)} %v_ref.3) | copy-start | bytes 196612
  113.5 16.3 %copy-start.7 = (s32[128]{0:T(128)S(1)}, s32[128]{0:T(128)}, u32[]{:S(2)}) copy-start(s32[128]{0:T(128)} %param.11) | copy-start | bytes 1540

commit v7 on v6

--- a/solution.py
+++ b/solution.py
@@ -189,32 +189,37 @@
     total = in_ref[0].astype(F32)
     for p in range(1, 2 * NP):
         total = total + in_ref[p].astype(F32)
-    out_ref[:, :, 0:512] = jnp.broadcast_to(total.astype(BF)[None], (NZ, 16, 512))
+    total = jnp.broadcast_to(total.astype(BF)[None], (NZ, 16, 512))
+    for n in range(4):
+        out_ref[:, n * 16 : (n + 1) * 16, :] = total[:, :, n * BLOCK : (n + 1) * BLOCK]
     x = first_ref[...]
     o = iota((2 * BLOCK, BLOCK), 0)
     i = iota((2 * BLOCK, BLOCK), 1)
     here = ((o & 7) == (i >> 4)) & ((o >> 4) == (i & 15))
     lower, higher = hot(here & ((o & 8) == 0)), hot(here & ((o & 8) != 0))
     rows = nn(lower, x[:, 0:384]) + nn(higher, x[:, 384:768])
-    out_ref[:, :, 512:896] = rows.astype(BF).reshape(NZ, 16, 384)
+    rows = rows.astype(BF).reshape(NZ, 16, 384)
+    for n in range(3):
+        out_ref[:, 64 + n * 16 : 80 + n * 16, :] = rows[:, :, n * BLOCK : (n + 1) * BLOCK]
     second = second_ref[...]
-    o = iota((2 * BLOCK, NZ), 0)
-    i = iota((2 * BLOCK, NZ), 1)
-    rows = jnp.zeros((2 * BLOCK, BLOCK), F32)
+    o = iota((BLOCK, NZ), 0)
+    i = iota((BLOCK, NZ), 1)
+    rows = jnp.zeros((BLOCK, BLOCK), F32)
     for n in range(6):
-        pick = hot(((o >> 4) == i) & ((o & 15) == n))
+        pick = hot(((o >> 3) == i) & ((o & 7) == n))
         rows = rows + nn(pick, second[:, n * BLOCK : (n + 1) * BLOCK])
-    out_ref[:, :, 896:1024] = rows.astype(BF).reshape(NZ, 16, BLOCK)
+    out_ref[:, 112:120, :] = rows.astype(BF).reshape(NZ, 8, BLOCK)
 
 
 def reduce_states(in_ref, out_ref):
     for zl in range(2):
-        total = in_ref[zl, :, 0:512].astype(F32)
+        total = in_ref[zl, 0:64, :].astype(F32)
         for z in range(2 + zl, NZ, 2):
-            total = total + in_ref[z, :, 0:512].astype(F32)
-        total = jnp.broadcast_to(total.astype(BF)[None], (NP, 16, 512))
-        out_ref[:, :, zl * HD : (zl + 1) * HD] = total[:, :, 0:HD]
-        out_ref[:, :, 512 + zl * HD : 512 + (zl + 1) * HD] = total[:, :, HD:]
+            total = total + in_ref[z, 0:64, :].astype(F32)
+        total = jnp.broadcast_to(total.astype(BF)[None], (NP, 64, BLOCK))
+        for n in range(4):
+            at = (n // 2) * 512 + zl * HD + (n % 2) * BLOCK
+            out_ref[:, :, at : at + BLOCK] = total[:, n * 16 : (n + 1) * 16, :]
 
 
 def finish(in_ref, back_ref, e_ref, wo_ref, k_ref, v_ref, gh_ref, gq_ref, gk_ref, gv_ref):
@@ -232,10 +237,11 @@
     row = iota((2 * BLOCK, BLOCK), 0)
     first = ((row & 7) == (e & 7)) & ((row >> 4) == (e >> 3)) & (rank < 0.5)
     lower, higher = hot(first & ((row & 8) == 0)), hot(first & ((row & 8) != 0))
-    rows = back_ref[:, :, 512:896].reshape(2 * BLOCK, 384)
-    second = back_ref[0, 0:8, 896:1024].astype(F32)
+    rows = [back_ref[:, 64 + n * 16 : 80 + n * 16, :] for n in range(3)]
+    rows = jnp.concatenate(rows, axis=2).reshape(2 * BLOCK, 384)
+    second = back_ref[0, 112:120, :].astype(F32)
     for z in range(1, NZ):
-        second = second + back_ref[z, 0:8, 896:1024].astype(F32)
+        second = second + back_ref[z, 112:120, :].astype(F32)
     second = jnp.concatenate([second[n : n + 1] for n in range(6)], axis=1)
     second = jnp.broadcast_to(second, (16, D)).astype(BF)
     one = iota((16, BLOCK), 0) == 0
@@ -265,7 +271,7 @@
     outs = [sds(16, 16, 512), sds(BLOCK, D), sds(NZ, D)]
     msgs, first, second = call(state_parts, outs, msgs, q, sq, w_out, keys, values)
     msgs = swap(msgs, PLANE + ("zl",))
-    back = swap(call(regroup, sds(NZ, 16, 1024), msgs, first, second), Z)
+    back = swap(call(regroup, sds(NZ, 120, BLOCK), msgs, first, second), Z)
     states = swap(call(reduce_states, sds(NP, 16, 1024), back), PLANE)
     outs = [sds(BLOCK, D)] + [sds(BLOCK, HD)] * 3
     return tuple(call(finish, outs, states, back, e, w_out, keys, values, home=4))

time: 132 us -> 131 us (level)
  no operation moved by 1% of the time
where the time goes in v7:
time: 131 us; the launch traced here: 130 us
  blocking collectives  124 us (95%)
  Pallas kernels  5.84 us (4%)
    all_to_all x7, blocking collectives, swap(): return lax.all_to_all(tiles, axis, split_axis=0, concat_axis=0, tiled=True)  124 us
    pallas_call x8, Pallas kernels, call(): pl.pallas_call(kernel, out_shape=[s if n < home else pltpu.VMEM(s.shape,...  5.84 us

profile of v7, /device:TPU:1, one launch (start us, length us, event | category | flops | bytes accessed | tf_op | source)
XLA Modules:
  0.0 130.5 jit_solution(7141054752812235284)
XLA Ops:
  0.6 1.4 %pack.1 = bf16[16,16,256]{2,1,0:T(8,128)(2,1)S(1)} custom-call(s32[1,128]{1,0:T(1,128)} %bitcast.8, bf16[192,128]{1,0:T(8,128)(2,1)} %bitcast.10, bf16[128,256]{1,0:T(8,128)(2,1)} %q_ref.1), custom_call_target="tpu_custom_call" | custom-call | flops 10000000000 | bytes 115200 | tf_op jit(solution)/shard_map/pack/pallas_call | solution.py:52
  2.0 27.5 %all_to_all.35.in_ref = bf16[16,16,256]{2,1,0:T(8,128)(2,1)S(1)} all-to-all(bf16[16,16,256]{2,1,0:T(8,128)(2,1)S(1)} %pack.1), channel_id=1, replica_groups=mesh['zh'=8,'zl'=2,'x'=4,'c'=2,'y'=4] {'zh','zl'}, dimensions={0} | all-to-all | bytes 262144 | tf_op jit(solution)/shard_map/all_to_all | solution.py:258
  29.5 0.0 copy-start
  29.5 0.4 forward.1
  30.0 20.9 %all_to_all.36.in_ref = bf16[32,16,384]{2,1,0:T(8,128)(2,1)S(1)} all-to-all(bf16[32,16,384]{2,1,0:T(8,128)(2,1)S(1)} %get-tuple-element.12), channel_id=1, replica_groups=mesh['zh'=8,'zl'=2,'x'=4,'c'=2,'y'=4] {'x','c','y'}, dimensions={0} | all-to-all | bytes 786432 | tf_op jit(solution)/shard_map/all_to_all | solution.py:258
  50.8 0.0 copy-done
  50.8 0.0 copy-done.1
  50.8 0.0 copy-done.2
  50.8 0.0 copy-done.6
  50.8 1.3 experts.1
  52.1 14.0 %all_to_all.37.in_ref = bf16[32,16,384]{2,1,0:T(8,128)(2,1)S(1)} all-to-all(bf16[32,16,384]{2,1,0:T(8,128)(2,1)S(1)} %experts.1), channel_id=1, replica_groups=mesh['zh'=8,'zl'=2,'x'=4,'c'=2,'y'=4] {'x','c','y'}, dimensions={0} | all-to-all | bytes 786432 | tf_op jit(solution)/shard_map/all_to_all | solution.py:258
  66.1 0.2 add_up.1
  66.3 7.8 %all_to_all.38.in_ref = bf16[4,216,128]{2,1,0:T(8,128)(2,1)S(1)} all-to-all(bf16[4,216,128]{2,1,0:T(8,128)(2,1)S(1)} %add_up.1), channel_id=1, replica_groups=mesh['zh'=8,'zl'=2,'x'=4,'c'=2,'y'=4] {'y'}, dimensions={0} | all-to-all | bytes 442368 | tf_op jit(solution)/shard_map/all_to_all | solution.py:258
  74.1 0.0 copy-done.3
  74.1 0.0 copy-done.4
  74.1 0.0 copy-done.5
  74.1 0.7 state_parts.1
  74.8 12.3 %all_to_all.39.in_ref = bf16[16,16,512]{2,1,0:T(8,128)(2,1)S(1)} all-to-all(bf16[16,16,512]{2,1,0:T(8,128)(2,1)S(1)} %get-tuple-element.17), channel_id=1, replica_groups=mesh['zh'=8,'zl'=2,'x'=4,'c'=2,'y'=4] {'x','c','zl'}, dimensions={0} | all-to-all | bytes 524288 | tf_op jit(solution)/shard_map/all_to_all | solution.py:258
  87.0 0.3 regroup.1
  87.4 25.0 %all_to_all.40.in_ref.back_ref = bf16[16,120,128]{2,1,0:T(8,128)(2,1)S(1)} all-to-all(bf16[16,120,128]{2,1,0:T(8,128)(2,1)S(1)} %regroup.1), channel_id=1, replica_groups=mesh['zh'=8,'zl'=2,'x'=4,'c'=2,'y'=4] {'zh','zl'}, dimensions={0} | all-to-all | bytes 983040 | tf_op jit(solution)/shard_map/all_to_all | solution.py:258
  112.3 0.1 reduce_states.1
  112.4 16.5 %all_to_all.41.in_ref = bf16[8,16,1024]{2,1,0:T(8,128)(2,1)S(1)} all-to-all(bf16[8,16,1024]{2,1,0:T(8,128)(2,1)S(1)} %reduce_states.1), channel_id=1, replica_groups=mesh['zh'=8,'zl'=2,'x'=4,'c'=2,'y'=4] {'x','c'}, dimensions={0} | all-to-all | bytes 524288 | tf_op jit(solution)/shard_map/all_to_all | solution.py:258
  128.9 0.0 copy-done.7
  128.9 1.6 %finish.1 = (bf16[128,768]{1,0:T(8,128)(2,1)}, bf16[128,256]{1,0:T(8,128)(2,1)}, bf16[128,256]{1,0:T(8,128)(2,1)}, bf16[128,256]{1,0:T(8,128)(2,1)}) custom-call(bf16[8,16,1024]{2,1,0:T(8,128)(2,1)S(1)} %all_to_all.41.in_ref, bf16[16,120,128]{2,1,0:T(8,128)(2,1)S(1)} %all_to_all.40.in_ref.back_ref, s32[1,128]{1,0:T(1,128)S(1)} %bitcast.9, ...), custom_call_target="tpu_custom_call" | custom-call | flops 10000000000 | bytes 1278464 | tf_op jit(solution)/shard_map/finish/pallas_call | solution.py:52
  (7 shorter events, 0.0 us)
Async XLA Ops:
  29.5 21.3 %copy-start = (bf16[1,768,768]{2,1,0:T(8,128)(2,1)S(1)}, bf16[1,768,768]{2,1,0:T(8,128)(2,1)}, u32[]{:S(2)}) copy-start(bf16[1,768,768]{2,1,0:T(8,128)(2,1)} %param.14) | copy-start | bytes 3538948
  29.5 21.3 %copy-start.1 = (bf16[1,768,768]{2,1,0:T(8,128)(2,1)S(1)}, bf16[1,768,768]{2,1,0:T(8,128)(2,1)}, u32[]{:S(2)}) copy-start(bf16[1,768,768]{2,1,0:T(8,128)(2,1)} %param.13) | copy-start | bytes 3538948
  29.5 21.3 %copy-start.2 = (bf16[256,768]{1,0:T(8,128)(2,1)S(1)}, bf16[256,768]{1,0:T(8,128)(2,1)}, u32[]{:S(2)}) copy-start(bf16[256,768]{1,0:T(8,128)(2,1)} %pre_ref.1) | copy-start | bytes 1179652
  29.5 21.3 %copy-start.6 = (s32[128,1]{0,1:T(1,128)S(1)}, s32[128,1]{0,1:T(1,128)}, u32[]{:S(2)}) copy-start(s32[128,1]{0,1:T(1,128)} %param.12) | copy-start | bytes 1540
  66.1 8.0 %copy-start.3 = (bf16[256,768]{1,0:T(8,128)(2,1)S(1)}, bf16[256,768]{1,0:T(8,128)(2,1)}, u32[]{:S(2)}) copy-start(bf16[256,768]{1,0:T(8,128)(2,1)} %wo_ref.3) | copy-start | bytes 1179652
  66.1 8.0 %copy-start.4 = (bf16[128,256]{1,0:T(8,128)(2,1)S(1)}, bf16[128,256]{1,0:T(8,128)(2,1)}, u32[]{:S(2)}) copy-start(bf16[128,256]{1,0:T(8,128)(2,1)} %k_ref.3) | copy-start | bytes 196612
  66.1 8.0 %copy-start.5 = (bf16[128,256]{1,0:T(8,128)(2,1)S(1)}, bf16[128,256]{1,0:T(8,128)(2,1)}, u32[]{:S(2)}) copy-start(bf16[128,256]{1,0:T(8,128)(2,1)} %v_ref.3) | copy-start | bytes 196612
  112.3 16.6 %copy-start.7 = (s32[128]{0:T(128)S(1)}, s32[128]{0:T(128)}, u32[]{:S(2)}) copy-start(s32[128]{0:T(128)} %param.11) | copy-start | bytes 1540

commit v8 on v7

--- a/solution.py
+++ b/solution.py
@@ -189,9 +189,11 @@
     total = in_ref[0].astype(F32)
     for p in range(1, 2 * NP):
         total = total + in_ref[p].astype(F32)
-    total = jnp.broadcast_to(total.astype(BF)[None], (NZ, 16, 512))
-    for n in range(4):
-        out_ref[:, n * 16 : (n + 1) * 16, :] = total[:, :, n * BLOCK : (n + 1) * BLOCK]
+    total = total.astype(BF)
+    for z in range(NZ):
+        for n in range(2):
+            at = (z % 2) * HD + n * BLOCK
+            out_ref[z, n * 16 : (n + 1) * 16, :] = total[:, at : at + BLOCK]
     x = first_ref[...]
     o = iota((2 * BLOCK, BLOCK), 0)
     i = iota((2 * BLOCK, BLOCK), 1)
@@ -200,7 +202,7 @@
     rows = nn(lower, x[:, 0:384]) + nn(higher, x[:, 384:768])
     rows = rows.astype(BF).reshape(NZ, 16, 384)
     for n in range(3):
-        out_ref[:, 64 + n * 16 : 80 + n * 16, :] = rows[:, :, n * BLOCK : (n + 1) * BLOCK]
+        out_ref[:, 32 + n * 16 : 48 + n * 16, :] = rows[:, :, n * BLOCK : (n + 1) * BLOCK]
     second = second_ref[...]
     o = iota((BLOCK, NZ), 0)
     i = iota((BLOCK, NZ), 1)
@@ -208,40 +210,41 @@
     for n in range(6):
         pick = hot(((o >> 3) == i) & ((o & 7) == n))
         rows = rows + nn(pick, second[:, n * BLOCK : (n + 1) * BLOCK])
-    out_ref[:, 112:120, :] = rows.astype(BF).reshape(NZ, 8, BLOCK)
+    out_ref[:, 80:88, :] = rows.astype(BF).reshape(NZ, 8, BLOCK)
 
 
 def reduce_states(in_ref, out_ref):
     for zl in range(2):
-        total = in_ref[zl, 0:64, :].astype(F32)
+        total = in_ref[zl, 0:32, :].astype(F32)
         for z in range(2 + zl, NZ, 2):
-            total = total + in_ref[z, 0:64, :].astype(F32)
-        total = jnp.broadcast_to(total.astype(BF)[None], (NP, 64, BLOCK))
-        for n in range(4):
-            at = (n // 2) * 512 + zl * HD + (n % 2) * BLOCK
+            total = total + in_ref[z, 0:32, :].astype(F32)
+        total = jnp.broadcast_to(total.astype(BF)[None], (2 * NP, 32, BLOCK))
+        for n in range(2):
+            at = zl * HD + n * BLOCK
             out_ref[:, :, at : at + BLOCK] = total[:, n * 16 : (n + 1) * 16, :]
 
 
 def finish(in_ref, back_ref, e_ref, wo_ref, k_ref, v_ref, gh_ref, gq_ref, gk_ref, gv_ref):
     scaling = 1.0 / math.sqrt(HD * BLOCK * BLOCK)
 
-    def whole(at):
-        a = in_ref[:, :, at : at + HD].reshape(NP, 1, 16, HD)
-        b = in_ref[:, :, at + HD : at + 2 * HD].reshape(NP, 1, 16, HD)
-        return jnp.concatenate([a, b], axis=1).reshape(HD, HD)
-
-    qt, kr = whole(0), whole(512)
+    def whole(zl):
+        pieces = []
+        for p in range(NP):
+            pieces += [in_ref[2 * p + zl, :, 0:HD], in_ref[2 * p + zl, :, HD:]]
+        return jnp.concatenate(pieces, axis=0)
+
+    qt, kr = whole(0), whole(1)
     e = e_ref[...]
     match, again = repeats(e)
     rank = jnp.sum(again, axis=0, keepdims=True)
     row = iota((2 * BLOCK, BLOCK), 0)
     first = ((row & 7) == (e & 7)) & ((row >> 4) == (e >> 3)) & (rank < 0.5)
     lower, higher = hot(first & ((row & 8) == 0)), hot(first & ((row & 8) != 0))
-    rows = [back_ref[:, 64 + n * 16 : 80 + n * 16, :] for n in range(3)]
+    rows = [back_ref[:, 32 + n * 16 : 48 + n * 16, :] for n in range(3)]
     rows = jnp.concatenate(rows, axis=2).reshape(2 * BLOCK, 384)
-    second = back_ref[0, 112:120, :].astype(F32)
+    second = back_ref[0, 80:88, :].astype(F32)
     for z in range(1, NZ):
-        second = second + back_ref[z, 112:120, :].astype(F32)
+        second = second + back_ref[z, 80:88, :].astype(F32)
     second = jnp.concatenate([second[n : n + 1] for n in range(6)], axis=1)
     second = jnp.broadcast_to(second, (16, D)).astype(BF)
     one = iota((16, BLOCK), 0) == 0
@@ -271,8 +274,8 @@
     outs = [sds(16, 16, 512), sds(BLOCK, D), sds(NZ, D)]
     msgs, first, second = call(state_parts, outs, msgs, q, sq, w_out, keys, values)
     msgs = swap(msgs, PLANE + ("zl",))
-    back = swap(call(regroup, sds(NZ, 120, BLOCK), msgs, first, second), Z)
-    states = swap(call(reduce_states, sds(NP, 16, 1024), back), PLANE)
+    back = swap(call(regroup, sds(NZ, 88, BLOCK), msgs, first, second), Z)
+    states = swap(call(reduce_states, sds(2 * NP, 16, 512), back), PLANE + ("zl",))
     outs = [sds(BLOCK, D)] + [sds(BLOCK, HD)] * 3
     return tuple(call(finish, outs, states, back, e, w_out, keys, values, home=4))
 

time: 131 us -> 126 us (0.962)
  blocking collectives: 124 us -> 119 us
    all_to_all x7, blocking collectives: 124 us -> 119 us  [swap(): return lax.all_to_all(tiles, axis, split_axis=0, concat_axis=0, tiled=True)]
where the time goes in v8:
time: 126 us
  blocking collectives  119 us (94%)
  Pallas kernels  5.82 us (5%)
    all_to_all x7, blocking collectives, swap(): return lax.all_to_all(tiles, axis, split_axis=0, concat_axis=0, tiled=True)  119 us
    pallas_call x8, Pallas kernels, call(): pl.pallas_call(kernel, out_shape=[s if n < home else pltpu.VMEM(s.shape,...  5.82 us

profile of v8, /device:TPU:1, one launch (start us, length us, event | category | flops | bytes accessed | tf_op | source)
XLA Modules:
  0.0 125.9 jit_solution(9057200540740933558)
XLA Ops:
  0.6 1.4 %pack.1 = bf16[16,16,256]{2,1,0:T(8,128)(2,1)S(1)} custom-call(s32[1,128]{1,0:T(1,128)} %bitcast.8, bf16[192,128]{1,0:T(8,128)(2,1)} %bitcast.10, bf16[128,256]{1,0:T(8,128)(2,1)} %q_ref.1), custom_call_target="tpu_custom_call" | custom-call | flops 10000000000 | bytes 115200 | tf_op jit(solution)/shard_map/pack/pallas_call | solution.py:52
  2.0 27.5 %all_to_all.35.in_ref = bf16[16,16,256]{2,1,0:T(8,128)(2,1)S(1)} all-to-all(bf16[16,16,256]{2,1,0:T(8,128)(2,1)S(1)} %pack.1), channel_id=1, replica_groups=mesh['zh'=8,'zl'=2,'x'=4,'c'=2,'y'=4] {'zh','zl'}, dimensions={0} | all-to-all | bytes 262144 | tf_op jit(solution)/shard_map/all_to_all | solution.py:261
  29.5 0.0 copy-start
  29.5 0.4 forward.1
  30.0 20.9 %all_to_all.36.in_ref = bf16[32,16,384]{2,1,0:T(8,128)(2,1)S(1)} all-to-all(bf16[32,16,384]{2,1,0:T(8,128)(2,1)S(1)} %get-tuple-element.12), channel_id=1, replica_groups=mesh['zh'=8,'zl'=2,'x'=4,'c'=2,'y'=4] {'x','c','y'}, dimensions={0} | all-to-all | bytes 786432 | tf_op jit(solution)/shard_map/all_to_all | solution.py:261
  50.8 0.0 copy-done
  50.8 0.0 copy-done.1
  50.8 0.0 copy-done.2
  50.8 0.0 copy-done.6
  50.8 1.3 experts.1
  52.1 14.0 %all_to_all.37.in_ref = bf16[32,16,384]{2,1,0:T(8,128)(2,1)S(1)} all-to-all(bf16[32,16,384]{2,1,0:T(8,128)(2,1)S(1)} %experts.1), channel_id=1, replica_groups=mesh['zh'=8,'zl'=2,'x'=4,'c'=2,'y'=4] {'x','c','y'}, dimensions={0} | all-to-all | bytes 786432 | tf_op jit(solution)/shard_map/all_to_all | solution.py:261
  66.1 0.2 add_up.1
  66.3 7.8 %all_to_all.38.in_ref = bf16[4,216,128]{2,1,0:T(8,128)(2,1)S(1)} all-to-all(bf16[4,216,128]{2,1,0:T(8,128)(2,1)S(1)} %add_up.1), channel_id=1, replica_groups=mesh['zh'=8,'zl'=2,'x'=4,'c'=2,'y'=4] {'y'}, dimensions={0} | all-to-all | bytes 442368 | tf_op jit(solution)/shard_map/all_to_all | solution.py:261
  74.1 0.0 copy-done.3
  74.1 0.0 copy-done.4
  74.1 0.0 copy-done.5
  74.1 0.7 state_parts.1
  74.8 12.3 %all_to_all.39.in_ref = bf16[16,16,512]{2,1,0:T(8,128)(2,1)S(1)} all-to-all(bf16[16,16,512]{2,1,0:T(8,128)(2,1)S(1)} %get-tuple-element.17), channel_id=1, replica_groups=mesh['zh'=8,'zl'=2,'x'=4,'c'=2,'y'=4] {'x','c','zl'}, dimensions={0} | all-to-all | bytes 524288 | tf_op jit(solution)/shard_map/all_to_all | solution.py:261
  87.0 0.3 regroup.1
  87.4 19.4 %all_to_all.40.in_ref.back_ref = bf16[16,88,128]{2,1,0:T(8,128)(2,1)S(1)} all-to-all(bf16[16,88,128]{2,1,0:T(8,128)(2,1)S(1)} %regroup.1), channel_id=1, replica_groups=mesh['zh'=8,'zl'=2,'x'=4,'c'=2,'y'=4] {'zh','zl'}, dimensions={0} | all-to-all | bytes 720896 | tf_op jit(solution)/shard_map/all_to_all | solution.py:261
  106.7 0.1 reduce_states.1
  106.8 17.5 %all_to_all.41.in_ref = bf16[16,16,512]{2,1,0:T(8,128)(2,1)S(1)} all-to-all(bf16[16,16,512]{2,1,0:T(8,128)(2,1)S(1)} %reduce_states.1), channel_id=1, replica_groups=mesh['zh'=8,'zl'=2,'x'=4,'c'=2,'y'=4] {'x','c','zl'}, dimensions={0} | all-to-all | bytes 524288 | tf_op jit(solution)/shard_map/all_to_all | solution.py:261
  124.3 0.0 copy-done.7
  124.3 1.6 %finish.1 = (bf16[128,768]{1,0:T(8,128)(2,1)}, bf16[128,256]{1,0:T(8,128)(2,1)}, bf16[128,256]{1,0:T(8,128)(2,1)}, bf16[128,256]{1,0:T(8,128)(2,1)}) custom-call(bf16[16,16,512]{2,1,0:T(8,128)(2,1)S(1)} %all_to_all.41.in_ref, bf16[16,88,128]{2,1,0:T(8,128)(2,1)S(1)} %all_to_all.40.in_ref.back_ref, s32[1,128]{1,0:T(1,128)S(1)} %bitcast.9, ...), custom_call_target="tpu_custom_call" | custom-call | flops 10000000000 | bytes 1147392 | tf_op jit(solution)/shard_map/finish/pallas_call | solution.py:52
  (7 shorter events, 0.0 us)
Async XLA Ops:
  29.5 21.3 %copy-start = (bf16[1,768,768]{2,1,0:T(8,128)(2,1)S(1)}, bf16[1,768,768]{2,1,0:T(8,128)(2,1)}, u32[]{:S(2)}) copy-start(bf16[1,768,768]{2,1,0:T(8,128)(2,1)} %param.14) | copy-start | bytes 3538948
  29.5 21.3 %copy-start.1 = (bf16[1,768,768]{2,1,0:T(8,128)(2,1)S(1)}, bf16[1,768,768]{2,1,0:T(8,128)(2,1)}, u32[]{:S(2)}) copy-start(bf16[1,768,768]{2,1,0:T(8,128)(2,1)} %param.13) | copy-start | bytes 3538948
  29.5 21.3 %copy-start.2 = (bf16[256,768]{1,0:T(8,128)(2,1)S(1)}, bf16[256,768]{1,0:T(8,128)(2,1)}, u32[]{:S(2)}) copy-start(bf16[256,768]{1,0:T(8,128)(2,1)} %pre_ref.1) | copy-start | bytes 1179652
  29.5 21.3 %copy-start.6 = (s32[128,1]{0,1:T(1,128)S(1)}, s32[128,1]{0,1:T(1,128)}, u32[]{:S(2)}) copy-start(s32[128,1]{0,1:T(1,128)} %param.12) | copy-start | bytes 1540
  66.1 8.0 %copy-start.3 = (bf16[256,768]{1,0:T(8,128)(2,1)S(1)}, bf16[256,768]{1,0:T(8,128)(2,1)}, u32[]{:S(2)}) copy-start(bf16[256,768]{1,0:T(8,128)(2,1)} %wo_ref.3) | copy-start | bytes 1179652
  66.1 8.0 %copy-start.4 = (bf16[128,256]{1,0:T(8,128)(2,1)S(1)}, bf16[128,256]{1,0:T(8,128)(2,1)}, u32[]{:S(2)}) copy-start(bf16[128,256]{1,0:T(8,128)(2,1)} %k_ref.3) | copy-start | bytes 196612
  66.1 8.0 %copy-start.5 = (bf16[128,256]{1,0:T(8,128)(2,1)S(1)}, bf16[128,256]{1,0:T(8,128)(2,1)}, u32[]{:S(2)}) copy-start(bf16[128,256]{1,0:T(8,128)(2,1)} %v_ref.3) | copy-start | bytes 196612
  106.7 17.6 %copy-start.7 = (s32[128]{0:T(128)S(1)}, s32[128]{0:T(128)}, u32[]{:S(2)}) copy-start(s32[128]{0:T(128)} %param.11) | copy-start | bytes 1540

commit v9 on v8

--- a/solution.py
+++ b/solution.py
@@ -234,21 +234,20 @@
         return jnp.concatenate(pieces, axis=0)
 
     qt, kr = whole(0), whole(1)
-    e = e_ref[...]
-    match, again = repeats(e)
+    match, again = repeats(e_ref[...])
     rank = jnp.sum(again, axis=0, keepdims=True)
-    row = iota((2 * BLOCK, BLOCK), 0)
-    first = ((row & 7) == (e & 7)) & ((row >> 4) == (e >> 3)) & (rank < 0.5)
-    lower, higher = hot(first & ((row & 8) == 0)), hot(first & ((row & 8) != 0))
+    first = (jnp.where(match, 1.0, 0.0) - again).astype(BF)
     rows = [back_ref[:, 32 + n * 16 : 48 + n * 16, :] for n in range(3)]
-    rows = jnp.concatenate(rows, axis=2).reshape(2 * BLOCK, 384)
+    rows = jnp.concatenate(rows, axis=2).astype(F32)
+    lower = rows[:, 0:8].reshape(BLOCK, 384).astype(BF)
+    higher = rows[:, 8:16].reshape(BLOCK, 384).astype(BF)
     second = back_ref[0, 80:88, :].astype(F32)
     for z in range(1, NZ):
         second = second + back_ref[z, 80:88, :].astype(F32)
     second = jnp.concatenate([second[n : n + 1] for n in range(6)], axis=1)
     second = jnp.broadcast_to(second, (16, D)).astype(BF)
     one = iota((16, BLOCK), 0) == 0
-    gh = jnp.concatenate([tn(lower, rows), tn(higher, rows)], axis=1)
+    gh = jnp.concatenate([tn(first, lower), tn(first, higher)], axis=1)
     gh = (gh + tn(hot(one & (rank > 0.5)), second)).astype(BF)
     gh_ref[...] = gh
     hg = nt(gh, wo_ref[...]).astype(BF)

time: 126 us -> 126 us (level)
  no operation moved by 1% of the time
where the time goes in v9:
time: 126 us
  blocking collectives  119 us (94%)
  Pallas kernels  5.78 us (5%)
    all_to_all x7, blocking collectives, swap(): return lax.all_to_all(tiles, axis, split_axis=0, concat_axis=0, tiled=True)  119 us
    pallas_call x8, Pallas kernels, call(): pl.pallas_call(kernel, out_shape=[s if n < home else pltpu.VMEM(s.shape,...  5.78 us

profile of v9, /device:TPU:1, one launch (start us, length us, event | category | flops | bytes accessed | tf_op | source)
XLA Modules:
  0.0 125.8 jit_solution(14223884664289804172)
XLA Ops:
  0.6 1.4 %pack.1 = bf16[16,16,256]{2,1,0:T(8,128)(2,1)S(1)} custom-call(s32[1,128]{1,0:T(1,128)} %bitcast.8, bf16[192,128]{1,0:T(8,128)(2,1)} %bitcast.10, bf16[128,256]{1,0:T(8,128)(2,1)} %q_ref.1), custom_call_target="tpu_custom_call" | custom-call | flops 10000000000 | bytes 115200 | tf_op jit(solution)/shard_map/pack/pallas_call | solution.py:52
  2.0 27.5 %all_to_all.35.in_ref = bf16[16,16,256]{2,1,0:T(8,128)(2,1)S(1)} all-to-all(bf16[16,16,256]{2,1,0:T(8,128)(2,1)S(1)} %pack.1), channel_id=1, replica_groups=mesh['zh'=8,'zl'=2,'x'=4,'c'=2,'y'=4] {'zh','zl'}, dimensions={0} | all-to-all | bytes 262144 | tf_op jit(solution)/shard_map/all_to_all | solution.py:260
  29.5 0.0 copy-start
  29.5 0.4 forward.1
  30.0 20.9 %all_to_all.36.in_ref = bf16[32,16,384]{2,1,0:T(8,128)(2,1)S(1)} all-to-all(bf16[32,16,384]{2,1,0:T(8,128)(2,1)S(1)} %get-tuple-element.12), channel_id=1, replica_groups=mesh['zh'=8,'zl'=2,'x'=4,'c'=2,'y'=4] {'x','c','y'}, dimensions={0} | all-to-all | bytes 786432 | tf_op jit(solution)/shard_map/all_to_all | solution.py:260
  50.8 0.0 copy-done
  50.8 0.0 copy-done.1
  50.8 0.0 copy-done.2
  50.8 0.0 copy-done.6
  50.8 1.3 experts.1
  52.1 14.0 %all_to_all.37.in_ref = bf16[32,16,384]{2,1,0:T(8,128)(2,1)S(1)} all-to-all(bf16[32,16,384]{2,1,0:T(8,128)(2,1)S(1)} %experts.1), channel_id=1, replica_groups=mesh['zh'=8,'zl'=2,'x'=4,'c'=2,'y'=4] {'x','c','y'}, dimensions={0} | all-to-all | bytes 786432 | tf_op jit(solution)/shard_map/all_to_all | solution.py:260
  66.1 0.2 add_up.1
  66.3 7.8 %all_to_all.38.in_ref = bf16[4,216,128]{2,1,0:T(8,128)(2,1)S(1)} all-to-all(bf16[4,216,128]{2,1,0:T(8,128)(2,1)S(1)} %add_up.1), channel_id=1, replica_groups=mesh['zh'=8,'zl'=2,'x'=4,'c'=2,'y'=4] {'y'}, dimensions={0} | all-to-all | bytes 442368 | tf_op jit(solution)/shard_map/all_to_all | solution.py:260
  74.1 0.0 copy-done.3
  74.1 0.0 copy-done.4
  74.1 0.0 copy-done.5
  74.1 0.7 state_parts.1
  74.8 12.3 %all_to_all.39.in_ref = bf16[16,16,512]{2,1,0:T(8,128)(2,1)S(1)} all-to-all(bf16[16,16,512]{2,1,0:T(8,128)(2,1)S(1)} %get-tuple-element.17), channel_id=1, replica_groups=mesh['zh'=8,'zl'=2,'x'=4,'c'=2,'y'=4] {'x','c','zl'}, dimensions={0} | all-to-all | bytes 524288 | tf_op jit(solution)/shard_map/all_to_all | solution.py:260
  87.0 0.3 regroup.1
  87.4 19.4 %all_to_all.40.in_ref.back_ref = bf16[16,88,128]{2,1,0:T(8,128)(2,1)S(1)} all-to-all(bf16[16,88,128]{2,1,0:T(8,128)(2,1)S(1)} %regroup.1), channel_id=1, replica_groups=mesh['zh'=8,'zl'=2,'x'=4,'c'=2,'y'=4] {'zh','zl'}, dimensions={0} | all-to-all | bytes 720896 | tf_op jit(solution)/shard_map/all_to_all | solution.py:260
  106.7 0.1 reduce_states.1
  106.8 17.5 %all_to_all.41.in_ref = bf16[16,16,512]{2,1,0:T(8,128)(2,1)S(1)} all-to-all(bf16[16,16,512]{2,1,0:T(8,128)(2,1)S(1)} %reduce_states.1), channel_id=1, replica_groups=mesh['zh'=8,'zl'=2,'x'=4,'c'=2,'y'=4] {'x','c','zl'}, dimensions={0} | all-to-all | bytes 524288 | tf_op jit(solution)/shard_map/all_to_all | solution.py:260
  124.3 0.0 copy-done.7
  124.3 1.5 %finish.1 = (bf16[128,768]{1,0:T(8,128)(2,1)}, bf16[128,256]{1,0:T(8,128)(2,1)}, bf16[128,256]{1,0:T(8,128)(2,1)}, bf16[128,256]{1,0:T(8,128)(2,1)}) custom-call(bf16[16,16,512]{2,1,0:T(8,128)(2,1)S(1)} %all_to_all.41.in_ref, bf16[16,88,128]{2,1,0:T(8,128)(2,1)S(1)} %all_to_all.40.in_ref.back_ref, s32[1,128]{1,0:T(1,128)S(1)} %bitcast.9, ...), custom_call_target="tpu_custom_call" | custom-call | flops 10000000000 | bytes 1147392 | tf_op jit(solution)/shard_map/finish/pallas_call | solution.py:52
  (7 shorter events, 0.0 us)
Async XLA Ops:
  29.5 21.3 %copy-start = (bf16[1,768,768]{2,1,0:T(8,128)(2,1)S(1)}, bf16[1,768,768]{2,1,0:T(8,128)(2,1)}, u32[]{:S(2)}) copy-start(bf16[1,768,768]{2,1,0:T(8,128)(2,1)} %param.14) | copy-start | bytes 3538948
  29.5 21.3 %copy-start.1 = (bf16[1,768,768]{2,1,0:T(8,128)(2,1)S(1)}, bf16[1,768,768]{2,1,0:T(8,128)(2,1)}, u32[]{:S(2)}) copy-start(bf16[1,768,768]{2,1,0:T(8,128)(2,1)} %param.13) | copy-start | bytes 3538948
  29.5 21.3 %copy-start.2 = (bf16[256,768]{1,0:T(8,128)(2,1)S(1)}, bf16[256,768]{1,0:T(8,128)(2,1)}, u32[]{:S(2)}) copy-start(bf16[256,768]{1,0:T(8,128)(2,1)} %pre_ref.1) | copy-start | bytes 1179652
  29.5 21.3 %copy-start.6 = (s32[128,1]{0,1:T(1,128)S(1)}, s32[128,1]{0,1:T(1,128)}, u32[]{:S(2)}) copy-start(s32[128,1]{0,1:T(1,128)} %param.12) | copy-start | bytes 1540
  66.1 8.0 %copy-start.3 = (bf16[256,768]{1,0:T(8,128)(2,1)S(1)}, bf16[256,768]{1,0:T(8,128)(2,1)}, u32[]{:S(2)}) copy-start(bf16[256,768]{1,0:T(8,128)(2,1)} %wo_ref.3) | copy-start | bytes 1179652
  66.1 8.0 %copy-start.4 = (bf16[128,256]{1,0:T(8,128)(2,1)S(1)}, bf16[128,256]{1,0:T(8,128)(2,1)}, u32[]{:S(2)}) copy-start(bf16[128,256]{1,0:T(8,128)(2,1)} %k_ref.3) | copy-start | bytes 196612
  66.1 8.0 %copy-start.5 = (bf16[128,256]{1,0:T(8,128)(2,1)S(1)}, bf16[128,256]{1,0:T(8,128)(2,1)}, u32[]{:S(2)}) copy-start(bf16[128,256]{1,0:T(8,128)(2,1)} %v_ref.3) | copy-start | bytes 196612
  106.7 17.6 %copy-start.7 = (s32[128]{0:T(128)S(1)}, s32[128]{0:T(128)}, u32[]{:S(2)}) copy-start(s32[128]{0:T(128)} %param.11) | copy-start | bytes 1540

commit v10 on v9

--- a/solution.py
+++ b/solution.py
@@ -181,8 +181,11 @@
     second_ref[...] = second
     wo = wo_ref[...]
     query = tn(nt(first, wo).astype(BF), q_ref[...]) + tn(nt(second, wo).astype(BF), sq_ref[...])
-    out_ref[:, :, 0:HD] = query.astype(BF).reshape(16, 16, HD)
-    out_ref[:, :, HD:] = tn(k_ref[...], v_ref[...]).astype(BF).reshape(16, 16, HD)
+    query = query.astype(BF).reshape(NP, 2, 16, HD)
+    key = tn(k_ref[...], v_ref[...]).astype(BF).reshape(NP, 2, 16, HD)
+    for zl in range(2):
+        out_ref[zl * NP : (zl + 1) * NP, :, 0:HD] = query[:, zl]
+        out_ref[zl * NP : (zl + 1) * NP, :, HD:] = key[:, zl]
 
 
 def regroup(in_ref, first_ref, second_ref, out_ref):
@@ -230,7 +233,7 @@
     def whole(zl):
         pieces = []
         for p in range(NP):
-            pieces += [in_ref[2 * p + zl, :, 0:HD], in_ref[2 * p + zl, :, HD:]]
+            pieces += [in_ref[zl * NP + p, :, 0:HD], in_ref[zl * NP + p, :, HD:]]
         return jnp.concatenate(pieces, axis=0)
 
     qt, kr = whole(0), whole(1)
@@ -272,9 +275,9 @@
     msgs = swap(call(add_up, sds(NH, 216, BLOCK), msgs, first, second), "y")
     outs = [sds(16, 16, 512), sds(BLOCK, D), sds(NZ, D)]
     msgs, first, second = call(state_parts, outs, msgs, q, sq, w_out, keys, values)
-    msgs = swap(msgs, PLANE + ("zl",))
+    msgs = swap(msgs, ("zl",) + PLANE)
     back = swap(call(regroup, sds(NZ, 88, BLOCK), msgs, first, second), Z)
-    states = swap(call(reduce_states, sds(2 * NP, 16, 512), back), PLANE + ("zl",))
+    states = swap(call(reduce_states, sds(2 * NP, 16, 512), back), ("zl",) + PLANE)
     outs = [sds(BLOCK, D)] + [sds(BLOCK, HD)] * 3
     return tuple(call(finish, outs, states, back, e, w_out, keys, values, home=4))
 

time: 126 us -> 126 us (level)
  no operation moved by 1% of the time
where the time goes in v10:
time: 126 us
  blocking collectives  120 us (95%)
  Pallas kernels  5.79 us (5%)
    all_to_all x7, blocking collectives, swap(): return lax.all_to_all(tiles, axis, split_axis=0, concat_axis=0, tiled=True)  120 us
    pallas_call x8, Pallas kernels, call(): pl.pallas_call(kernel, out_shape=[s if n < home else pltpu.VMEM(s.shape,...  5.79 us

profile of v10, /device:TPU:1, one launch (start us, length us, event | category | flops | bytes accessed | tf_op | source)
XLA Modules:
  0.0 126.1 jit_solution(1544783777433031112)
XLA Ops:
  0.6 1.4 %pack.1 = bf16[16,16,256]{2,1,0:T(8,128)(2,1)S(1)} custom-call(s32[1,128]{1,0:T(1,128)} %bitcast.8, bf16[192,128]{1,0:T(8,128)(2,1)} %bitcast.10, bf16[128,256]{1,0:T(8,128)(2,1)} %q_ref.1), custom_call_target="tpu_custom_call" | custom-call | flops 10000000000 | bytes 115200 | tf_op jit(solution)/shard_map/pack/pallas_call | solution.py:52
  2.0 27.5 %all_to_all.35.in_ref = bf16[16,16,256]{2,1,0:T(8,128)(2,1)S(1)} all-to-all(bf16[16,16,256]{2,1,0:T(8,128)(2,1)S(1)} %pack.1), channel_id=1, replica_groups=mesh['zh'=8,'zl'=2,'x'=4,'c'=2,'y'=4] {'zh','zl'}, dimensions={0} | all-to-all | bytes 262144 | tf_op jit(solution)/shard_map/all_to_all | solution.py:263
  29.5 0.0 copy-start
  29.5 0.4 forward.1
  30.0 20.9 %all_to_all.36.in_ref = bf16[32,16,384]{2,1,0:T(8,128)(2,1)S(1)} all-to-all(bf16[32,16,384]{2,1,0:T(8,128)(2,1)S(1)} %get-tuple-element.12), channel_id=1, replica_groups=mesh['zh'=8,'zl'=2,'x'=4,'c'=2,'y'=4] {'x','c','y'}, dimensions={0} | all-to-all | bytes 786432 | tf_op jit(solution)/shard_map/all_to_all | solution.py:263
  50.8 0.0 copy-done
  50.8 0.0 copy-done.1
  50.8 0.0 copy-done.2
  50.8 0.0 copy-done.6
  50.8 1.3 experts.1
  52.1 14.0 %all_to_all.37.in_ref = bf16[32,16,384]{2,1,0:T(8,128)(2,1)S(1)} all-to-all(bf16[32,16,384]{2,1,0:T(8,128)(2,1)S(1)} %experts.1), channel_id=1, replica_groups=mesh['zh'=8,'zl'=2,'x'=4,'c'=2,'y'=4] {'x','c','y'}, dimensions={0} | all-to-all | bytes 786432 | tf_op jit(solution)/shard_map/all_to_all | solution.py:263
  66.1 0.2 add_up.1
  66.3 7.8 %all_to_all.38.in_ref = bf16[4,216,128]{2,1,0:T(8,128)(2,1)S(1)} all-to-all(bf16[4,216,128]{2,1,0:T(8,128)(2,1)S(1)} %add_up.1), channel_id=1, replica_groups=mesh['zh'=8,'zl'=2,'x'=4,'c'=2,'y'=4] {'y'}, dimensions={0} | all-to-all | bytes 442368 | tf_op jit(solution)/shard_map/all_to_all | solution.py:263
  74.1 0.0 copy-done.3
  74.1 0.0 copy-done.4
  74.1 0.0 copy-done.5
  74.1 0.7 state_parts.1
  74.8 12.3 %all_to_all.39.in_ref = bf16[16,16,512]{2,1,0:T(8,128)(2,1)S(1)} all-to-all(bf16[16,16,512]{2,1,0:T(8,128)(2,1)S(1)} %get-tuple-element.17), channel_id=1, replica_groups=mesh['zh'=8,'zl'=2,'x'=4,'c'=2,'y'=4] {'zl','x','c'}, dimensions={0} | all-to-all | bytes 524288 | tf_op jit(solution)/shard_map/all_to_all | solution.py:263
  87.0 0.3 regroup.1
  87.4 19.3 %all_to_all.40.in_ref.back_ref = bf16[16,88,128]{2,1,0:T(8,128)(2,1)S(1)} all-to-all(bf16[16,88,128]{2,1,0:T(8,128)(2,1)S(1)} %regroup.1), channel_id=1, replica_groups=mesh['zh'=8,'zl'=2,'x'=4,'c'=2,'y'=4] {'zh','zl'}, dimensions={0} | all-to-all | bytes 720896 | tf_op jit(solution)/shard_map/all_to_all | solution.py:263
  106.6 0.1 reduce_states.1
  106.7 17.8 %all_to_all.41.in_ref = bf16[16,16,512]{2,1,0:T(8,128)(2,1)S(1)} all-to-all(bf16[16,16,512]{2,1,0:T(8,128)(2,1)S(1)} %reduce_states.1), channel_id=1, replica_groups=mesh['zh'=8,'zl'=2,'x'=4,'c'=2,'y'=4] {'zl','x','c'}, dimensions={0} | all-to-all | bytes 524288 | tf_op jit(solution)/shard_map/all_to_all | solution.py:263
  124.5 0.0 copy-done.7
  124.5 1.5 %finish.1 = (bf16[128,768]{1,0:T(8,128)(2,1)}, bf16[128,256]{1,0:T(8,128)(2,1)}, bf16[128,256]{1,0:T(8,128)(2,1)}, bf16[128,256]{1,0:T(8,128)(2,1)}) custom-call(bf16[16,16,512]{2,1,0:T(8,128)(2,1)S(1)} %all_to_all.41.in_ref, bf16[16,88,128]{2,1,0:T(8,128)(2,1)S(1)} %all_to_all.40.in_ref.back_ref, s32[1,128]{1,0:T(1,128)S(1)} %bitcast.9, ...), custom_call_target="tpu_custom_call" | custom-call | flops 10000000000 | bytes 1147392 | tf_op jit(solution)/shard_map/finish/pallas_call | solution.py:52
  (7 shorter events, 0.0 us)
Async XLA Ops:
  29.5 21.3 %copy-start = (bf16[1,768,768]{2,1,0:T(8,128)(2,1)S(1)}, bf16[1,768,768]{2,1,0:T(8,128)(2,1)}, u32[]{:S(2)}) copy-start(bf16[1,768,768]{2,1,0:T(8,128)(2,1)} %param.14) | copy-start | bytes 3538948
  29.5 21.3 %copy-start.1 = (bf16[1,768,768]{2,1,0:T(8,128)(2,1)S(1)}, bf16[1,768,768]{2,1,0:T(8,128)(2,1)}, u32[]{:S(2)}) copy-start(bf16[1,768,768]{2,1,0:T(8,128)(2,1)} %param.13) | copy-start | bytes 3538948
  29.5 21.3 %copy-start.2 = (bf16[256,768]{1,0:T(8,128)(2,1)S(1)}, bf16[256,768]{1,0:T(8,128)(2,1)}, u32[]{:S(2)}) copy-start(bf16[256,768]{1,0:T(8,128)(2,1)} %pre_ref.1) | copy-start | bytes 1179652
  29.5 21.3 %copy-start.6 = (s32[128,1]{0,1:T(1,128)S(1)}, s32[128,1]{0,1:T(1,128)}, u32[]{:S(2)}) copy-start(s32[128,1]{0,1:T(1,128)} %param.12) | copy-start | bytes 1540
  66.1 8.0 %copy-start.3 = (bf16[256,768]{1,0:T(8,128)(2,1)S(1)}, bf16[256,768]{1,0:T(8,128)(2,1)}, u32[]{:S(2)}) copy-start(bf16[256,768]{1,0:T(8,128)(2,1)} %wo_ref.3) | copy-start | bytes 1179652
  66.1 8.0 %copy-start.4 = (bf16[128,256]{1,0:T(8,128)(2,1)S(1)}, bf16[128,256]{1,0:T(8,128)(2,1)}, u32[]{:S(2)}) copy-start(bf16[128,256]{1,0:T(8,128)(2,1)} %k_ref.3) | copy-start | bytes 196612
  66.1 8.0 %copy-start.5 = (bf16[128,256]{1,0:T(8,128)(2,1)S(1)}, bf16[128,256]{1,0:T(8,128)(2,1)}, u32[]{:S(2)}) copy-start(bf16[128,256]{1,0:T(8,128)(2,1)} %v_ref.3) | copy-start | bytes 196612
  106.6 17.9 %copy-start.7 = (s32[128]{0:T(128)S(1)}, s32[128]{0:T(128)}, u32[]{:S(2)}) copy-start(s32[128]{0:T(128)} %param.11) | copy-start | bytes 1540
